TPU v7x, 128 devices: a whole 4x4x4 slice. The times are simulated.
128 devices in a mesh: req: 16 (over x, z), tp: 8 (over y, core).
Axes of the slice: x: 4, y: 4, z: 4, core: 2. Of those that a mesh axis runs over, the one named last changes fastest.
Arguments:
- hidden: bfloat16 [8192, 2048], P('req', 'tp'), may hold values from -6 to 6
- qkv_weight: bfloat16 [2048, 3072], P('req', 'tp'), may hold values from -0.125 to 0.125
- out_weight: bfloat16 [2048, 2048], P('tp', 'req'), may hold values from -0.125 to 0.125
- kv_pages: bfloat16 [1024, 128, 1024], P('req', None, 'tp'), may hold values from -160 to 160, as said below
- cache_pages: int32 [16], replicated, may hold values from 1 to 256, 960 in all
- slot_order: int32 [1024], replicated, may hold values from 0 to 1023, each once
Outputs:
- attention_out: bfloat16 [8192, 2048], P('req', 'tp')
- pages_out: bfloat16 [1024, 128, 1024], P('req', None, 'tp')
Inputs may be any that keep to these rules, and one draw needn't show every extreme that they name: `cache_pages`: each request has at least one cached page and at most 256, and one request has exactly 256; all cached pages plus 4 new pages per request fill exactly 1024 slots. `slot_order`: each global slot appears once. `kv_pages`: cached rotated keys and values.
All inputs are finite; a program needn't handle non-finite values.
Results may differ from a plain program's by a relative error of at most 0.02.
The roundings to bfloat16 on the way count: a program that leaves them out, or rounds other values in their place, can miss the bound.
Values may be sent and summed in bfloat16 or wider, within the bound.
A program may use at most 128 MiB of HBM per device.

v0:
```python
import math

import jax
import jax.numpy as jnp
from jax import lax
from jax.sharding import PartitionSpec as P

HD = 64
GROUP = 4
SPAN = 512


THETA = 1000000.0
NEG_BIG = -1e30


def rotary(values, positions):
    head_width = values.shape[-1]
    half_width = head_width // 2
    inv_freq = jnp.power(THETA, -(jnp.arange(half_width, dtype=jnp.float32) * 2.0 / head_width))
    angles = positions.astype(jnp.float32)[..., None] * inv_freq
    cosines = jnp.cos(angles)
    sines = jnp.sin(angles)
    lower_half = values[..., :half_width]
    upper_half = values[..., half_width:]
    return jnp.concatenate(
        [lower_half * cosines - upper_half * sines, upper_half * cosines + lower_half * sines],
        axis=-1,
    )


def to_columns(stat):
    return jnp.moveaxis(stat, -1, -3)[..., None]


def locate(slot_ids, cache_pages, slot_order, new_pages):
    requests = cache_pages.shape[0]
    slot_count = slot_order.shape[0]
    counts = cache_pages + new_pages
    page_ends = jnp.cumsum(counts)
    starts = page_ends - counts
    ranking = jnp.sum(
        jnp.where(
            slot_order[None, :] == slot_ids[:, None],
            jnp.arange(slot_count, dtype=jnp.int32)[None, :],
            0,
        ),
        axis=1,
    )
    holder = jnp.sum((starts[None, :] <= ranking[:, None]).astype(jnp.int32), axis=1) - 1
    onehot = jnp.arange(requests, dtype=jnp.int32)[None, :] == holder[:, None]
    first_page = jnp.sum(jnp.where(onehot, starts[None, :], 0), axis=1)
    cached = jnp.sum(jnp.where(onehot, cache_pages[None, :], 0), axis=1)
    return (holder, ranking - first_page, cached)


def write_pages(kv_pages, fresh, slot_req, page_index, cached, new_pages):
    page_rows = kv_pages.shape[1]
    lane_width = kv_pages.shape[2]
    fresh_pages = fresh.reshape(-1, page_rows, lane_width)
    pick = slot_req * new_pages + jnp.clip(page_index - cached, 0, new_pages - 1)
    return jnp.where((page_index >= cached)[:, None, None], fresh_pages[pick], kv_pages)


def block_terms(queries, query_start, page_block, slot_req, key_start, is_live):
    block_slots = page_block.shape[0]
    page_rows = page_block.shape[1]
    kv_heads = queries.shape[2]
    head_width = queries.shape[4]
    span_rows = queries.shape[1]
    kv_pairs = page_block.reshape(block_slots, page_rows, kv_heads, 2, head_width)
    key_rows = kv_pairs[:, :, :, 0, :]
    value_rows = kv_pairs[:, :, :, 1, :]
    chosen = queries[slot_req]
    scores = jnp.einsum(
        "bckgd,bpkd->bkgcp", chosen, key_rows, preferred_element_type=jnp.float32
    ) * (1.0 / math.sqrt(head_width))
    query_pos = query_start[slot_req][:, None] + jnp.arange(span_rows, dtype=jnp.int32)[None, :]
    key_pos = key_start[:, None] + jnp.arange(page_rows, dtype=jnp.int32)[None, :]
    visible = (key_pos[:, None, :] <= query_pos[:, :, None]) & is_live[:, None, None]
    visible = visible[:, None, None, :, :]
    masked = jnp.where(visible, scores, NEG_BIG)
    block_max = jnp.max(masked, axis=-1)
    exp_terms = jnp.where(visible, jnp.exp(masked - block_max[..., None]), 0.0)
    block_sum = jnp.sum(exp_terms, axis=-1)
    weights = exp_terms.astype(jnp.bfloat16)
    block_out = jnp.einsum(
        "bkgcp,bpkd->bckgd", weights, value_rows, preferred_element_type=jnp.float32
    )
    return (block_out, block_max, block_sum)


def fold(running, terms, slot_req):
    acc_out, acc_max, acc_sum = running
    block_out, block_max, block_sum = terms
    for j in range(block_out.shape[0]):
        target = slot_req[j]
        old_max = lax.dynamic_index_in_dim(acc_max, target, 0, keepdims=False)
        new_max = jnp.maximum(old_max, block_max[j])
        keep_old = jnp.exp(old_max - new_max)
        take_new = jnp.exp(block_max[j] - new_max)
        old_out = lax.dynamic_index_in_dim(acc_out, target, 0, keepdims=False)
        old_sum = lax.dynamic_index_in_dim(acc_sum, target, 0, keepdims=False)
        acc_out = lax.dynamic_update_index_in_dim(
            acc_out, old_out * to_columns(keep_old) + block_out[j] * to_columns(take_new), target, 0
        )
        acc_sum = lax.dynamic_update_index_in_dim(
            acc_sum, old_sum * keep_old + block_sum[j] * take_new, target, 0
        )
        acc_max = lax.dynamic_update_index_in_dim(acc_max, new_max, target, 0)
    return (acc_out, acc_max, acc_sum)


def init_state(requests, span_rows, kv_heads, group_size, head_width):
    return (
        jnp.zeros((requests, span_rows, kv_heads, group_size, head_width), jnp.float32),
        jnp.full((requests, kv_heads, group_size, span_rows), NEG_BIG, jnp.float32),
        jnp.zeros((requests, kv_heads, group_size, span_rows), jnp.float32),
    )


def body(hidden, qkv_weight, out_weight, kv_pages, cache_pages, slot_order):
    whole = lax.all_gather(hidden, "tp", axis=1, tiled=True)
    tok_rows = whole.shape[0]
    projected = jnp.dot(
        whole,
        lax.all_gather(qkv_weight, "req", axis=0, tiled=True),
        preferred_element_type=jnp.float32,
    )
    local_slots = kv_pages.shape[0]
    page_rows = kv_pages.shape[1]
    lane_width = kv_pages.shape[2]
    kv_heads = lane_width // (2 * HD)
    local_reqs = tok_rows // SPAN
    new_pages = SPAN // page_rows
    my_index = lax.axis_index("req")
    query_start = cache_pages * page_rows
    home_start = lax.dynamic_slice_in_dim(query_start, my_index * local_reqs, local_reqs, 0)
    projected = projected.reshape(local_reqs, SPAN, kv_heads, GROUP + 2, HD)
    positions = (home_start[:, None] + jnp.arange(SPAN, dtype=jnp.int32)[None, :])[:, :, None, None]
    queries = rotary(projected[:, :, :, :GROUP, :], positions).astype(jnp.bfloat16)
    key_new = rotary(projected[:, :, :, GROUP : GROUP + 1, :], positions).astype(jnp.bfloat16)
    value_new = projected[:, :, :, GROUP + 1 :, :].astype(jnp.bfloat16)
    fresh = jnp.concatenate([key_new, value_new], axis=3).reshape(local_reqs, SPAN, lane_width)
    my_slots = my_index * local_slots + jnp.arange(local_slots, dtype=jnp.int32)
    block_slots = math.gcd(local_slots, max(1, 512 // page_rows))
    fresh_all = lax.all_gather(fresh, "req", axis=0, tiled=True)
    slot_req, page_index, cached = locate(my_slots, cache_pages, slot_order, new_pages)
    pages_out = write_pages(kv_pages, fresh_all, slot_req, page_index, cached, new_pages)
    piece_pages = lax.all_gather(pages_out, "req", axis=0, tiled=True)
    piece_count = piece_pages.shape[0]
    piece_ids = jnp.arange(piece_count, dtype=jnp.int32)
    piece_req, piece_index, unused_cached = locate(piece_ids, cache_pages, slot_order, new_pages)
    local_req = piece_req - my_index * local_reqs
    is_mine = (local_req >= 0) & (local_req < local_reqs)
    ordering = jnp.argsort(jnp.where(is_mine, 0, 1).astype(jnp.int32), stable=True)
    ordering = jnp.concatenate([ordering, jnp.zeros((block_slots,), jnp.int32)])
    used_count = jnp.sum(is_mine.astype(jnp.int32))

    def advance(j, state_now):
        low_slot = j * block_slots
        picked = lax.dynamic_slice_in_dim(ordering, low_slot, block_slots, 0)
        page_block = piece_pages[picked]
        is_live = low_slot + jnp.arange(block_slots, dtype=jnp.int32) < used_count
        block_req = jnp.clip(local_req[picked], 0, local_reqs - 1)
        key_start = piece_index[picked] * page_rows
        terms = block_terms(queries, home_start, page_block, block_req, key_start, is_live)
        return fold(state_now, terms, block_req)

    acc_out, acc_max, acc_sum = lax.fori_loop(
        0,
        (used_count + block_slots - 1) // block_slots,
        advance,
        init_state(local_reqs, SPAN, kv_heads, GROUP, HD),
    )
    attention = acc_out / to_columns(acc_sum)
    attention_flat = attention.astype(jnp.bfloat16).reshape(tok_rows, kv_heads * GROUP * HD)
    head_terms = jnp.dot(
        attention_flat,
        lax.all_gather(out_weight, "req", axis=1, tiled=True),
        preferred_element_type=jnp.float32,
    )
    attention_out = lax.psum_scatter(
        head_terms.astype(jnp.bfloat16), "tp", scatter_dimension=1, tiled=True
    )
    return (attention_out, pages_out)


def solution(mesh):
    return jax.shard_map(
        body,
        mesh=mesh,
        in_specs=(P("req", "tp"), P("req", "tp"), P("tp", "req"), P("req", None, "tp"), P(), P()),
        out_specs=(P("req", "tp"), P("req", None, "tp")),
        check_vma=False,
    )
```

profile of v0, /device:TPU:0, one launch (start us, length us, event | category | flops | bytes accessed | tf_op | source)
XLA Modules:
  0.0 880.4 jit_solution(123321950454702308)
XLA Ops:
  11.6 45.0 %all-gather.8.cloned.1.call-done = bf16[2048,384]{1,0:T(8,128)(2,1)} async-done(((bf16[128,384]{1,0:T(8,128)(2,1)}), bf16[2048,384]{1,0:T(8,128)(2,1)}) %all-gather.8.cloned.1.call-update) | async-done | bytes 1572880 | tf_op jit(solution)/shard_map/all_gather | solution.py:127
  56.5 27.8 %all-gather.6.cloned.1.call-done = bf16[512,2048]{1,0:T(8,128)(2,1)} async-done(((bf16[512,256]{1,0:T(8,128)(2,1)}), bf16[512,2048]{1,0:T(8,128)(2,1)}) %all-gather.6.cloned.1.call-update) | async-done | bytes 2097168 | tf_op jit(solution)/shard_map/all_gather | solution.py:123
  84.3 3.1 fusion.54
  89.0 45.6 %all-gather.10.cloned.1.call-done = bf16[16,512,128]{2,1,0:T(8,128)(2,1)} async-done(((bf16[1,512,128]{2,1,0:T(8,128)(2,1)}), bf16[16,512,128]{2,1,0:T(8,128)(2,1)}) %all-gather.10.cloned.1.call-update) | async-done | bytes 2097168 | tf_op jit(solution)/shard_map/all_gather | solution.py:147
  134.6 2.5 gather_fusion.2
  137.1 3.2 broadcast_select_fusion
  143.2 4.4 sort.17
  147.8 189.2 %all-gather.12.cloned.1.call-done = bf16[1024,128,128]{2,1,0:T(8,128)(2,1)} async-done(((bf16[64,128,128]{2,1,0:T(8,128)(2,1)}), bf16[1024,128,128]{2,1,0:T(8,128)(2,1)}) %all-gather.12.cloned.1.call-update) | async-done | bytes 33554448 | tf_op jit(solution)/shard_map/all_gather | solution.py:150
  337.1 76.9 %while.15 = (s32[]{:T(128)}, f32[1,512,1,4,64]{1,4,3,0,2:T(8,128)S(1)}, f32[1,1,4,512]{3,2,1,0:T(4,128)S(1)}, f32[1,1,4,512]{3,2,1,0:T(4,128)S(1)}, s32[]{:T(128...) while((s32[]{:T(128)}, ...), condition=%wide.region_13.14_spmd.clone, body=%wide.region_10.13_spmd.clone.sunk | while | flops 284227616 | bytes 20279676 | solution.py:170
  339.4 1.4 gather_fusion.1
  347.0 1.4 gather_fusion.1
  354.7 1.4 gather_fusion.1
  362.4 1.4 gather_fusion.1
  370.1 1.4 gather_fusion.1
  372.5 1.2 fusion.68
  377.8 1.4 gather_fusion.1
  380.2 1.2 fusion.68
  385.5 1.4 gather_fusion.1
  387.9 1.2 fusion.68
  393.2 1.4 gather_fusion.1
  400.8 1.4 gather_fusion.1
  408.5 1.4 gather_fusion.1
  414.0 3.3 convolution_convert_fusion
  417.4 456.1 %reduce-scatter.2.cloned.1.call-done = bf16[512,256]{1,0:T(8,128)(2,1)} async-done(((bf16[512,2048]{1,0:T(8,128)(2,1)}), bf16[512,256]{1,0:T(8,128)(2,1)}) %reduce-scatter.2.cloned.1.call-update) | async-done | bytes 262160 | tf_op jit(solution)/shard_map/reduce_scatter | solution.py:183
  (209 shorter events, 67.1 us)
Async XLA Ops:
  7.2 81.7 %copy-start.1 = (s32[16]{0:T(128)S(1)}, s32[16]{0:T(128)}, u32[]{:S(2)}) copy-start(s32[16]{0:T(128)} %param.12) | copy-start | bytes 196
  7.2 81.4 %copy-start = (s32[1024]{0:T(1024)S(1)}, s32[1024]{0:T(1024)}, u32[]{:S(2)}) copy-start(s32[1024]{0:T(1024)} %param.13) | copy-start | bytes 12292
  7.2 49.3 %all-gather.8.cloned.1.call-start = ((), (), s32[]{:S(2)}) async-start(), calls=%async_computation.2 | async-start | bytes 1671168 | tf_op jit(solution)/shard_map/all_gather | solution.py:127
  7.9 76.4 %all-gather.6.cloned.1.call-start = ((), (), s32[]{:S(2)}) async-start(), calls=%async_computation.1 | async-start | bytes 2359296 | tf_op jit(solution)/shard_map/all_gather | solution.py:123
  8.7 125.9 %all-gather.10.cloned.1.call-start = ((), (), s32[]{:S(2)}) async-start(), calls=%async_computation.3 | async-start | bytes 2228224 | tf_op jit(solution)/shard_map/all_gather | solution.py:147
  88.5 248.5 %all-gather.12.cloned.1.call-start = ((), (), s32[]{:S(2)}) async-start(), calls=%async_computation.4 | async-start | bytes 35651584 | tf_op jit(solution)/shard_map/all_gather | solution.py:150
  140.4 273.6 %all-gather.14.cloned.1.call-start = ((), (), s32[]{:S(2)}) async-start(), calls=%async_computation.5 | async-start | bytes 1114112 | tf_op jit(solution)/shard_map/all_gather | solution.py:180
  141.0 732.5 %reduce-scatter.2.cloned.1.call-start = ((), (), s32[]{:S(2)}) async-start(), calls=%async_computation.6 | async-start | bytes 2359296 | tf_op jit(solution)/shard_map/reduce_scatter | solution.py:183
Sparse Core Ops, SparseCore 0:
  10.2 46.2 all-gather.7
  58.2 26.0 all-gather.5
  88.6 45.9 all-gather.9
  140.5 196.4 all-gather.11
  338.9 42.8 all-gather.13
  417.5 455.9 reduce-scatter.1
where the time goes:
time: 886 us; the launch traced here: 880 us
  waiting for transfers between devices  766 us (86%)
  other arithmetic  45.5 us (5%)
  matrix products  28 us (3%)
  local copies, waits for them, and re-layouts  25.4 us (3%)
  between operations  14.9 us (2%)
    reduce_scatter x1, waiting for transfers between devices, body(): lax.psum_scatter(head_terms.astype(jnp.bfloat16), 'tp', scatter_dimension...  456 us
    all_gather x1, waiting for transfers between devices, body(): piece_pages = lax.all_gather(pages_out, 'req', axis=0, tiled=True)  189 us
    all_gather x1, waiting for transfers between devices, body(): fresh_all = lax.all_gather(fresh, 'req', axis=0, tiled=True)  45.6 us
    all_gather x1, waiting for transfers between devices, body(): lax.all_gather(qkv_weight, 'req', axis=0, tiled=True)  45 us
    all_gather x1, waiting for transfers between devices, body(): whole = lax.all_gather(hidden, 'tp', axis=1, tiled=True)  27.8 us
  transfers between devices with their start and end apart: 6, of which 5 were waited for; matrix products, arithmetic and copies ran while one was open for 10% of the time, Pallas kernels for 0%

commit v1 on v0

v1 whole, which is shorter than its diff:
```python
import math

import jax
import jax.numpy as jnp
from jax import lax
from jax.experimental import pallas as pl
from jax.experimental.pallas import tpu as pltpu
from jax.sharding import PartitionSpec as P

HD = 64
GROUP = 4
SPAN = 512


THETA = 1000000.0
NEG_BIG = -1e30


def rotary(values, positions):
    head_width = values.shape[-1]
    half_width = head_width // 2
    inv_freq = jnp.power(THETA, -(jnp.arange(half_width, dtype=jnp.float32) * 2.0 / head_width))
    angles = positions.astype(jnp.float32)[..., None] * inv_freq
    cosines = jnp.cos(angles)
    sines = jnp.sin(angles)
    lower_half = values[..., :half_width]
    upper_half = values[..., half_width:]
    return jnp.concatenate(
        [lower_half * cosines - upper_half * sines, upper_half * cosines + lower_half * sines],
        axis=-1,
    )


def locate(slot_ids, cache_pages, slot_order, new_pages):
    requests = cache_pages.shape[0]
    slot_count = slot_order.shape[0]
    counts = cache_pages + new_pages
    page_ends = jnp.cumsum(counts)
    starts = page_ends - counts
    ranking = jnp.sum(
        jnp.where(
            slot_order[None, :] == slot_ids[:, None],
            jnp.arange(slot_count, dtype=jnp.int32)[None, :],
            0,
        ),
        axis=1,
    )
    holder = jnp.sum((starts[None, :] <= ranking[:, None]).astype(jnp.int32), axis=1) - 1
    onehot = jnp.arange(requests, dtype=jnp.int32)[None, :] == holder[:, None]
    first_page = jnp.sum(jnp.where(onehot, starts[None, :], 0), axis=1)
    cached = jnp.sum(jnp.where(onehot, cache_pages[None, :], 0), axis=1)
    return (holder, ranking - first_page, cached)


def write_pages(kv_pages, fresh, slot_req, page_index, cached, new_pages):
    page_rows = kv_pages.shape[1]
    lane_width = kv_pages.shape[2]
    fresh_pages = fresh.reshape(-1, page_rows, lane_width)
    pick = slot_req * new_pages + jnp.clip(page_index - cached, 0, new_pages - 1)
    return jnp.where((page_index >= cached)[:, None, None], fresh_pages[pick], kv_pages)


def slot_attention(sreq, perm, kstart, qstart, packed, pages):
    reqs, span_rows, _ = packed.shape
    slots, page_rows, _ = pages.shape
    qw = GROUP * HD

    def kernel(sreq_ref, perm_ref, kstart_ref, qstart_ref, q_ref, page_ref, o_ref, st_ref, m_sc, l_sc, acc_sc):
        i = pl.program_id(0)
        n = pl.num_programs(0)
        req = sreq_ref[i]
        prev = sreq_ref[jnp.maximum(i - 1, 0)]
        nxt = sreq_ref[jnp.minimum(i + 1, n - 1)]
        first = jnp.logical_or(i == 0, prev != req)
        last = jnp.logical_or(i == n - 1, nxt != req)

        @pl.when(first)
        def _():
            m_sc[...] = jnp.full(m_sc.shape, NEG_BIG, jnp.float32)
            l_sc[...] = jnp.zeros(l_sc.shape, jnp.float32)
            acc_sc[...] = jnp.zeros(acc_sc.shape, jnp.float32)

        kst = kstart_ref[i]
        qst = qstart_ref[req]
        page = page_ref[0]
        keys = page[:, :HD]
        vals = page[:, HD:]
        q_all = q_ref[0]
        row = lax.broadcasted_iota(jnp.int32, (span_rows, page_rows), 0) + qst
        col = lax.broadcasted_iota(jnp.int32, (span_rows, page_rows), 1) + kst
        vis = col <= row
        for g in range(GROUP):
            qg = q_all[:, g * HD:(g + 1) * HD]
            s = lax.dot_general(qg, keys, (((1,), (1,)), ((), ())), preferred_element_type=jnp.float32)
            s = jnp.where(vis, s, NEG_BIG)
            m_prev = m_sc[g]
            m_next = jnp.maximum(m_prev, jnp.max(s, axis=1, keepdims=True))
            alpha = jnp.exp(m_prev - m_next)
            p = jnp.where(vis, jnp.exp(s - m_next), 0.0)
            l_sc[g] = alpha * l_sc[g] + jnp.sum(p, axis=1, keepdims=True)
            m_sc[g] = m_next
            pv = jnp.dot(p.astype(jnp.bfloat16), vals, preferred_element_type=jnp.float32)
            acc_sc[g] = acc_sc[g] * alpha[:, :HD] + pv

        @pl.when(last)
        def _():
            lane = lax.broadcasted_iota(jnp.int32, (span_rows, page_rows), 1)
            st = jnp.zeros((span_rows, page_rows), jnp.float32)
            for g in range(GROUP):
                l_g = l_sc[g]
                safe = jnp.where(l_g > 0.0, l_g, 1.0)
                o_ref[0, :, g * HD:(g + 1) * HD] = (acc_sc[g] / safe[:, :HD]).astype(o_ref.dtype)
                st = jnp.where(lane == g, m_sc[g], st)
                st = jnp.where(lane == GROUP + g, l_g, st)
            st_ref[0] = st[:, :2 * GROUP]

    grid_spec = pltpu.PrefetchScalarGridSpec(
        num_scalar_prefetch=4,
        grid=(slots,),
        in_specs=[
            pl.BlockSpec((1, span_rows, qw), lambda i, sr, pm, ks, qs: (sr[i], 0, 0)),
            pl.BlockSpec((1, page_rows, 2 * HD), lambda i, sr, pm, ks, qs: (pm[i], 0, 0)),
        ],
        out_specs=[
            pl.BlockSpec((1, span_rows, qw), lambda i, sr, pm, ks, qs: (sr[i], 0, 0)),
            pl.BlockSpec((1, span_rows, 2 * GROUP), lambda i, sr, pm, ks, qs: (sr[i], 0, 0)),
        ],
        scratch_shapes=[
            pltpu.VMEM((GROUP, span_rows, page_rows), jnp.float32),
            pltpu.VMEM((GROUP, span_rows, page_rows), jnp.float32),
            pltpu.VMEM((GROUP, span_rows, HD), jnp.float32),
        ],
    )
    return pl.pallas_call(
        kernel,
        grid_spec=grid_spec,
        out_shape=[
            jax.ShapeDtypeStruct((reqs, span_rows, qw), jnp.bfloat16),
            jax.ShapeDtypeStruct((reqs, span_rows, 2 * GROUP), jnp.float32),
        ],
        compiler_params=pltpu.CompilerParams(dimension_semantics=("arbitrary",)),
    )(sreq, perm, kstart, qstart, packed, pages)


def body(hidden, qkv_weight, out_weight, kv_pages, cache_pages, slot_order):
    whole = lax.all_gather(hidden, "tp", axis=1, tiled=True)
    tok_rows = whole.shape[0]
    projected = jnp.dot(
        whole,
        lax.all_gather(qkv_weight, "req", axis=0, tiled=True),
        preferred_element_type=jnp.float32,
    )
    local_slots = kv_pages.shape[0]
    page_rows = kv_pages.shape[1]
    lane_width = kv_pages.shape[2]
    kv_heads = lane_width // (2 * HD)
    assert kv_heads == 1 and tok_rows == SPAN
    new_pages = SPAN // page_rows
    requests = cache_pages.shape[0]
    my_index = lax.axis_index("req")
    query_start = cache_pages * page_rows
    home_start = lax.dynamic_slice_in_dim(query_start, my_index, 1, 0)
    projected = projected.reshape(SPAN, GROUP + 2, HD)
    positions = (home_start + jnp.arange(SPAN, dtype=jnp.int32))[:, None]
    rotated = rotary(projected[:, : GROUP + 1, :], positions)
    scale = jnp.concatenate(
        [jnp.full((GROUP, 1), 1.0 / math.sqrt(HD), jnp.float32), jnp.ones((1, 1), jnp.float32)], axis=0
    )
    rotated = (rotated * scale).astype(jnp.bfloat16)
    value_new = projected[:, GROUP + 1 :, :].astype(jnp.bfloat16)
    packed = jnp.concatenate([rotated, value_new], axis=1).reshape(1, SPAN, (GROUP + 2) * HD)
    packed_all = lax.all_gather(packed, "req", axis=0, tiled=True)
    fresh_all = packed_all[:, :, GROUP * HD :]

    my_slots = my_index * local_slots + jnp.arange(local_slots, dtype=jnp.int32)
    slot_req, page_index, cached = locate(my_slots, cache_pages, slot_order, new_pages)
    pages_out = write_pages(kv_pages, fresh_all, slot_req, page_index, cached, new_pages)

    perm = jnp.argsort(slot_req, stable=True).astype(jnp.int32)
    sreq = slot_req[perm].astype(jnp.int32)
    kstart = (page_index[perm] * page_rows).astype(jnp.int32)
    part_o, part_st = slot_attention(sreq, perm, kstart, query_start.astype(jnp.int32), packed_all, pages_out)

    got_o = lax.all_to_all(part_o, "req", 0, 0, tiled=True)
    got_st = lax.all_to_all(part_st, "req", 0, 0, tiled=True)

    all_slots = jnp.arange(slot_order.shape[0], dtype=jnp.int32)
    all_req, unused_index, unused_cached = locate(all_slots, cache_pages, slot_order, new_pages)
    holds = (all_req.reshape(-1, local_slots) == my_index).any(axis=1)
    valid = holds[:, None, None]
    m_parts = jnp.where(valid, got_st[:, :, :GROUP], NEG_BIG)
    l_parts = jnp.where(valid, got_st[:, :, GROUP:], 0.0)
    top = jnp.max(m_parts, axis=0)
    w = l_parts * jnp.exp(m_parts - top[None])
    den = jnp.sum(w, axis=0)
    o_parts = jnp.where(valid[..., None], got_o.reshape(requests, SPAN, GROUP, HD).astype(jnp.float32), 0.0)
    num = jnp.sum(o_parts * w[..., None], axis=0)
    attention_flat = (num / den[..., None]).astype(jnp.bfloat16).reshape(SPAN, GROUP * HD)

    head_terms = jnp.dot(
        attention_flat,
        lax.all_gather(out_weight, "req", axis=1, tiled=True),
        preferred_element_type=jnp.float32,
    )
    attention_out = lax.psum_scatter(
        head_terms.astype(jnp.bfloat16), "tp", scatter_dimension=1, tiled=True
    )
    return (attention_out, pages_out)


def solution(mesh):
    return jax.shard_map(
        body,
        mesh=mesh,
        in_specs=(P("req", "tp"), P("req", "tp"), P("tp", "req"), P("req", None, "tp"), P(), P()),
        out_specs=(P("req", "tp"), P("req", None, "tp")),
        check_vma=False,
    )
```

time: 886 us -> 375 us (0.42)
  waiting for transfers between devices: 766 us -> 219 us
  Pallas kernels: 0 us -> 76 us
  other arithmetic: 45.5 us -> 16.4 us
  matrix products: 28 us -> 6.35 us
  blocking collectives: 0 us -> 14.4 us
    reduce_scatter x1, waiting for transfers between devices: 456 us -> 33.3 us  [body(): lax.psum_scatter(head_terms.astype(jnp.bfloat16), 'tp', scatter_dimension...]
    all_gather x2 -> x1, waiting for transfers between devices: 235 us -> 57.4 us  [body(): packed_all = lax.all_gather(packed, 'req', axis=0, tiled=True)]
    pallas_call x0 -> x1, Pallas kernels: none -> 76 us  [slot_attention(): pl.pallas_call(kernel, grid_spec=grid_spec, out_shape=[jax.ShapeDtypeStru...]
    all_to_all x0 -> x1, waiting for transfers between devices: none -> 40 us  [body(): got_o = lax.all_to_all(part_o, 'req', 0, 0, tiled=True)]
    dot_general x20 -> x0, matrix products: 21.6 us -> none  [the longest x10 12.4 us: block_terms(): jnp.einsum('bkgcp,bpkd->bckgd', weights, value_rows, preferred_element_ty...]
    gather x30 -> x2, local copies, waits for them, and re-layouts: 21.3 us -> 2.06 us  [the longest x1 1.28 us: body(): sreq = slot_req[perm].astype(jnp.int32)]
    all_to_all x0 -> x1, blocking collectives: none -> 14.4 us  [body(): got_st = lax.all_to_all(part_st, 'req', 0, 0, tiled=True)]
    all_gather x1, waiting for transfers between devices: 0.02 us -> 14 us  [body(): lax.all_gather(out_weight, 'req', axis=1, tiled=True)]
  transfers between devices with their start and end apart: 6 -> 6, of which waited for: 5 -> 6; matrix products, arithmetic and copies ran while one was open for 10% -> 8% of each run, Pallas kernels for 0% -> 0%
where the time goes in v1:
time: 375 us
  waiting for transfers between devices  219 us (58%)
  Pallas kernels  76 us (20%)
  local copies, waits for them, and re-layouts  24.1 us (6%)
  other arithmetic  16.4 us (4%)
  blocking collectives  14.4 us (4%)
  between operations  14 us (4%)
  matrix products  6.35 us (2%)
  starting transfers between devices  4.72 us (1%)
    pallas_call x1, Pallas kernels, slot_attention(): pl.pallas_call(kernel, grid_spec=grid_spec, out_shape=[jax.ShapeDtypeStru...  76 us
    all_gather x1, waiting for transfers between devices, body(): packed_all = lax.all_gather(packed, 'req', axis=0, tiled=True)  57.4 us
    all_gather x1, waiting for transfers between devices, body(): lax.all_gather(qkv_weight, 'req', axis=0, tiled=True)  44.6 us
    all_to_all x1, waiting for transfers between devices, body(): got_o = lax.all_to_all(part_o, 'req', 0, 0, tiled=True)  40 us
    reduce_scatter x1, waiting for transfers between devices, body(): lax.psum_scatter(head_terms.astype(jnp.bfloat16), 'tp', scatter_dimension...  33.3 us
    all_gather x1, waiting for transfers between devices, body(): whole = lax.all_gather(hidden, 'tp', axis=1, tiled=True)  27.8 us
    all_to_all x1, blocking collectives, body(): got_st = lax.all_to_all(part_st, 'req', 0, 0, tiled=True)  14.4 us
    all_gather x1, waiting for transfers between devices, body(): lax.all_gather(out_weight, 'req', axis=1, tiled=True)  14 us
  transfers between devices with their start and end apart: 6, of which 6 were waited for; matrix products, arithmetic and copies ran while one was open for 8% of the time, Pallas kernels for 0%

profile of v1, /device:TPU:0, one launch (start us, length us, event | category | flops | bytes accessed | tf_op | source)
XLA Modules:
  0.0 374.9 jit_solution(8957718522891573744)
XLA Ops:
  7.2 0.7 all-gather.7.cloned.1.call-update
  7.9 0.7 all-gather.5.cloned.1.call-update
  11.8 44.6 %all-gather.7.cloned.1.call-done = bf16[2048,384]{1,0:T(8,128)(2,1)} async-done(((bf16[128,384]{1,0:T(8,128)(2,1)}), bf16[2048,384]{1,0:T(8,128)(2,1)}) %all-gather.7.cloned.1.call-update) | async-done | bytes 1572880 | tf_op jit(solution)/shard_map/all_gather | solution.py:150
  56.5 27.8 %all-gather.5.cloned.1.call-done = bf16[512,2048]{1,0:T(8,128)(2,1)} async-done(((bf16[512,256]{1,0:T(8,128)(2,1)}), bf16[512,2048]{1,0:T(8,128)(2,1)}) %all-gather.5.cloned.1.call-update) | async-done | bytes 2097168 | tf_op jit(solution)/shard_map/all_gather | solution.py:146
  84.3 3.1 fusion.7
  87.7 0.9 copy.24
  88.9 2.0 sort.17
  91.0 1.3 gather_fusion
  92.4 0.8 gather_fusion.1
  93.7 57.4 %all-gather.9.cloned.1.call-done.q_ref = bf16[16,512,384]{2,1,0:T(8,128)(2,1)} async-done(((bf16[1,512,384]{2,1,0:T(8,128)(2,1)}), bf16[16,512,384]{2,1,0:T(8,128)(2,1)}) %all-gather.9.cloned.1.call-update) | async-done | bytes 6291472 | tf_op jit(solution)/shard_map/all_gather | solution.py:172
  151.1 1.6 slice-done
  152.7 2.1 gather_fusion.2
  154.8 3.8 %broadcast_select_fusion.page_ref = bf16[64,128,128]{2,1,0:T(8,128)(2,1)} fusion(bf16[64,128,128]{2,1,0:T(8,128)(2,1)} %gather_fusion.2, bf16[64,128,128]{2,1,0:T(8,128)(2,1)} %param.9, pred[64]{0:T(512)(128)(4,1)S(1)} %get-tuple-element.12), kind=kLoop, calls=%fused_computation.7 | loop fusion | flops 1048576 | bytes 6291520 | tf_op jit(solution)/shard_map/jit(_where)/select_n | solution.py:60
  158.7 76.0 %shard_map.77 = (bf16[16,512,256]{2,1,0:T(8,128)(2,1)}, f32[16,512,8]{2,1,0:T(8,128)}) custom-call(s32[64]{0:T(128)} %gather_fusion, s32[64]{0:T(128)} %copy-done.4, s32[64]{0:T(128)} %broadcast_multiply_fusion.1.kstart_ref, s32[16]{0:T(128)} %copy-done.1, bf16[16,512,384]{2,1,0:T(8,128)(2,1)} %all-gather.9.cloned.1.call-done.q_ref, ...), custom_call_target="tpu_custom_call" | custom-call | tf_op jit(solution)/shard_map/pallas_call | solution.py:134
  234.7 2.8 copy.25
  237.5 14.4 %all_to_all.10 = f32[16,512,8]{1,2,0:T(8,128)S(1)} all-to-all(f32[16,512,8]{1,2,0:T(8,128)S(1)} %copy.25), channel_id=1, replica_groups=mesh['req'=16,'tp'=8] {'req'}, dimensions={0} | all-to-all | bytes 524288 | tf_op jit(solution)/shard_map/all_to_all | solution.py:185
  251.9 4.5 %all-to-all-start = ((bf16[16,512,256]{2,1,0:T(8,128)(2,1)}), bf16[16,512,256]{2,1,0:T(8,128)(2,1)}, u32[]{:S(2)}, u32[]{:S(2)}) async-start(bf16[16,512,256]{2,1,0:T(8,128)(2,1)} %get-tuple-element.6), calls=%async_computation | async-start | bytes 8388608 | tf_op jit(solution)/shard_map/all_to_all | solution.py:184
  258.2 4.3 %mul.118 = f32[16,512,4,64]{1,3,2,0:T(8,128)} broadcast(f32[16,512,4]{1,2,0:T(4,128)S(1)} %get-tuple-element.11), dimensions={0,1,2} | broadcast | bytes 8519680 | tf_op jit(solution)/shard_map/mul | solution.py:197
  262.4 9.3 %copy.26 = f32[16,512,256]{2,1,0:T(8,128)} copy(f32[16,512,256]{1,2,0:T(8,128)} %bitcast.15) | data formatting | bytes 16777216 | tf_op jit(solution)/shard_map/mul | solution.py:197
  272.0 40.0 %all-to-all-done = bf16[16,512,256]{2,1,0:T(8,128)(2,1)} async-done(((bf16[16,512,256]{2,1,0:T(8,128)(2,1)}), bf16[16,512,256]{2,1,0:T(8,128)(2,1)}, u32[]{:S(2)}, u32[]{:S(2)}) %all-to-all-start) | async-done | bytes 4194336 | tf_op jit(solution)/shard_map/all_to_all | solution.py:184
  312.0 5.9 %multiply_reduce_fusion = f32[512,256]{1,0:T(8,128)S(1)} fusion(f32[16,512,256]{2,1,0:T(8,128)} %copy.26, bf16[16,512,256]{2,1,0:T(8,128)(2,1)} %all-to-all-done, pred[16]{0:T(512)(128)(4,1)S(1)} %reduce_or.9), kind=kLoop, calls=%fused_computation.3 | loop fusion | flops 8257536 | bytes 13107216 | tf_op jit(solution)/shard_map/reduce_sum | solution.py:197
  317.8 14.0 %all-gather.11.cloned.1.call-done = bf16[256,2048]{1,0:T(8,128)(2,1)} async-done(((bf16[256,128]{1,0:T(8,128)(2,1)}), bf16[256,2048]{1,0:T(8,128)(2,1)}) %all-gather.11.cloned.1.call-update) | async-done | bytes 1048592 | tf_op jit(solution)/shard_map/all_gather | solution.py:202
  331.8 3.3 convolution_convert_fusion
  335.1 33.3 %reduce-scatter.2.cloned.1.call-done = bf16[512,256]{1,0:T(8,128)(2,1)} async-done(((bf16[512,2048]{1,0:T(8,128)(2,1)}), bf16[512,256]{1,0:T(8,128)(2,1)}) %reduce-scatter.2.cloned.1.call-update) | async-done | bytes 262160 | tf_op jit(solution)/shard_map/reduce_scatter | solution.py:205
  (53 shorter events, 6.4 us)
Async XLA Ops:
  7.2 49.3 %all-gather.7.cloned.1.call-start = ((), (), s32[]{:S(2)}) async-start(), calls=%async_computation.4 | async-start | bytes 1671168 | tf_op jit(solution)/shard_map/all_gather | solution.py:150
  7.9 76.4 %all-gather.5.cloned.1.call-start = ((), (), s32[]{:S(2)}) async-start(), calls=%async_computation.3 | async-start | bytes 2359296 | tf_op jit(solution)/shard_map/all_gather | solution.py:146
  8.6 142.5 %all-gather.9.cloned.1.call-start = ((), (), s32[]{:S(2)}) async-start(), calls=%async_computation.5 | async-start | bytes 6684672 | tf_op jit(solution)/shard_map/all_gather | solution.py:172
  10.3 77.1 %copy-start.1 = (s32[16]{0:T(128)}, s32[16]{0:T(128)S(1)}, u32[]{:S(2)}) copy-start(s32[16]{0:T(128)S(1)} %get-tuple-element.18.qstart_ref) | copy-start | bytes 196
  11.8 75.6 %copy-start.3 = (f32[5]{0:T(128)S(1)}, f32[5]{0:T(128)}, u32[]{:S(2)}) copy-start(f32[5]{0:T(128)} %constant.14.clone.1) | copy-start | bytes 64
  87.4 1.3 copy-start
  87.5 4.8 %copy-start.2 = (s32[16]{0:T(128)S(1)}, s32[16]{0:T(128)}, u32[]{:S(2)}) copy-start(s32[16]{0:T(128)} %param.10) | copy-start | bytes 196
  91.0 60.2 %copy-start.4 = (s32[64]{0:T(128)}, s32[64]{0:T(128)S(1)}, u32[]{:S(2)}) copy-start(s32[64]{0:T(128)S(1)} %get-tuple-element.5.perm_ref) | copy-start | bytes 772
  151.1 1.6 slice-start
  251.9 60.1 %all-to-all-start = ((bf16[16,512,256]{2,1,0:T(8,128)(2,1)}), bf16[16,512,256]{2,1,0:T(8,128)(2,1)}, u32[]{:S(2)}, u32[]{:S(2)}) async-start(bf16[16,512,256]{2,1,0:T(8,128)(2,1)} %get-tuple-element.6), calls=%async_computation | async-start | bytes 8388608 | tf_op jit(solution)/shard_map/all_to_all | solution.py:184
  256.5 75.4 %all-gather.11.cloned.1.call-start = ((), (), s32[]{:S(2)}) async-start(), calls=%async_computation.6 | async-start | bytes 1114112 | tf_op jit(solution)/shard_map/all_gather | solution.py:202
  257.0 111.4 %reduce-scatter.2.cloned.1.call-start = ((), (), s32[]{:S(2)}) async-start(), calls=%async_computation.7 | async-start | bytes 2359296 | tf_op jit(solution)/shard_map/reduce_scatter | solution.py:205
Sparse Core Ops, SparseCore 0:
  10.2 46.2 all-gather.6
  58.2 26.0 all-gather.4
  88.7 62.3 all-gather.8
  259.1 72.7 all-gather.10
  335.3 33.1 reduce-scatter.1

commit v2 on v1

--- a/solution.py
+++ b/solution.py
@@ -86,21 +86,37 @@
         keys = page[:, :HD]
         vals = page[:, HD:]
         q_all = q_ref[0]
-        row = lax.broadcasted_iota(jnp.int32, (span_rows, page_rows), 0) + qst
-        col = lax.broadcasted_iota(jnp.int32, (span_rows, page_rows), 1) + kst
-        vis = col <= row
-        for g in range(GROUP):
-            qg = q_all[:, g * HD:(g + 1) * HD]
-            s = lax.dot_general(qg, keys, (((1,), (1,)), ((), ())), preferred_element_type=jnp.float32)
-            s = jnp.where(vis, s, NEG_BIG)
-            m_prev = m_sc[g]
-            m_next = jnp.maximum(m_prev, jnp.max(s, axis=1, keepdims=True))
-            alpha = jnp.exp(m_prev - m_next)
-            p = jnp.where(vis, jnp.exp(s - m_next), 0.0)
-            l_sc[g] = alpha * l_sc[g] + jnp.sum(p, axis=1, keepdims=True)
-            m_sc[g] = m_next
-            pv = jnp.dot(p.astype(jnp.bfloat16), vals, preferred_element_type=jnp.float32)
-            acc_sc[g] = acc_sc[g] * alpha[:, :HD] + pv
+
+        def update(masked):
+            if masked:
+                row = lax.broadcasted_iota(jnp.int32, (span_rows, page_rows), 0) + qst
+                col = lax.broadcasted_iota(jnp.int32, (span_rows, page_rows), 1) + kst
+                vis = col <= row
+            for g in range(GROUP):
+                qg = q_all[:, g * HD:(g + 1) * HD]
+                s = lax.dot_general(qg, keys, (((1,), (1,)), ((), ())), preferred_element_type=jnp.float32)
+                if masked:
+                    s = jnp.where(vis, s, NEG_BIG)
+                m_prev = m_sc[g]
+                m_next = jnp.maximum(m_prev, jnp.max(s, axis=1, keepdims=True))
+                alpha = jnp.exp(m_prev - m_next)
+                p = jnp.exp(s - m_next)
+                if masked:
+                    p = jnp.where(vis, p, 0.0)
+                l_sc[g] = alpha * l_sc[g] + jnp.sum(p, axis=1, keepdims=True)
+                m_sc[g] = m_next
+                pv = jnp.dot(p.astype(jnp.bfloat16), vals, preferred_element_type=jnp.float32)
+                acc_sc[g] = acc_sc[g] * alpha[:, :HD] + pv
+
+        partial = kst + (page_rows - 1) > qst
+
+        @pl.when(partial)
+        def _():
+            update(True)
+
+        @pl.when(jnp.logical_not(partial))
+        def _():
+            update(False)
 
         @pl.when(last)
         def _():
@@ -145,11 +161,15 @@
 def body(hidden, qkv_weight, out_weight, kv_pages, cache_pages, slot_order):
     whole = lax.all_gather(hidden, "tp", axis=1, tiled=True)
     tok_rows = whole.shape[0]
-    projected = jnp.dot(
-        whole,
-        lax.all_gather(qkv_weight, "req", axis=0, tiled=True),
-        preferred_element_type=jnp.float32,
-    )
+    n_req = lax.axis_size("req")
+    qkv_size = qkv_weight.size
+    both = jnp.concatenate([qkv_weight.reshape(1, -1), out_weight.reshape(1, -1)], axis=1)
+    both = lax.all_gather(both, "req", axis=0, tiled=True)
+    qkv_full = both[:, :qkv_size].reshape(n_req * qkv_weight.shape[0], qkv_weight.shape[1])
+    out_full = jnp.moveaxis(
+        both[:, qkv_size:].reshape(n_req, out_weight.shape[0], out_weight.shape[1]), 0, 1
+    ).reshape(out_weight.shape[0], n_req * out_weight.shape[1])
+    projected = jnp.dot(whole, qkv_full, preferred_element_type=jnp.float32)
     local_slots = kv_pages.shape[0]
     page_rows = kv_pages.shape[1]
     lane_width = kv_pages.shape[2]
@@ -181,8 +201,18 @@
     kstart = (page_index[perm] * page_rows).astype(jnp.int32)
     part_o, part_st = slot_attention(sreq, perm, kstart, query_start.astype(jnp.int32), packed_all, pages_out)
 
-    got_o = lax.all_to_all(part_o, "req", 0, 0, tiled=True)
-    got_st = lax.all_to_all(part_st, "req", 0, 0, tiled=True)
+    hi = lax.reduce_precision(part_st, exponent_bits=8, mantissa_bits=7)
+    rest = part_st - hi
+    mid = lax.reduce_precision(rest, exponent_bits=8, mantissa_bits=7)
+    lo = rest - mid
+    hi, mid, lo = (t.astype(jnp.bfloat16) for t in (hi, mid, lo))
+    st_rows = (SPAN * 3 * 2 * GROUP) // (GROUP * HD)
+    st_bits = jnp.concatenate([hi, mid, lo], axis=2).reshape(requests, st_rows, GROUP * HD)
+    sent = jnp.concatenate([part_o, st_bits], axis=1)
+    got = lax.all_to_all(sent, "req", 0, 0, tiled=True)
+    got_o = got[:, :SPAN]
+    got_bits = got[:, SPAN:].reshape(requests, SPAN, 3, 2 * GROUP).astype(jnp.float32)
+    got_st = (got_bits[:, :, 0] + got_bits[:, :, 1]) + got_bits[:, :, 2]
 
     all_slots = jnp.arange(slot_order.shape[0], dtype=jnp.int32)
     all_req, unused_index, unused_cached = locate(all_slots, cache_pages, slot_order, new_pages)
@@ -197,11 +227,7 @@
     num = jnp.sum(o_parts * w[..., None], axis=0)
     attention_flat = (num / den[..., None]).astype(jnp.bfloat16).reshape(SPAN, GROUP * HD)
 
-    head_terms = jnp.dot(
-        attention_flat,
-        lax.all_gather(out_weight, "req", axis=1, tiled=True),
-        preferred_element_type=jnp.float32,
-    )
+    head_terms = jnp.dot(attention_flat, out_full, preferred_element_type=jnp.float32)
     attention_out = lax.psum_scatter(
         head_terms.astype(jnp.bfloat16), "tp", scatter_dimension=1, tiled=True
     )

time: 375 us -> 418 us (1.11)
  waiting for transfers between devices: 219 us -> 239 us
  local copies, waits for them, and re-layouts: 24.1 us -> 41.5 us
  other arithmetic: 16.4 us -> 33.1 us
  blocking collectives: 14.4 us -> 0 us
    all_to_all x1, waiting for transfers between devices: 40 us -> 67.6 us  [body(): got = lax.all_to_all(sent, 'req', 0, 0, tiled=True)]
    all_to_all x1 -> x0, blocking collectives: 14.4 us -> none  [body(): got_st = lax.all_to_all(part_st, 'req', 0, 0, tiled=True)]
    unnamed x10 -> x17, local copies, waits for them, and re-layouts: 0.03 us -> 10.4 us
    all_gather x1, waiting for transfers between devices: 27.8 us -> 20.1 us  [body(): whole = lax.all_gather(hidden, 'tp', axis=1, tiled=True)]
    concatenate x0 -> x2, other arithmetic: none -> 6.47 us  [the longest x1 4.55 us: body(): sent = jnp.concatenate([part_o, st_bits], axis=1)]
    reshape x0 -> x3, local copies, waits for them, and re-layouts: none -> 5.36 us  [the longest x1 3.88 us: body(): jnp.concatenate([hi, mid, lo], axis=2)]
    convert_element_type x0 -> x3, other arithmetic: none -> 4.95 us  [the longest x1 3.83 us: body(): hi, mid, lo = (t.astype(jnp.bfloat16) for t in (hi, mid, lo))]
    all_gather x2 -> x1, waiting for transfers between devices: 58.6 us -> 55.4 us  [body(): both = lax.all_gather(both, 'req', axis=0, tiled=True)]
  transfers between devices with their start and end apart: 6 -> 5, of which waited for: 6 -> 5; matrix products, arithmetic and copies ran while one was open for 8% -> 4% of each run, Pallas kernels for 0% -> 0%
where the time goes in v2:
time: 418 us; the launch traced here: 417 us
  waiting for transfers between devices  239 us (57%)
  Pallas kernels  79.3 us (19%)
  local copies, waits for them, and re-layouts  41.5 us (10%)
  other arithmetic  33.1 us (8%)
  between operations  14 us (3%)
  starting transfers between devices  5.66 us (1%)
  matrix products  4.72 us (1%)
    pallas_call x1, Pallas kernels, slot_attention(): pl.pallas_call(kernel, grid_spec=grid_spec, out_shape=[jax.ShapeDtypeStru...  79.3 us
    all_to_all x1, waiting for transfers between devices, body(): got = lax.all_to_all(sent, 'req', 0, 0, tiled=True)  67.6 us
    all_gather x1, waiting for transfers between devices, body(): packed_all = lax.all_gather(packed, 'req', axis=0, tiled=True)  57.4 us
    all_gather x1, waiting for transfers between devices, body(): both = lax.all_gather(both, 'req', axis=0, tiled=True)  55.4 us
    reduce_scatter x1, waiting for transfers between devices, body(): lax.psum_scatter(head_terms.astype(jnp.bfloat16), 'tp', scatter_dimension...  37.3 us
    all_gather x1, waiting for transfers between devices, body(): whole = lax.all_gather(hidden, 'tp', axis=1, tiled=True)  20.1 us
    mul x2, local copies, waits for them, and re-layouts, body(): num = jnp.sum(o_parts * w[..., None], axis=0)  13.6 us
    unnamed x17, local copies, waits for them, and re-layouts  10.4 us
  transfers between devices with their start and end apart: 5, of which 5 were waited for; matrix products, arithmetic and copies ran while one was open for 4% of the time, Pallas kernels for 0%

profile of v2, /device:TPU:0, one launch (start us, length us, event | category | flops | bytes accessed | tf_op | source)
XLA Modules:
  0.0 417.0 jit_solution(12586663817548750402)
XLA Ops:
  14.2 55.4 %all-gather.9.cloned.1.call-done = bf16[16,1,81920]{2,1,0:T(2,128)(2,1)} async-done(((bf16[1,1,81920]{2,1,0:T(2,128)(2,1)}), bf16[16,1,81920]{2,1,0:T(2,128)(2,1)}) %all-gather.9.cloned.1.call-update) | async-done | bytes 2621456 | tf_op jit(solution)/shard_map/all_gather | solution.py:167
  69.6 5.4 %copy.52 = bf16[16,1,81920]{2,0,1:T(8,128)(2,1)S(1)} copy(bf16[16,1,81920]{2,1,0:T(2,128)(2,1)} %all-gather.9.cloned.1.call-done) | data formatting | bytes 5242880
  75.0 1.5 copy-done
  77.6 20.1 %all-gather.5.cloned.1.call-done = bf16[512,2048]{1,0:T(8,128)(2,1)} async-done(((bf16[512,256]{1,0:T(8,128)(2,1)}), bf16[512,2048]{1,0:T(8,128)(2,1)}) %all-gather.5.cloned.1.call-update) | async-done | bytes 2097168 | tf_op jit(solution)/shard_map/all_gather | solution.py:162
  97.7 2.6 fusion.14
  101.9 2.0 sort.17
  106.7 57.4 %all-gather.7.cloned.1.call-done.q_ref = bf16[16,512,384]{2,1,0:T(8,128)(2,1)} async-done(((bf16[1,512,384]{2,1,0:T(8,128)(2,1)}), bf16[16,512,384]{2,1,0:T(8,128)(2,1)}) %all-gather.7.cloned.1.call-update) | async-done | bytes 6291472 | tf_op jit(solution)/shard_map/all_gather | solution.py:192
  164.1 1.6 slice-done
  165.7 2.1 gather_fusion.2
  167.8 3.8 broadcast_select_fusion.page_ref
  171.7 79.3 %shard_map.77 = (bf16[16,512,256]{2,1,0:T(8,128)(2,1)}, f32[16,512,8]{2,1,0:T(8,128)}) custom-call(s32[64]{0:T(128)} %gather_fusion, s32[64]{0:T(128)} %copy-done.5, s32[64]{0:T(128)} %broadcast_multiply_fusion.1.kstart_ref, s32[16]{0:T(128)} %copy-done.2, bf16[16,512,384]{2,1,0:T(8,128)(2,1)} %all-gather.7.cloned.1.call-done.q_ref, ...), custom_call_target="tpu_custom_call" | custom-call | tf_op jit(solution)/shard_map/pallas_call | solution.py:150
  251.0 3.8 reduce-precision_convert_fusion.1
  254.8 1.9 pad_maximum_fusion.1
  256.8 3.9 reshape.240
  260.6 4.6 %pad_maximum_fusion = bf16[16,560,256]{2,1,0:T(8,128)(2,1)} fusion(bf16[16,48,256]{2,1,0:T(8,128)(2,1)S(1)} %reshape.240, bf16[16,512,256]{2,1,0:T(8,128)(2,1)} %get-tuple-element.6), kind=kLoop, calls=%fused_computation.9 | loop fusion | flops 9175040 | bytes 9175040 | tf_op jit(solution)/shard_map/concatenate | solution.py:211
  265.2 5.3 %all-to-all-start = ((bf16[16,560,256]{2,1,0:T(8,128)(2,1)}), bf16[16,560,256]{2,1,0:T(8,128)(2,1)}, u32[]{:S(2)}, u32[]{:S(2)}) async-start(bf16[16,560,256]{2,1,0:T(8,128)(2,1)} %pad_maximum_fusion), calls=%async_computation | async-start | bytes 9175040 | tf_op jit(solution)/shard_map/all_to_all | solution.py:212
  273.6 67.6 %all-to-all-done = bf16[16,560,256]{2,1,0:T(8,128)(2,1)} async-done(((bf16[16,560,256]{2,1,0:T(8,128)(2,1)}), bf16[16,560,256]{2,1,0:T(8,128)(2,1)}, u32[]{:S(2)}, u32[]{:S(2)}) %all-to-all-start) | async-done | bytes 4587552 | tf_op jit(solution)/shard_map/all_to_all | solution.py:212
  342.3 4.0 copy.40
  346.3 3.2 fusion.2
  351.3 4.3 %mul.118 = f32[16,512,4,64]{1,3,2,0:T(8,128)} broadcast(f32[16,512,4]{1,2,0:T(4,128)S(1)} %copy.41), dimensions={0,1,2} | broadcast | bytes 8519680 | tf_op jit(solution)/shard_map/mul | solution.py:227
  355.6 9.3 %copy.42 = f32[16,512,256]{2,1,0:T(8,128)} copy(f32[16,512,256]{1,2,0:T(8,128)} %bitcast.41) | data formatting | bytes 16777216 | tf_op jit(solution)/shard_map/mul | solution.py:227
  364.9 5.9 %multiply_reduce_fusion = f32[512,256]{1,0:T(8,128)S(1)} fusion(f32[16,512,256]{2,1,0:T(8,128)} %copy.42, bf16[16,560,256]{2,1,0:T(8,128)(2,1)} %all-to-all-done, pred[16]{0:T(512)(128)(4,1)S(1)} %reduce_or.9), kind=kLoop, calls=%fused_computation.4 | loop fusion | flops 8257536 | bytes 13107216 | tf_op jit(solution)/shard_map/reduce_sum | solution.py:227
  371.0 2.1 convolution_convert_fusion
  373.2 37.3 %reduce-scatter.2.cloned.1.call-done = bf16[512,256]{1,0:T(8,128)(2,1)} async-done(((bf16[512,2048]{1,0:T(8,128)(2,1)}), bf16[512,256]{1,0:T(8,128)(2,1)}) %reduce-scatter.2.cloned.1.call-update) | async-done | bytes 262160 | tf_op jit(solution)/shard_map/reduce_scatter | solution.py:231
  (67 shorter events, 18.5 us)
Async XLA Ops:
  7.2 62.5 %all-gather.9.cloned.1.call-start = ((), (), s32[]{:S(2)}) async-start(), calls=%async_computation.5 | async-start | bytes 5570560 | tf_op jit(solution)/shard_map/all_gather | solution.py:167
  10.3 87.4 %all-gather.5.cloned.1.call-start = ((), (), s32[]{:S(2)}) async-start(), calls=%async_computation.2 | async-start | bytes 2359296 | tf_op jit(solution)/shard_map/all_gather | solution.py:162
  11.1 153.1 %all-gather.7.cloned.1.call-start = ((), (), s32[]{:S(2)}) async-start(), calls=%async_computation.3 | async-start | bytes 6684672 | tf_op jit(solution)/shard_map/all_gather | solution.py:192
  12.7 62.3 %copy-start.2 = (s32[16]{0:T(128)}, s32[16]{0:T(128)S(1)}, u32[]{:S(2)}) copy-start(s32[16]{0:T(128)S(1)} %get-tuple-element.19.qstart_ref) | copy-start | bytes 196
  75.0 1.5 copy-start
  77.6 22.9 %copy-start.4 = (f32[5]{0:T(128)S(1)}, f32[5]{0:T(128)}, u32[]{:S(2)}) copy-start(f32[5]{0:T(128)} %constant.14.clone.1) | copy-start | bytes 64
  100.3 1.3 copy-start.1
  100.5 4.8 %copy-start.3 = (s32[16]{0:T(128)S(1)}, s32[16]{0:T(128)}, u32[]{:S(2)}) copy-start(s32[16]{0:T(128)} %param.10) | copy-start | bytes 196
  103.9 60.2 %copy-start.5 = (s32[64]{0:T(128)}, s32[64]{0:T(128)S(1)}, u32[]{:S(2)}) copy-start(s32[64]{0:T(128)S(1)} %get-tuple-element.5.perm_ref) | copy-start | bytes 772
  164.1 1.6 slice-start
  265.2 76.0 %all-to-all-start = ((bf16[16,560,256]{2,1,0:T(8,128)(2,1)}), bf16[16,560,256]{2,1,0:T(8,128)(2,1)}, u32[]{:S(2)}, u32[]{:S(2)}) async-start(bf16[16,560,256]{2,1,0:T(8,128)(2,1)} %pad_maximum_fusion), calls=%async_computation | async-start | bytes 9175040 | tf_op jit(solution)/shard_map/all_to_all | solution.py:212
  270.5 140.0 %reduce-scatter.2.cloned.1.call-start = ((), (), s32[]{:S(2)}) async-start(), calls=%async_computation.4 | async-start | bytes 2359296 | tf_op jit(solution)/shard_map/reduce_scatter | solution.py:231
Sparse Core Ops, SparseCore 0:
  10.7 58.8 all-gather.8
  71.3 26.3 all-gather.4
  101.7 62.3 all-gather.6
  373.3 37.1 reduce-scatter.1

commit v3 on v2

--- a/solution.py
+++ b/solution.py
@@ -61,7 +61,7 @@
 
 
 def slot_attention(sreq, perm, kstart, qstart, packed, pages):
-    reqs, span_rows, _ = packed.shape
+    reqs, _, span_rows = packed.shape
     slots, page_rows, _ = pages.shape
     qw = GROUP * HD
 
@@ -85,28 +85,30 @@
         page = page_ref[0]
         keys = page[:, :HD]
         vals = page[:, HD:]
-        q_all = q_ref[0]
 
         def update(masked):
             if masked:
-                row = lax.broadcasted_iota(jnp.int32, (span_rows, page_rows), 0) + qst
-                col = lax.broadcasted_iota(jnp.int32, (span_rows, page_rows), 1) + kst
-                vis = col <= row
+                key_pos = lax.broadcasted_iota(jnp.int32, (page_rows, span_rows), 0) + kst
+                query_pos = lax.broadcasted_iota(jnp.int32, (page_rows, span_rows), 1) + qst
+                vis = key_pos <= query_pos
             for g in range(GROUP):
-                qg = q_all[:, g * HD:(g + 1) * HD]
-                s = lax.dot_general(qg, keys, (((1,), (1,)), ((), ())), preferred_element_type=jnp.float32)
+                q_g = q_ref[0, g * HD:(g + 1) * HD, :]
+                s = jnp.dot(keys, q_g, preferred_element_type=jnp.float32)
                 if masked:
                     s = jnp.where(vis, s, NEG_BIG)
                 m_prev = m_sc[g]
-                m_next = jnp.maximum(m_prev, jnp.max(s, axis=1, keepdims=True))
+                m_next = jnp.maximum(m_prev, jnp.max(s, axis=0, keepdims=True))
                 alpha = jnp.exp(m_prev - m_next)
                 p = jnp.exp(s - m_next)
                 if masked:
                     p = jnp.where(vis, p, 0.0)
-                l_sc[g] = alpha * l_sc[g] + jnp.sum(p, axis=1, keepdims=True)
+                l_sc[g] = alpha * l_sc[g] + jnp.sum(p, axis=0, keepdims=True)
                 m_sc[g] = m_next
-                pv = jnp.dot(p.astype(jnp.bfloat16), vals, preferred_element_type=jnp.float32)
-                acc_sc[g] = acc_sc[g] * alpha[:, :HD] + pv
+                pv = lax.dot_general(
+                    vals, p.astype(jnp.bfloat16), (((0,), (0,)), ((), ())),
+                    preferred_element_type=jnp.float32,
+                )
+                acc_sc[g] = acc_sc[g] * alpha + pv
 
         partial = kst + (page_rows - 1) > qst
 
@@ -120,39 +122,36 @@
 
         @pl.when(last)
         def _():
-            lane = lax.broadcasted_iota(jnp.int32, (span_rows, page_rows), 1)
-            st = jnp.zeros((span_rows, page_rows), jnp.float32)
             for g in range(GROUP):
                 l_g = l_sc[g]
                 safe = jnp.where(l_g > 0.0, l_g, 1.0)
-                o_ref[0, :, g * HD:(g + 1) * HD] = (acc_sc[g] / safe[:, :HD]).astype(o_ref.dtype)
-                st = jnp.where(lane == g, m_sc[g], st)
-                st = jnp.where(lane == GROUP + g, l_g, st)
-            st_ref[0] = st[:, :2 * GROUP]
+                o_ref[0, g * HD:(g + 1) * HD, :] = (acc_sc[g] / safe).astype(o_ref.dtype)
+                st_ref[0, g:g + 1, :] = m_sc[g]
+                st_ref[0, GROUP + g:GROUP + g + 1, :] = l_g
 
     grid_spec = pltpu.PrefetchScalarGridSpec(
         num_scalar_prefetch=4,
         grid=(slots,),
         in_specs=[
-            pl.BlockSpec((1, span_rows, qw), lambda i, sr, pm, ks, qs: (sr[i], 0, 0)),
+            pl.BlockSpec((1, qw, span_rows), lambda i, sr, pm, ks, qs: (sr[i], 0, 0)),
             pl.BlockSpec((1, page_rows, 2 * HD), lambda i, sr, pm, ks, qs: (pm[i], 0, 0)),
         ],
         out_specs=[
-            pl.BlockSpec((1, span_rows, qw), lambda i, sr, pm, ks, qs: (sr[i], 0, 0)),
-            pl.BlockSpec((1, span_rows, 2 * GROUP), lambda i, sr, pm, ks, qs: (sr[i], 0, 0)),
+            pl.BlockSpec((1, qw, span_rows), lambda i, sr, pm, ks, qs: (sr[i], 0, 0)),
+            pl.BlockSpec((1, 2 * GROUP, span_rows), lambda i, sr, pm, ks, qs: (sr[i], 0, 0)),
         ],
         scratch_shapes=[
-            pltpu.VMEM((GROUP, span_rows, page_rows), jnp.float32),
-            pltpu.VMEM((GROUP, span_rows, page_rows), jnp.float32),
-            pltpu.VMEM((GROUP, span_rows, HD), jnp.float32),
+            pltpu.VMEM((GROUP, 1, span_rows), jnp.float32),
+            pltpu.VMEM((GROUP, 1, span_rows), jnp.float32),
+            pltpu.VMEM((GROUP, HD, span_rows), jnp.float32),
         ],
     )
     return pl.pallas_call(
         kernel,
         grid_spec=grid_spec,
         out_shape=[
-            jax.ShapeDtypeStruct((reqs, span_rows, qw), jnp.bfloat16),
-            jax.ShapeDtypeStruct((reqs, span_rows, 2 * GROUP), jnp.float32),
+            jax.ShapeDtypeStruct((reqs, qw, span_rows), jnp.bfloat16),
+            jax.ShapeDtypeStruct((reqs, 2 * GROUP, span_rows), jnp.float32),
         ],
         compiler_params=pltpu.CompilerParams(dimension_semantics=("arbitrary",)),
     )(sreq, perm, kstart, qstart, packed, pages)
@@ -188,9 +187,11 @@
     )
     rotated = (rotated * scale).astype(jnp.bfloat16)
     value_new = projected[:, GROUP + 1 :, :].astype(jnp.bfloat16)
-    packed = jnp.concatenate([rotated, value_new], axis=1).reshape(1, SPAN, (GROUP + 2) * HD)
+    q_t = jnp.transpose(rotated[:, :GROUP, :], (1, 2, 0)).reshape(GROUP * HD, SPAN)
+    fresh = jnp.concatenate([rotated[:, GROUP:, :], value_new], axis=1).reshape(2 * HD, SPAN)
+    packed = jnp.concatenate([q_t, fresh], axis=0)[None]
     packed_all = lax.all_gather(packed, "req", axis=0, tiled=True)
-    fresh_all = packed_all[:, :, GROUP * HD :]
+    fresh_all = packed_all[:, GROUP * HD :, :].reshape(requests, SPAN, 2 * HD)
 
     my_slots = my_index * local_slots + jnp.arange(local_slots, dtype=jnp.int32)
     slot_req, page_index, cached = locate(my_slots, cache_pages, slot_order, new_pages)
@@ -205,27 +206,26 @@
     rest = part_st - hi
     mid = lax.reduce_precision(rest, exponent_bits=8, mantissa_bits=7)
     lo = rest - mid
-    hi, mid, lo = (t.astype(jnp.bfloat16) for t in (hi, mid, lo))
-    st_rows = (SPAN * 3 * 2 * GROUP) // (GROUP * HD)
-    st_bits = jnp.concatenate([hi, mid, lo], axis=2).reshape(requests, st_rows, GROUP * HD)
-    sent = jnp.concatenate([part_o, st_bits], axis=1)
+    sent = jnp.concatenate([part_o] + [t.astype(jnp.bfloat16) for t in (hi, mid, lo)], axis=1)
     got = lax.all_to_all(sent, "req", 0, 0, tiled=True)
-    got_o = got[:, :SPAN]
-    got_bits = got[:, SPAN:].reshape(requests, SPAN, 3, 2 * GROUP).astype(jnp.float32)
-    got_st = (got_bits[:, :, 0] + got_bits[:, :, 1]) + got_bits[:, :, 2]
+    qw = GROUP * HD
+    got_o = got[:, :qw].reshape(requests, GROUP, HD, SPAN)
+    got_bits = got[:, qw:].reshape(requests, 3, 2 * GROUP, SPAN).astype(jnp.float32)
+    got_st = (got_bits[:, 0] + got_bits[:, 1]) + got_bits[:, 2]
 
     all_slots = jnp.arange(slot_order.shape[0], dtype=jnp.int32)
     all_req, unused_index, unused_cached = locate(all_slots, cache_pages, slot_order, new_pages)
     holds = (all_req.reshape(-1, local_slots) == my_index).any(axis=1)
     valid = holds[:, None, None]
-    m_parts = jnp.where(valid, got_st[:, :, :GROUP], NEG_BIG)
-    l_parts = jnp.where(valid, got_st[:, :, GROUP:], 0.0)
+    m_parts = jnp.where(valid, got_st[:, :GROUP], NEG_BIG)
+    l_parts = jnp.where(valid, got_st[:, GROUP:], 0.0)
     top = jnp.max(m_parts, axis=0)
     w = l_parts * jnp.exp(m_parts - top[None])
     den = jnp.sum(w, axis=0)
-    o_parts = jnp.where(valid[..., None], got_o.reshape(requests, SPAN, GROUP, HD).astype(jnp.float32), 0.0)
-    num = jnp.sum(o_parts * w[..., None], axis=0)
-    attention_flat = (num / den[..., None]).astype(jnp.bfloat16).reshape(SPAN, GROUP * HD)
+    o_parts = jnp.where(valid[..., None], got_o.astype(jnp.float32), 0.0)
+    num = jnp.sum(o_parts * w[:, :, None, :], axis=0)
+    attention_t = (num / den[:, None, :]).astype(jnp.bfloat16)
+    attention_flat = jnp.transpose(attention_t, (2, 0, 1)).reshape(SPAN, GROUP * HD)
 
     head_terms = jnp.dot(attention_flat, out_full, preferred_element_type=jnp.float32)
     attention_out = lax.psum_scatter(

time: 418 us -> 390 us (0.933)
  local copies, waits for them, and re-layouts: 41.5 us -> 26.5 us
  other arithmetic: 33.1 us -> 21.8 us
    mul x3 -> x0, local copies, waits for them, and re-layouts: 13.9 us -> none  [the longest x2 13.6 us: body(): num = jnp.sum(o_parts * w[..., None], axis=0)]
    reshape x2 -> x1, local copies, waits for them, and re-layouts: 4.8 us -> 0.21 us  [body(): jnp.concatenate([rotated[:, GROUP:, :], value_new], axis=1)]
    another operation x1 -> x2, local copies, waits for them, and re-layouts: 0.09 us -> 4.45 us  [the longest x1 4.37 us: write_pages(): fresh_pages = fresh.reshape(-1, page_rows, lane_width)]
    unnamed x17 -> x15, local copies, waits for them, and re-layouts: 10.4 us -> 7.62 us
  transfers between devices with their start and end apart: 5 -> 5, of which waited for: 5 -> 5; matrix products, arithmetic and copies ran while one was open for 4% -> 5% of each run, Pallas kernels for 0% -> 0%
where the time goes in v3:
time: 390 us; the launch traced here: 389 us
  waiting for transfers between devices  238 us (61%)
  Pallas kernels  78 us (20%)
  local copies, waits for them, and re-layouts  26.5 us (7%)
  other arithmetic  21.8 us (6%)
  between operations  14 us (4%)
  starting transfers between devices  5.38 us (1%)
  matrix products  5.2 us (1%)
    pallas_call x1, Pallas kernels, slot_attention(): pl.pallas_call(kernel, grid_spec=grid_spec, out_shape=[jax.ShapeDtypeStru...  78 us
    all_to_all x1, waiting for transfers between devices, body(): got = lax.all_to_all(sent, 'req', 0, 0, tiled=True)  68.9 us
    all_gather x1, waiting for transfers between devices, body(): packed_all = lax.all_gather(packed, 'req', axis=0, tiled=True)  57.4 us
    all_gather x1, waiting for transfers between devices, body(): both = lax.all_gather(both, 'req', axis=0, tiled=True)  55.4 us
    reduce_scatter x1, waiting for transfers between devices, body(): lax.psum_scatter(head_terms.astype(jnp.bfloat16), 'tp', scatter_dimension...  37.2 us
    all_gather x1, waiting for transfers between devices, body(): whole = lax.all_gather(hidden, 'tp', axis=1, tiled=True)  18.7 us
  transfers between devices with their start and end apart: 5, of which 5 were waited for; matrix products, arithmetic and copies ran while one was open for 5% of the time, Pallas kernels for 0%

profile of v3, /device:TPU:0, one launch (start us, length us, event | category | flops | bytes accessed | tf_op | source)
XLA Modules:
  0.0 389.3 jit_solution(5257429675819674106)
XLA Ops:
  8.2 1.0 copy.26
  9.2 1.1 maximum_bitcast_fusion
  14.2 55.4 %all-gather.10.cloned.1.call-done = bf16[16,1,81920]{2,1,0:T(2,128)(2,1)} async-done(((bf16[1,1,81920]{2,1,0:T(2,128)(2,1)}), bf16[16,1,81920]{2,1,0:T(2,128)(2,1)}) %all-gather.10.cloned.1.call-update) | async-done | bytes 2621456 | tf_op jit(solution)/shard_map/all_gather | solution.py:166
  69.6 5.4 %copy.31 = bf16[16,1,81920]{2,0,1:T(8,128)(2,1)S(1)} copy(bf16[16,1,81920]{2,1,0:T(2,128)(2,1)} %all-gather.10.cloned.1.call-done) | data formatting | bytes 5242880
  75.0 1.2 slice.70
  76.2 2.8 reshape.223
  79.0 18.7 %all-gather.6.cloned.1.call-done = bf16[512,2048]{1,0:T(8,128)(2,1)} async-done(((bf16[512,256]{1,0:T(8,128)(2,1)}), bf16[512,2048]{1,0:T(8,128)(2,1)}) %all-gather.6.cloned.1.call-update) | async-done | bytes 2097168 | tf_op jit(solution)/shard_map/all_gather | solution.py:161
  97.7 3.1 fusion.11
  102.6 2.0 sort.17
  104.7 1.3 gather_fusion
  107.4 57.4 %all-gather.8.cloned.1.call-done = bf16[6144,512]{1,0:T(8,128)(2,1)} async-done(((bf16[384,512]{1,0:T(8,128)(2,1)}), bf16[6144,512]{1,0:T(8,128)(2,1)}) %all-gather.8.cloned.1.call-update) | async-done | bytes 6291472 | tf_op jit(solution)/shard_map/all_gather | solution.py:193
  164.8 3.1 slice.76
  167.9 4.4 %reshape_reshape.3 = bf16[64,128,128]{2,1,0:T(8,128)(2,1)} reshape(bf16[16,128,512]{2,1,0:T(8,128)(2,1)} %slice.76) | data formatting | bytes 4194304 | tf_op jit(solution)/shard_map/reshape;reshape | solution.py:58
  172.3 3.7 gather_fusion.2
  176.0 3.8 broadcast_select_fusion.page_ref
  179.8 78.0 %shard_map.77 = (bf16[16,256,512]{2,1,0:T(8,128)(2,1)}, f32[16,8,512]{2,1,0:T(8,128)}) custom-call(s32[64]{0:T(128)} %gather_fusion, s32[64]{0:T(128)} %copy-done.4, s32[64]{0:T(128)} %broadcast_multiply_fusion.1.kstart_ref, s32[16]{0:T(128)} %copy-done.1, bf16[16,384,512]{2,1,0:T(8,128)(2,1)} %bitcast.54, bf16[64,128,128]{2,1,0:T(8,128)(2,1)} %broadcast_select_fusion.page_ref), custom_call_target="tpu_custom_call" | custom-call | tf_op jit(solution)/shard_map/pallas_call | solution.py:149
  257.9 1.0 reduce-precision_convert_fusion.1
  258.9 3.9 pad_maximum_fusion
  262.7 5.0 %all-to-all-start = ((bf16[16,280,512]{2,1,0:T(8,128)(2,1)}), bf16[16,280,512]{2,1,0:T(8,128)(2,1)}, u32[]{:S(2)}, u32[]{:S(2)}) async-start(bf16[16,280,512]{2,1,0:T(8,128)(2,1)} %pad_maximum_fusion), calls=%async_computation | async-start | bytes 9175040 | tf_op jit(solution)/shard_map/all_to_all | solution.py:210
  269.6 68.9 %all-to-all-done = bf16[16,280,512]{2,1,0:T(8,128)(2,1)} async-done(((bf16[16,280,512]{2,1,0:T(8,128)(2,1)}), bf16[16,280,512]{2,1,0:T(8,128)(2,1)}, u32[]{:S(2)}, u32[]{:S(2)}) %all-to-all-start) | async-done | bytes 4587552 | tf_op jit(solution)/shard_map/all_to_all | solution.py:210
  338.5 1.1 fusion.2
  340.0 3.4 fusion
  343.5 2.1 convolution_convert_fusion
  345.6 37.2 %reduce-scatter.2.cloned.1.call-done = bf16[512,256]{1,0:T(8,128)(2,1)} async-done(((bf16[512,2048]{1,0:T(8,128)(2,1)}), bf16[512,256]{1,0:T(8,128)(2,1)}) %reduce-scatter.2.cloned.1.call-update) | async-done | bytes 262160 | tf_op jit(solution)/shard_map/reduce_scatter | solution.py:231
  (62 shorter events, 10.3 us)
Async XLA Ops:
  7.2 62.5 %all-gather.10.cloned.1.call-start = ((), (), s32[]{:S(2)}) async-start(), calls=%async_computation.5 | async-start | bytes 5570560 | tf_op jit(solution)/shard_map/all_gather | solution.py:166
  10.3 87.4 %all-gather.6.cloned.1.call-start = ((), (), s32[]{:S(2)}) async-start(), calls=%async_computation.2 | async-start | bytes 2359296 | tf_op jit(solution)/shard_map/all_gather | solution.py:161
  11.1 153.8 %all-gather.8.cloned.1.call-start = ((), (), s32[]{:S(2)}) async-start(), calls=%async_computation.4 | async-start | bytes 6684672 | tf_op jit(solution)/shard_map/all_gather | solution.py:193
  12.7 63.5 %copy-start.1 = (s32[16]{0:T(128)}, s32[16]{0:T(128)S(1)}, u32[]{:S(2)}) copy-start(s32[16]{0:T(128)S(1)} %get-tuple-element.21.qstart_ref) | copy-start | bytes 196
  79.0 21.9 %copy-start.3 = (f32[5]{0:T(128)S(1)}, f32[5]{0:T(128)}, u32[]{:S(2)}) copy-start(f32[5]{0:T(128)} %constant.14.clone.1) | copy-start | bytes 64
  79.0 23.3 %copy-start = (s32[1024]{0:T(1024)S(1)}, s32[1024]{0:T(1024)}, u32[]{:S(2)}) copy-start(s32[1024]{0:T(1024)} %param.11) | copy-start | bytes 12292
  100.8 5.2 %copy-start.2 = (s32[16]{0:T(128)S(1)}, s32[16]{0:T(128)}, u32[]{:S(2)}) copy-start(s32[16]{0:T(128)} %param.10) | copy-start | bytes 196
  104.7 67.6 %copy-start.4 = (s32[64]{0:T(128)}, s32[64]{0:T(128)S(1)}, u32[]{:S(2)}) copy-start(s32[64]{0:T(128)S(1)} %get-tuple-element.5.perm_ref) | copy-start | bytes 772
  262.7 75.8 %all-to-all-start = ((bf16[16,280,512]{2,1,0:T(8,128)(2,1)}), bf16[16,280,512]{2,1,0:T(8,128)(2,1)}, u32[]{:S(2)}, u32[]{:S(2)}) async-start(bf16[16,280,512]{2,1,0:T(8,128)(2,1)} %pad_maximum_fusion), calls=%async_computation | async-start | bytes 9175040 | tf_op jit(solution)/shard_map/all_to_all | solution.py:210
  267.8 115.0 %reduce-scatter.2.cloned.1.call-start = ((), (), s32[]{:S(2)}) async-start(), calls=%async_computation.3 | async-start | bytes 2359296 | tf_op jit(solution)/shard_map/reduce_scatter | solution.py:231
Sparse Core Ops, SparseCore 0:
  10.7 58.8 all-gather.9
  71.3 26.3 all-gather.5
  102.4 62.3 all-gather.7
  345.7 36.9 reduce-scatter.1

commit v4 on v3

--- a/solution.py
+++ b/solution.py
@@ -188,10 +188,17 @@
     rotated = (rotated * scale).astype(jnp.bfloat16)
     value_new = projected[:, GROUP + 1 :, :].astype(jnp.bfloat16)
     q_t = jnp.transpose(rotated[:, :GROUP, :], (1, 2, 0)).reshape(GROUP * HD, SPAN)
-    fresh = jnp.concatenate([rotated[:, GROUP:, :], value_new], axis=1).reshape(2 * HD, SPAN)
-    packed = jnp.concatenate([q_t, fresh], axis=0)[None]
-    packed_all = lax.all_gather(packed, "req", axis=0, tiled=True)
-    fresh_all = packed_all[:, GROUP * HD :, :].reshape(requests, SPAN, 2 * HD)
+    fresh = jnp.concatenate([rotated[:, GROUP:, :], value_new], axis=1)
+    halves = 2
+    sub = SPAN // halves
+    qw = GROUP * HD
+    gathered = []
+    for h in range(halves):
+        piece = q_t[:, h * sub:(h + 1) * sub]
+        if h == 0:
+            piece = jnp.concatenate([piece, fresh.reshape(-1, sub)], axis=0)
+        gathered.append(lax.all_gather(piece[None], "req", axis=0, tiled=True))
+    fresh_all = gathered[0][:, qw:, :].reshape(requests, SPAN, 2 * HD)
 
     my_slots = my_index * local_slots + jnp.arange(local_slots, dtype=jnp.int32)
     slot_req, page_index, cached = locate(my_slots, cache_pages, slot_order, new_pages)
@@ -200,37 +207,41 @@
     perm = jnp.argsort(slot_req, stable=True).astype(jnp.int32)
     sreq = slot_req[perm].astype(jnp.int32)
     kstart = (page_index[perm] * page_rows).astype(jnp.int32)
-    part_o, part_st = slot_attention(sreq, perm, kstart, query_start.astype(jnp.int32), packed_all, pages_out)
-
-    hi = lax.reduce_precision(part_st, exponent_bits=8, mantissa_bits=7)
-    rest = part_st - hi
-    mid = lax.reduce_precision(rest, exponent_bits=8, mantissa_bits=7)
-    lo = rest - mid
-    sent = jnp.concatenate([part_o] + [t.astype(jnp.bfloat16) for t in (hi, mid, lo)], axis=1)
-    got = lax.all_to_all(sent, "req", 0, 0, tiled=True)
-    qw = GROUP * HD
-    got_o = got[:, :qw].reshape(requests, GROUP, HD, SPAN)
-    got_bits = got[:, qw:].reshape(requests, 3, 2 * GROUP, SPAN).astype(jnp.float32)
-    got_st = (got_bits[:, 0] + got_bits[:, 1]) + got_bits[:, 2]
 
     all_slots = jnp.arange(slot_order.shape[0], dtype=jnp.int32)
     all_req, unused_index, unused_cached = locate(all_slots, cache_pages, slot_order, new_pages)
     holds = (all_req.reshape(-1, local_slots) == my_index).any(axis=1)
     valid = holds[:, None, None]
-    m_parts = jnp.where(valid, got_st[:, :GROUP], NEG_BIG)
-    l_parts = jnp.where(valid, got_st[:, GROUP:], 0.0)
-    top = jnp.max(m_parts, axis=0)
-    w = l_parts * jnp.exp(m_parts - top[None])
-    den = jnp.sum(w, axis=0)
-    o_parts = jnp.where(valid[..., None], got_o.astype(jnp.float32), 0.0)
-    num = jnp.sum(o_parts * w[:, :, None, :], axis=0)
-    attention_t = (num / den[:, None, :]).astype(jnp.bfloat16)
-    attention_flat = jnp.transpose(attention_t, (2, 0, 1)).reshape(SPAN, GROUP * HD)
-
-    head_terms = jnp.dot(attention_flat, out_full, preferred_element_type=jnp.float32)
-    attention_out = lax.psum_scatter(
-        head_terms.astype(jnp.bfloat16), "tp", scatter_dimension=1, tiled=True
-    )
+
+    outs = []
+    for h in range(halves):
+        q_start = (query_start + h * sub).astype(jnp.int32)
+        part_o, part_st = slot_attention(sreq, perm, kstart, q_start, gathered[h], pages_out)
+        hi = lax.reduce_precision(part_st, exponent_bits=8, mantissa_bits=7)
+        rest = part_st - hi
+        mid = lax.reduce_precision(rest, exponent_bits=8, mantissa_bits=7)
+        lo = rest - mid
+        sent = jnp.concatenate([part_o] + [t.astype(jnp.bfloat16) for t in (hi, mid, lo)], axis=1)
+        got = lax.all_to_all(sent, "req", 0, 0, tiled=True)
+        got_o = got[:, :qw].reshape(requests, GROUP, HD, sub)
+        got_bits = got[:, qw:].reshape(requests, 3, 2 * GROUP, sub).astype(jnp.float32)
+        got_st = (got_bits[:, 0] + got_bits[:, 1]) + got_bits[:, 2]
+
+        m_parts = jnp.where(valid, got_st[:, :GROUP], NEG_BIG)
+        l_parts = jnp.where(valid, got_st[:, GROUP:], 0.0)
+        top = jnp.max(m_parts, axis=0)
+        w = l_parts * jnp.exp(m_parts - top[None])
+        den = jnp.sum(w, axis=0)
+        o_parts = jnp.where(valid[..., None], got_o.astype(jnp.float32), 0.0)
+        num = jnp.sum(o_parts * w[:, :, None, :], axis=0)
+        attention_t = (num / den[:, None, :]).astype(jnp.bfloat16)
+        attention_flat = jnp.transpose(attention_t, (2, 0, 1)).reshape(sub, qw)
+
+        head_terms = jnp.dot(attention_flat, out_full, preferred_element_type=jnp.float32)
+        outs.append(
+            lax.psum_scatter(head_terms.astype(jnp.bfloat16), "tp", scatter_dimension=1, tiled=True)
+        )
+    attention_out = jnp.concatenate(outs, axis=0)
     return (attention_out, pages_out)
 
 

time: 390 us -> 442 us (1.13)
  Pallas kernels: 78 us -> 140 us
  waiting for transfers between devices: 238 us -> 213 us
  starting transfers between devices: 5.38 us -> 12.7 us
  other arithmetic: 21.8 us -> 28.3 us
    pallas_call x1 -> x2, Pallas kernels: 78 us -> 140 us  [slot_attention(): pl.pallas_call(kernel, grid_spec=grid_spec, out_shape=[jax.ShapeDtypeStru...]
    all_to_all x1 -> x2, waiting for transfers between devices: 68.9 us -> 28.7 us  [body(): got = lax.all_to_all(sent, 'req', 0, 0, tiled=True)]
    reduce_scatter x1 -> x2, waiting for transfers between devices: 37.2 us -> 62.3 us  [body(): lax.psum_scatter(head_terms.astype(jnp.bfloat16), 'tp', scatter_dimension...]
    all_gather x1 -> x2, waiting for transfers between devices: 57.4 us -> 47.3 us  [body(): gathered.append(lax.all_gather(piece[None], 'req', axis=0, tiled=True))]
    all_to_all x1 -> x2, starting transfers between devices: 5.04 us -> 12.3 us  [body(): got = lax.all_to_all(sent, 'req', 0, 0, tiled=True)]
  transfers between devices with their start and end apart: 5 -> 8, of which waited for: 5 -> 6; matrix products, arithmetic and copies ran while one was open for 5% -> 10% of each run, Pallas kernels for 0% -> 32%
where the time goes in v4:
time: 442 us
  waiting for transfers between devices  213 us (48%)
  Pallas kernels  140 us (32%)
  other arithmetic  28.3 us (6%)
  local copies, waits for them, and re-layouts  27 us (6%)
  between operations  14.4 us (3%)
  starting transfers between devices  12.7 us (3%)
  matrix products  6.05 us (1%)
    pallas_call x2, Pallas kernels, slot_attention(): pl.pallas_call(kernel, grid_spec=grid_spec, out_shape=[jax.ShapeDtypeStru...  140 us
    reduce_scatter x2, waiting for transfers between devices, body(): lax.psum_scatter(head_terms.astype(jnp.bfloat16), 'tp', scatter_dimension...  62.3 us
    all_gather x1, waiting for transfers between devices, body(): both = lax.all_gather(both, 'req', axis=0, tiled=True)  54.8 us
    all_gather x2, waiting for transfers between devices, body(): gathered.append(lax.all_gather(piece[None], 'req', axis=0, tiled=True))  47.3 us
    all_to_all x2, waiting for transfers between devices, body(): got = lax.all_to_all(sent, 'req', 0, 0, tiled=True)  28.7 us
    all_gather x1, waiting for transfers between devices, body(): whole = lax.all_gather(hidden, 'tp', axis=1, tiled=True)  18.7 us
    all_to_all x2, starting transfers between devices, body(): got = lax.all_to_all(sent, 'req', 0, 0, tiled=True)  12.3 us
  transfers between devices with their start and end apart: 8, of which 6 were waited for; matrix products, arithmetic and copies ran while one was open for 10% of the time, Pallas kernels for 32%

profile of v4, /device:TPU:0, one launch (start us, length us, event | category | flops | bytes accessed | tf_op | source)
XLA Modules:
  0.0 441.6 jit_solution(7332028918193817632)
XLA Ops:
  14.8 54.8 %all-gather.14.cloned.1.call-done = bf16[16,1,81920]{2,1,0:T(2,128)(2,1)} async-done(((bf16[1,1,81920]{2,1,0:T(2,128)(2,1)}), bf16[16,1,81920]{2,1,0:T(2,128)(2,1)}) %all-gather.14.cloned.1.call-update) | async-done | bytes 2621456 | tf_op jit(solution)/shard_map/all_gather | solution.py:166
  69.6 5.4 %copy.43 = bf16[16,1,81920]{2,0,1:T(8,128)(2,1)S(1)} copy(bf16[16,1,81920]{2,1,0:T(2,128)(2,1)} %all-gather.14.cloned.1.call-done) | data formatting | bytes 5242880
  76.2 2.8 reshape.237
  79.0 18.7 %all-gather.8.cloned.1.call-done = bf16[512,2048]{1,0:T(8,128)(2,1)} async-done(((bf16[512,256]{1,0:T(8,128)(2,1)}), bf16[512,2048]{1,0:T(8,128)(2,1)}) %all-gather.8.cloned.1.call-update) | async-done | bytes 2097168 | tf_op jit(solution)/shard_map/all_gather | solution.py:161
  97.7 3.1 fusion.22
  103.5 2.0 sort.17
  108.3 47.2 %all-gather.10.cloned.1.call-done = bf16[8192,256]{1,0:T(8,128)(2,1)} async-done(((bf16[512,256]{1,0:T(8,128)(2,1)}), bf16[8192,256]{1,0:T(8,128)(2,1)}) %all-gather.10.cloned.1.call-update) | async-done | bytes 4194320 | tf_op jit(solution)/shard_map/all_gather | solution.py:200
  155.5 3.1 slice.113
  158.6 4.1 reshape_reshape.3
  162.7 3.7 gather_fusion.2
  166.5 3.9 broadcast_select_fusion.page_ref
  170.4 70.2 %shard_map.77 = (bf16[16,256,256]{2,1,0:T(8,128)(2,1)}, f32[16,8,256]{2,1,0:T(8,128)}) custom-call(s32[64]{0:T(128)} %gather_fusion, s32[64]{0:T(128)} %copy-done.3, s32[64]{0:T(128)} %broadcast_multiply_fusion.1.kstart_ref, s32[16]{0:T(128)} %copy-done.1, bf16[16,512,256]{2,1,0:T(8,128)(2,1)} %bitcast.91, bf16[64,128,128]{2,1,0:T(8,128)(2,1)} %broadcast_select_fusion.page_ref), custom_call_target="tpu_custom_call" | custom-call | tf_op jit(solution)/shard_map/pallas_call | solution.py:149
  241.5 3.2 pad_maximum_fusion
  244.7 5.1 %all-to-all-start = ((bf16[16,280,256]{2,1,0:T(8,128)(2,1)}), bf16[16,280,256]{2,1,0:T(8,128)(2,1)}, u32[]{:S(2)}, u32[]{:S(2)}) async-start(bf16[16,280,256]{2,1,0:T(8,128)(2,1)} %pad_maximum_fusion), calls=%async_computation | async-start | bytes 4587520 | tf_op jit(solution)/shard_map/all_to_all | solution.py:225
  249.9 70.2 %shard_map.78 = (bf16[16,256,256]{2,1,0:T(8,128)(2,1)}, f32[16,8,256]{2,1,0:T(8,128)}) custom-call(s32[64]{0:T(128)} %gather_fusion, s32[64]{0:T(128)} %copy-done.3, s32[64]{0:T(128)} %broadcast_multiply_fusion.1.kstart_ref, s32[16]{0:T(128)} %get-tuple-element.38.qstart_ref, bf16[16,256,256]{2,1,0:T(8,128)(2,1)} %bitcast.95, ...), custom_call_target="tpu_custom_call" | custom-call | tf_op jit(solution)/shard_map/pallas_call | solution.py:149
  321.0 3.1 pad_maximum_fusion.1
  324.2 7.1 %all-to-all-start.1 = ((bf16[16,280,256]{2,1,0:T(8,128)(2,1)}), bf16[16,280,256]{2,1,0:T(8,128)(2,1)}, u32[]{:S(2)}, u32[]{:S(2)}) async-start(bf16[16,280,256]{2,1,0:T(8,128)(2,1)} %pad_maximum_fusion.1), calls=%async_computation.2 | async-start | bytes 4587520 | tf_op jit(solution)/shard_map/all_to_all | solution.py:225
  334.1 28.7 %all-to-all-done.1 = bf16[16,280,256]{2,1,0:T(8,128)(2,1)} async-done(((bf16[16,280,256]{2,1,0:T(8,128)(2,1)}), bf16[16,280,256]{2,1,0:T(8,128)(2,1)}, u32[]{:S(2)}, u32[]{:S(2)}) %all-to-all-start.1) | async-done | bytes 2293792 | tf_op jit(solution)/shard_map/all_to_all | solution.py:225
  364.1 3.5 fusion.1
  367.6 1.5 convolution_convert_fusion.1
  369.2 1.5 convolution_convert_fusion
  370.7 29.1 %reduce-scatter.3.cloned.1.call-done = bf16[256,256]{1,0:T(8,128)(2,1)} async-done(((bf16[256,2048]{1,0:T(8,128)(2,1)}), bf16[256,256]{1,0:T(8,128)(2,1)}) %reduce-scatter.3.cloned.1.call-update) | async-done | bytes 131088 | tf_op jit(solution)/shard_map/reduce_scatter | solution.py:242
  399.8 33.3 %reduce-scatter.5.cloned.1.call-done = bf16[256,256]{1,0:T(8,128)(2,1)} async-done(((bf16[256,2048]{1,0:T(8,128)(2,1)}), bf16[256,256]{1,0:T(8,128)(2,1)}) %reduce-scatter.5.cloned.1.call-update) | async-done | bytes 131088 | tf_op jit(solution)/shard_map/reduce_scatter | solution.py:242
  433.1 1.7 pad_maximum_fusion.3
  (79 shorter events, 20.2 us)
Async XLA Ops:
  7.2 62.5 %all-gather.14.cloned.1.call-start = ((), (), s32[]{:S(2)}) async-start(), calls=%async_computation.9 | async-start | bytes 5570560 | tf_op jit(solution)/shard_map/all_gather | solution.py:166
  10.3 87.4 %all-gather.8.cloned.1.call-start = ((), (), s32[]{:S(2)}) async-start(), calls=%async_computation.4 | async-start | bytes 2359296 | tf_op jit(solution)/shard_map/all_gather | solution.py:161
  11.1 144.5 %all-gather.10.cloned.1.call-start = ((), (), s32[]{:S(2)}) async-start(), calls=%async_computation.7 | async-start | bytes 4456448 | tf_op jit(solution)/shard_map/all_gather | solution.py:200
  13.3 61.7 %copy-start.1 = (s32[16]{0:T(128)}, s32[16]{0:T(128)S(1)}, u32[]{:S(2)}) copy-start(s32[16]{0:T(128)S(1)} %get-tuple-element.40.qstart_ref) | copy-start | bytes 196
  79.0 21.9 %copy-start.4 = (f32[5]{0:T(128)S(1)}, f32[5]{0:T(128)}, u32[]{:S(2)}) copy-start(f32[5]{0:T(128)} %constant.14.clone.1) | copy-start | bytes 64
  100.9 2.1 copy-start
  100.9 6.0 %copy-start.2 = (s32[16]{0:T(128)S(1)}, s32[16]{0:T(128)}, u32[]{:S(2)}) copy-start(s32[16]{0:T(128)} %param.10) | copy-start | bytes 196
  102.9 146.9 %all-gather.12.cloned.1.call-start = ((), (), s32[]{:S(2)}) async-start(), calls=%async_computation.8 | async-start | bytes 2228224 | tf_op jit(solution)/shard_map/all_gather | solution.py:200
  105.6 53.1 %copy-start.3 = (s32[64]{0:T(128)}, s32[64]{0:T(128)S(1)}, u32[]{:S(2)}) copy-start(s32[64]{0:T(128)S(1)} %get-tuple-element.7.perm_ref) | copy-start | bytes 772
  244.7 79.5 %all-to-all-start = ((bf16[16,280,256]{2,1,0:T(8,128)(2,1)}), bf16[16,280,256]{2,1,0:T(8,128)(2,1)}, u32[]{:S(2)}, u32[]{:S(2)}) async-start(bf16[16,280,256]{2,1,0:T(8,128)(2,1)} %pad_maximum_fusion), calls=%async_computation | async-start | bytes 4587520 | tf_op jit(solution)/shard_map/all_to_all | solution.py:225
  324.2 38.6 %all-to-all-start.1 = ((bf16[16,280,256]{2,1,0:T(8,128)(2,1)}), bf16[16,280,256]{2,1,0:T(8,128)(2,1)}, u32[]{:S(2)}, u32[]{:S(2)}) async-start(bf16[16,280,256]{2,1,0:T(8,128)(2,1)} %pad_maximum_fusion.1), calls=%async_computation.2 | async-start | bytes 4587520 | tf_op jit(solution)/shard_map/all_to_all | solution.py:225
  331.3 68.5 %reduce-scatter.3.cloned.1.call-start = ((), (), s32[]{:S(2)}) async-start(), calls=%async_computation.5 | async-start | bytes 1179648 | tf_op jit(solution)/shard_map/reduce_scatter | solution.py:242
  369.1 64.0 %reduce-scatter.5.cloned.1.call-start = ((), (), s32[]{:S(2)}) async-start(), calls=%async_computation.6 | async-start | bytes 1179648 | tf_op jit(solution)/shard_map/reduce_scatter | solution.py:242
Sparse Core Ops, SparseCore 0:
  10.7 58.8 all-gather.13
  71.3 26.3 all-gather.7
  103.1 52.4 all-gather.9
  157.5 44.8 all-gather.11
  369.2 30.5 reduce-scatter.2
  402.0 30.9 reduce-scatter.4

commit v5 on v4

--- a/solution.py
+++ b/solution.py
@@ -82,7 +82,7 @@
 
         kst = kstart_ref[i]
         qst = qstart_ref[req]
-        page = page_ref[0]
+        page = page_ref[perm_ref[i]]
         keys = page[:, :HD]
         vals = page[:, HD:]
 
@@ -92,7 +92,7 @@
                 query_pos = lax.broadcasted_iota(jnp.int32, (page_rows, span_rows), 1) + qst
                 vis = key_pos <= query_pos
             for g in range(GROUP):
-                q_g = q_ref[0, g * HD:(g + 1) * HD, :]
+                q_g = q_ref[req, g * HD:(g + 1) * HD, :]
                 s = jnp.dot(keys, q_g, preferred_element_type=jnp.float32)
                 if masked:
                     s = jnp.where(vis, s, NEG_BIG)
@@ -125,20 +125,20 @@
             for g in range(GROUP):
                 l_g = l_sc[g]
                 safe = jnp.where(l_g > 0.0, l_g, 1.0)
-                o_ref[0, g * HD:(g + 1) * HD, :] = (acc_sc[g] / safe).astype(o_ref.dtype)
-                st_ref[0, g:g + 1, :] = m_sc[g]
-                st_ref[0, GROUP + g:GROUP + g + 1, :] = l_g
+                o_ref[req, g * HD:(g + 1) * HD, :] = (acc_sc[g] / safe).astype(o_ref.dtype)
+                st_ref[req, g:g + 1, :] = m_sc[g]
+                st_ref[req, GROUP + g:GROUP + g + 1, :] = l_g
 
     grid_spec = pltpu.PrefetchScalarGridSpec(
         num_scalar_prefetch=4,
         grid=(slots,),
         in_specs=[
-            pl.BlockSpec((1, qw, span_rows), lambda i, sr, pm, ks, qs: (sr[i], 0, 0)),
-            pl.BlockSpec((1, page_rows, 2 * HD), lambda i, sr, pm, ks, qs: (pm[i], 0, 0)),
+            pl.BlockSpec((reqs, qw, span_rows), lambda i, sr, pm, ks, qs: (0, 0, 0)),
+            pl.BlockSpec((slots, page_rows, 2 * HD), lambda i, sr, pm, ks, qs: (0, 0, 0)),
         ],
         out_specs=[
-            pl.BlockSpec((1, qw, span_rows), lambda i, sr, pm, ks, qs: (sr[i], 0, 0)),
-            pl.BlockSpec((1, 2 * GROUP, span_rows), lambda i, sr, pm, ks, qs: (sr[i], 0, 0)),
+            pl.BlockSpec((reqs, qw, span_rows), lambda i, sr, pm, ks, qs: (0, 0, 0)),
+            pl.BlockSpec((reqs, 2 * GROUP, span_rows), lambda i, sr, pm, ks, qs: (0, 0, 0)),
         ],
         scratch_shapes=[
             pltpu.VMEM((GROUP, 1, span_rows), jnp.float32),
@@ -153,7 +153,9 @@
             jax.ShapeDtypeStruct((reqs, qw, span_rows), jnp.bfloat16),
             jax.ShapeDtypeStruct((reqs, 2 * GROUP, span_rows), jnp.float32),
         ],
-        compiler_params=pltpu.CompilerParams(dimension_semantics=("arbitrary",)),
+        compiler_params=pltpu.CompilerParams(
+            dimension_semantics=("arbitrary",), vmem_limit_bytes=48 * 1024 * 1024
+        ),
     )(sreq, perm, kstart, qstart, packed, pages)
 
 
@@ -238,10 +240,10 @@
         attention_flat = jnp.transpose(attention_t, (2, 0, 1)).reshape(sub, qw)
 
         head_terms = jnp.dot(attention_flat, out_full, preferred_element_type=jnp.float32)
-        outs.append(
-            lax.psum_scatter(head_terms.astype(jnp.bfloat16), "tp", scatter_dimension=1, tiled=True)
-        )
-    attention_out = jnp.concatenate(outs, axis=0)
+        outs.append(head_terms.astype(jnp.bfloat16))
+    attention_out = lax.psum_scatter(
+        jnp.concatenate(outs, axis=0), "tp", scatter_dimension=1, tiled=True
+    )
     return (attention_out, pages_out)
 
 

time: 442 us -> 394 us (0.89)
  waiting for transfers between devices: 213 us -> 184 us
  other arithmetic: 28.3 us -> 18.6 us
  Pallas kernels: 140 us -> 135 us
    reduce_scatter x2 -> x1, waiting for transfers between devices: 62.3 us -> 32.3 us  [body(): lax.psum_scatter(jnp.concatenate(outs, axis=0), 'tp', scatter_dimension=1...]
    unnamed x15 -> x17, local copies, waits for them, and re-layouts: 7.62 us -> 12.9 us
    pallas_call x2, Pallas kernels: 140 us -> 135 us  [slot_attention(): pl.pallas_call(kernel, grid_spec=grid_spec, out_shape=[jax.ShapeDtypeStru...]
  transfers between devices with their start and end apart: 8 -> 7, of which waited for: 6 -> 5; matrix products, arithmetic and copies ran while one was open for 10% -> 8% of each run, Pallas kernels for 32% -> 34%
where the time goes in v5:
time: 394 us; the launch traced here: 393 us
  waiting for transfers between devices  184 us (47%)
  Pallas kernels  135 us (34%)
  local copies, waits for them, and re-layouts  25.1 us (6%)
  other arithmetic  18.6 us (5%)
  between operations  14.1 us (4%)
  starting transfers between devices  13 us (3%)
    pallas_call x2, Pallas kernels, slot_attention(): pl.pallas_call(kernel, grid_spec=grid_spec, out_shape=[jax.ShapeDtypeStru...  135 us
    all_gather x1, waiting for transfers between devices, body(): both = lax.all_gather(both, 'req', axis=0, tiled=True)  55.4 us
    all_gather x2, waiting for transfers between devices, body(): gathered.append(lax.all_gather(piece[None], 'req', axis=0, tiled=True))  48.3 us
    reduce_scatter x1, waiting for transfers between devices, body(): lax.psum_scatter(jnp.concatenate(outs, axis=0), 'tp', scatter_dimension=1...  32.3 us
    all_to_all x2, waiting for transfers between devices, body(): got = lax.all_to_all(sent, 'req', 0, 0, tiled=True)  26.5 us
    all_gather x1, waiting for transfers between devices, body(): whole = lax.all_gather(hidden, 'tp', axis=1, tiled=True)  20.3 us
    unnamed x17, local copies, waits for them, and re-layouts  12.9 us
    all_to_all x2, starting transfers between devices, body(): got = lax.all_to_all(sent, 'req', 0, 0, tiled=True)  12.6 us
  transfers between devices with their start and end apart: 7, of which 5 were waited for; matrix products, arithmetic and copies ran while one was open for 8% of the time, Pallas kernels for 34%

profile of v5, /device:TPU:0, one launch (start us, length us, event | category | flops | bytes accessed | tf_op | source)
XLA Modules:
  0.0 393.3 jit_solution(15733600186650435567)
XLA Ops:
  14.2 55.4 %all-gather.14.cloned.1.call-done = bf16[16,1,81920]{2,1,0:T(2,128)(2,1)} async-done(((bf16[1,1,81920]{2,1,0:T(2,128)(2,1)}), bf16[16,1,81920]{2,1,0:T(2,128)(2,1)}) %all-gather.14.cloned.1.call-update) | async-done | bytes 2621456 | tf_op jit(solution)/shard_map/all_gather | solution.py:168
  69.6 5.4 %copy.43 = bf16[16,1,81920]{2,0,1:T(8,128)(2,1)S(1)} copy(bf16[16,1,81920]{2,1,0:T(2,128)(2,1)} %all-gather.14.cloned.1.call-done) | data formatting | bytes 5242880
  75.0 1.5 copy-done.2
  77.4 20.3 %all-gather.8.cloned.1.call-done = bf16[512,2048]{1,0:T(8,128)(2,1)} async-done(((bf16[512,256]{1,0:T(8,128)(2,1)}), bf16[512,2048]{1,0:T(8,128)(2,1)}) %all-gather.8.cloned.1.call-update) | async-done | bytes 2097168 | tf_op jit(solution)/shard_map/all_gather | solution.py:163
  97.7 2.6 fusion.22
  103.1 2.0 sort.17
  106.8 48.2 %all-gather.10.cloned.1.call-done = bf16[8192,256]{1,0:T(8,128)(2,1)} async-done(((bf16[512,256]{1,0:T(8,128)(2,1)}), bf16[8192,256]{1,0:T(8,128)(2,1)}) %all-gather.10.cloned.1.call-update) | async-done | bytes 4194320 | tf_op jit(solution)/shard_map/all_gather | solution.py:202
  155.1 1.7 slice.113
  156.8 2.1 reshape_reshape.3
  158.9 2.5 gather_fusion.2
  161.5 1.9 broadcast_select_fusion.page_ref
  163.4 67.9 %shard_map.77 = (bf16[16,256,256]{2,1,0:T(8,128)(2,1)S(1)}, f32[16,8,256]{2,1,0:T(8,128)S(1)}) custom-call(s32[64]{0:T(128)S(1)} %gather_fusion, s32[64]{0:T(128)S(1)} %get-tuple-element.7.perm_ref, s32[64]{0:T(128)S(1)} %broadcast_multiply_fusion.1.kstart_ref, s32[16]{0:T(128)S(1)} %get-tuple-element.40.qstart_ref, bf16[16,512,256]{2,1,0:T(8,128)(2,1)} %bitcast.92, ...), custom_call_target="tpu_custom_call" | custom-call | tf_op jit(solution)/shard_map/pallas_call | solution.py:149
  231.4 1.6 pad_maximum_fusion
  232.9 5.3 %all-to-all-start = ((bf16[16,280,256]{2,1,0:T(8,128)(2,1)}), bf16[16,280,256]{2,1,0:T(8,128)(2,1)S(1)}, u32[]{:S(2)}, u32[]{:S(2)}) async-start(bf16[16,280,256]{2,1,0:T(8,128)(2,1)} %pad_maximum_fusion), calls=%async_computation | async-start | bytes 4587520 | tf_op jit(solution)/shard_map/all_to_all | solution.py:227
  238.3 1.6 copy-done.1
  239.9 67.3 %shard_map.78 = (bf16[16,256,256]{2,1,0:T(8,128)(2,1)S(1)}, f32[16,8,256]{2,1,0:T(8,128)S(1)}) custom-call(s32[64]{0:T(128)S(1)} %gather_fusion, s32[64]{0:T(128)S(1)} %get-tuple-element.7.perm_ref, s32[64]{0:T(128)S(1)} %broadcast_multiply_fusion.1.kstart_ref, s32[16]{0:T(128)S(1)} %get-tuple-element.38.qstart_ref, bf16[16,256,256]{2,1,0:T(8,128)(2,1)S(1)} %bitcast.88, ...), custom_call_target="tpu_custom_call" | custom-call | tf_op jit(solution)/shard_map/pallas_call | solution.py:149
  307.2 1.5 pad_maximum_fusion.1
  308.7 7.3 %all-to-all-start.1 = ((bf16[16,280,256]{2,1,0:T(8,128)(2,1)}), bf16[16,280,256]{2,1,0:T(8,128)(2,1)}, u32[]{:S(2)}, u32[]{:S(2)}) async-start(bf16[16,280,256]{2,1,0:T(8,128)(2,1)} %pad_maximum_fusion.1), calls=%async_computation.1 | async-start | bytes 4587520 | tf_op jit(solution)/shard_map/all_to_all | solution.py:227
  317.1 1.3 slice_bitcast_fusion
  319.6 1.5 copy.33
  321.1 26.5 %all-to-all-done.1 = bf16[16,280,256]{2,1,0:T(8,128)(2,1)} async-done(((bf16[16,280,256]{2,1,0:T(8,128)(2,1)}), bf16[16,280,256]{2,1,0:T(8,128)(2,1)}, u32[]{:S(2)}, u32[]{:S(2)}) %all-to-all-start.1) | async-done | bytes 2293792 | tf_op jit(solution)/shard_map/all_to_all | solution.py:227
  348.8 2.9 fusion.1
  352.8 1.6 pad_maximum_fusion.2
  354.4 32.3 %reduce-scatter.2.cloned.1.call-done = bf16[512,256]{1,0:T(8,128)(2,1)} async-done(((bf16[512,2048]{1,0:T(8,128)(2,1)}), bf16[512,256]{1,0:T(8,128)(2,1)}) %reduce-scatter.2.cloned.1.call-update) | async-done | bytes 262160 | tf_op jit(solution)/shard_map/reduce_scatter | solution.py:244
  (78 shorter events, 16.8 us)
Async XLA Ops:
  7.2 62.5 %all-gather.14.cloned.1.call-start = ((), (), s32[]{:S(2)}) async-start(), calls=%async_computation.7 | async-start | bytes 5570560 | tf_op jit(solution)/shard_map/all_gather | solution.py:168
  10.3 87.4 %all-gather.8.cloned.1.call-start = ((), (), s32[]{:S(2)}) async-start(), calls=%async_computation.3 | async-start | bytes 2359296 | tf_op jit(solution)/shard_map/all_gather | solution.py:163
  11.1 144.0 %all-gather.10.cloned.1.call-start = ((), (), s32[]{:S(2)}) async-start(), calls=%async_computation.5 | async-start | bytes 4456448 | tf_op jit(solution)/shard_map/all_gather | solution.py:202
  75.0 1.5 copy-start.2
  77.4 23.1 %copy-start.5 = (f32[5]{0:T(128)S(1)}, f32[5]{0:T(128)}, u32[]{:S(2)}) copy-start(f32[5]{0:T(128)} %constant.14.clone.1) | copy-start | bytes 64
  100.5 2.1 copy-start.3
  100.5 5.4 %copy-start.4 = (s32[16]{0:T(128)S(1)}, s32[16]{0:T(128)}, u32[]{:S(2)}) copy-start(s32[16]{0:T(128)} %param.10) | copy-start | bytes 196
  102.5 135.8 %all-gather.12.cloned.1.call-start = ((), (), s32[]{:S(2)}) async-start(), calls=%async_computation.6 | async-start | bytes 2228224 | tf_op jit(solution)/shard_map/all_gather | solution.py:202
  163.4 67.9 %copy-start = (bf16[64,128,128]{2,1,0:T(8,128)(2,1)}, bf16[64,128,128]{2,1,0:T(8,128)(2,1)S(1)}, u32[]{:S(2)}) copy-start(bf16[64,128,128]{2,1,0:T(8,128)(2,1)S(1)} %broadcast_select_fusion.page_ref) | copy-start | bytes 6291460
  232.9 75.8 %all-to-all-start = ((bf16[16,280,256]{2,1,0:T(8,128)(2,1)}), bf16[16,280,256]{2,1,0:T(8,128)(2,1)S(1)}, u32[]{:S(2)}, u32[]{:S(2)}) async-start(bf16[16,280,256]{2,1,0:T(8,128)(2,1)} %pad_maximum_fusion), calls=%async_computation | async-start | bytes 4587520 | tf_op jit(solution)/shard_map/all_to_all | solution.py:227
  238.3 1.6 copy-start.1
  308.7 38.8 %all-to-all-start.1 = ((bf16[16,280,256]{2,1,0:T(8,128)(2,1)}), bf16[16,280,256]{2,1,0:T(8,128)(2,1)}, u32[]{:S(2)}, u32[]{:S(2)}) async-start(bf16[16,280,256]{2,1,0:T(8,128)(2,1)} %pad_maximum_fusion.1), calls=%async_computation.1 | async-start | bytes 4587520 | tf_op jit(solution)/shard_map/all_to_all | solution.py:227
  316.1 70.7 %reduce-scatter.2.cloned.1.call-start = ((), (), s32[]{:S(2)}) async-start(), calls=%async_computation.4 | async-start | bytes 2359296 | tf_op jit(solution)/shard_map/reduce_scatter | solution.py:244
Sparse Core Ops, SparseCore 0:
  10.7 58.8 all-gather.13
  71.3 26.3 all-gather.7
  102.6 52.4 all-gather.9
  157.0 44.8 all-gather.11
  354.6 32.1 reduce-scatter.1

commit v6 on v5

--- a/solution.py
+++ b/solution.py
@@ -60,10 +60,10 @@
     return jnp.where((page_index >= cached)[:, None, None], fresh_pages[pick], kv_pages)
 
 
-def slot_attention(sreq, perm, kstart, qstart, packed, pages):
-    reqs, _, span_rows = packed.shape
+def slot_attention(sreq, perm, kstart, qstart, packed, pages, sub):
+    reqs, _, width = packed.shape
     slots, page_rows, _ = pages.shape
-    qw = GROUP * HD
+    assert width == GROUP * sub and sub & (sub - 1) == 0
 
     def kernel(sreq_ref, perm_ref, kstart_ref, qstart_ref, q_ref, page_ref, o_ref, st_ref, m_sc, l_sc, acc_sc):
         i = pl.program_id(0)
@@ -85,30 +85,28 @@
         page = page_ref[perm_ref[i]]
         keys = page[:, :HD]
         vals = page[:, HD:]
+        q = q_ref[req]
 
         def update(masked):
+            s = jnp.dot(keys, q, preferred_element_type=jnp.float32)
             if masked:
-                key_pos = lax.broadcasted_iota(jnp.int32, (page_rows, span_rows), 0) + kst
-                query_pos = lax.broadcasted_iota(jnp.int32, (page_rows, span_rows), 1) + qst
-                vis = key_pos <= query_pos
-            for g in range(GROUP):
-                q_g = q_ref[req, g * HD:(g + 1) * HD, :]
-                s = jnp.dot(keys, q_g, preferred_element_type=jnp.float32)
-                if masked:
-                    s = jnp.where(vis, s, NEG_BIG)
-                m_prev = m_sc[g]
-                m_next = jnp.maximum(m_prev, jnp.max(s, axis=0, keepdims=True))
-                alpha = jnp.exp(m_prev - m_next)
-                p = jnp.exp(s - m_next)
-                if masked:
-                    p = jnp.where(vis, p, 0.0)
-                l_sc[g] = alpha * l_sc[g] + jnp.sum(p, axis=0, keepdims=True)
-                m_sc[g] = m_next
-                pv = lax.dot_general(
-                    vals, p.astype(jnp.bfloat16), (((0,), (0,)), ((), ())),
-                    preferred_element_type=jnp.float32,
-                )
-                acc_sc[g] = acc_sc[g] * alpha + pv
+                key_pos = lax.broadcasted_iota(jnp.int32, (page_rows, width), 0) + kst
+                token = jnp.bitwise_and(lax.broadcasted_iota(jnp.int32, (page_rows, width), 1), sub - 1)
+                vis = key_pos <= token + qst
+                s = jnp.where(vis, s, NEG_BIG)
+            m_prev = m_sc[...]
+            m_next = jnp.maximum(m_prev, jnp.max(s, axis=0, keepdims=True))
+            alpha = jnp.exp(m_prev - m_next)
+            p = jnp.exp(s - m_next)
+            if masked:
+                p = jnp.where(vis, p, 0.0)
+            l_sc[...] = alpha * l_sc[...] + jnp.sum(p, axis=0, keepdims=True)
+            m_sc[...] = m_next
+            pv = lax.dot_general(
+                vals, p.astype(jnp.bfloat16), (((0,), (0,)), ((), ())),
+                preferred_element_type=jnp.float32,
+            )
+            acc_sc[...] = acc_sc[...] * alpha + pv
 
         partial = kst + (page_rows - 1) > qst
 
@@ -122,36 +120,35 @@
 
         @pl.when(last)
         def _():
-            for g in range(GROUP):
-                l_g = l_sc[g]
-                safe = jnp.where(l_g > 0.0, l_g, 1.0)
-                o_ref[req, g * HD:(g + 1) * HD, :] = (acc_sc[g] / safe).astype(o_ref.dtype)
-                st_ref[req, g:g + 1, :] = m_sc[g]
-                st_ref[req, GROUP + g:GROUP + g + 1, :] = l_g
+            l_all = l_sc[...]
+            safe = jnp.where(l_all > 0.0, l_all, 1.0)
+            o_ref[req] = (acc_sc[...] / safe).astype(o_ref.dtype)
+            st_ref[req, 0:1, :] = m_sc[...]
+            st_ref[req, 1:2, :] = l_all
 
     grid_spec = pltpu.PrefetchScalarGridSpec(
         num_scalar_prefetch=4,
         grid=(slots,),
         in_specs=[
-            pl.BlockSpec((reqs, qw, span_rows), lambda i, sr, pm, ks, qs: (0, 0, 0)),
+            pl.BlockSpec((reqs, HD, width), lambda i, sr, pm, ks, qs: (0, 0, 0)),
             pl.BlockSpec((slots, page_rows, 2 * HD), lambda i, sr, pm, ks, qs: (0, 0, 0)),
         ],
         out_specs=[
-            pl.BlockSpec((reqs, qw, span_rows), lambda i, sr, pm, ks, qs: (0, 0, 0)),
-            pl.BlockSpec((reqs, 2 * GROUP, span_rows), lambda i, sr, pm, ks, qs: (0, 0, 0)),
+            pl.BlockSpec((reqs, HD, width), lambda i, sr, pm, ks, qs: (0, 0, 0)),
+            pl.BlockSpec((reqs, 2, width), lambda i, sr, pm, ks, qs: (0, 0, 0)),
         ],
         scratch_shapes=[
-            pltpu.VMEM((GROUP, 1, span_rows), jnp.float32),
-            pltpu.VMEM((GROUP, 1, span_rows), jnp.float32),
-            pltpu.VMEM((GROUP, HD, span_rows), jnp.float32),
+            pltpu.VMEM((1, width), jnp.float32),
+            pltpu.VMEM((1, width), jnp.float32),
+            pltpu.VMEM((HD, width), jnp.float32),
         ],
     )
     return pl.pallas_call(
         kernel,
         grid_spec=grid_spec,
         out_shape=[
-            jax.ShapeDtypeStruct((reqs, qw, span_rows), jnp.bfloat16),
-            jax.ShapeDtypeStruct((reqs, 2 * GROUP, span_rows), jnp.float32),
+            jax.ShapeDtypeStruct((reqs, HD, width), jnp.bfloat16),
+            jax.ShapeDtypeStruct((reqs, 2, width), jnp.float32),
         ],
         compiler_params=pltpu.CompilerParams(
             dimension_semantics=("arbitrary",), vmem_limit_bytes=48 * 1024 * 1024
@@ -189,18 +186,17 @@
     )
     rotated = (rotated * scale).astype(jnp.bfloat16)
     value_new = projected[:, GROUP + 1 :, :].astype(jnp.bfloat16)
-    q_t = jnp.transpose(rotated[:, :GROUP, :], (1, 2, 0)).reshape(GROUP * HD, SPAN)
     fresh = jnp.concatenate([rotated[:, GROUP:, :], value_new], axis=1)
     halves = 2
     sub = SPAN // halves
-    qw = GROUP * HD
+    width = GROUP * sub
     gathered = []
     for h in range(halves):
-        piece = q_t[:, h * sub:(h + 1) * sub]
+        piece = jnp.transpose(rotated[h * sub:(h + 1) * sub, :GROUP, :], (2, 1, 0)).reshape(HD, width)
         if h == 0:
-            piece = jnp.concatenate([piece, fresh.reshape(-1, sub)], axis=0)
+            piece = jnp.concatenate([piece, fresh.reshape(-1, width)], axis=0)
         gathered.append(lax.all_gather(piece[None], "req", axis=0, tiled=True))
-    fresh_all = gathered[0][:, qw:, :].reshape(requests, SPAN, 2 * HD)
+    fresh_all = gathered[0][:, HD:, :].reshape(requests, SPAN, 2 * HD)
 
     my_slots = my_index * local_slots + jnp.arange(local_slots, dtype=jnp.int32)
     slot_req, page_index, cached = locate(my_slots, cache_pages, slot_order, new_pages)
@@ -218,26 +214,26 @@
     outs = []
     for h in range(halves):
         q_start = (query_start + h * sub).astype(jnp.int32)
-        part_o, part_st = slot_attention(sreq, perm, kstart, q_start, gathered[h], pages_out)
+        part_o, part_st = slot_attention(sreq, perm, kstart, q_start, gathered[h], pages_out, sub)
         hi = lax.reduce_precision(part_st, exponent_bits=8, mantissa_bits=7)
         rest = part_st - hi
         mid = lax.reduce_precision(rest, exponent_bits=8, mantissa_bits=7)
         lo = rest - mid
         sent = jnp.concatenate([part_o] + [t.astype(jnp.bfloat16) for t in (hi, mid, lo)], axis=1)
         got = lax.all_to_all(sent, "req", 0, 0, tiled=True)
-        got_o = got[:, :qw].reshape(requests, GROUP, HD, sub)
-        got_bits = got[:, qw:].reshape(requests, 3, 2 * GROUP, sub).astype(jnp.float32)
+        got_o = got[:, :HD].reshape(requests, HD, GROUP, sub)
+        got_bits = got[:, HD:].reshape(requests, 3, 2, GROUP, sub).astype(jnp.float32)
         got_st = (got_bits[:, 0] + got_bits[:, 1]) + got_bits[:, 2]
 
-        m_parts = jnp.where(valid, got_st[:, :GROUP], NEG_BIG)
-        l_parts = jnp.where(valid, got_st[:, GROUP:], 0.0)
+        m_parts = jnp.where(valid, got_st[:, 0], NEG_BIG)
+        l_parts = jnp.where(valid, got_st[:, 1], 0.0)
         top = jnp.max(m_parts, axis=0)
         w = l_parts * jnp.exp(m_parts - top[None])
         den = jnp.sum(w, axis=0)
         o_parts = jnp.where(valid[..., None], got_o.astype(jnp.float32), 0.0)
-        num = jnp.sum(o_parts * w[:, :, None, :], axis=0)
-        attention_t = (num / den[:, None, :]).astype(jnp.bfloat16)
-        attention_flat = jnp.transpose(attention_t, (2, 0, 1)).reshape(sub, qw)
+        num = jnp.sum(o_parts * w[:, None, :, :], axis=0)
+        attention_t = (num / den[None]).astype(jnp.bfloat16)
+        attention_flat = jnp.transpose(attention_t, (2, 1, 0)).reshape(sub, GROUP * HD)
 
         head_terms = jnp.dot(attention_flat, out_full, preferred_element_type=jnp.float32)
         outs.append(head_terms.astype(jnp.bfloat16))

time: 394 us -> 336 us (0.85)
  Pallas kernels: 135 us -> 68.7 us
  local copies, waits for them, and re-layouts: 25.1 us -> 34.4 us
  waiting for transfers between devices: 184 us -> 178 us
  other arithmetic: 18.6 us -> 23.7 us
    pallas_call x2, Pallas kernels: 135 us -> 68.7 us  [slot_attention(): pl.pallas_call(kernel, grid_spec=grid_spec, out_shape=[jax.ShapeDtypeStru...]
    all_to_all x2, waiting for transfers between devices: 26.5 us -> 21.8 us  [body(): got = lax.all_to_all(sent, 'req', 0, 0, tiled=True)]
    convert_element_type x0 -> x4, local copies, waits for them, and re-layouts: none -> 4.02 us  [the longest x2 3.99 us: body(): got[:, HD:].reshape(requests, 3, 2, GROUP, sub).astype(jnp.float32)]
    unnamed x17 -> x19, local copies, waits for them, and re-layouts: 12.9 us -> 12.9 us
  transfers between devices with their start and end apart: 7 -> 7, of which waited for: 5 -> 5; matrix products, arithmetic and copies ran while one was open for 8% -> 11% of each run, Pallas kernels for 34% -> 20%
where the time goes in v6:
time: 336 us; the launch traced here: 335 us
  waiting for transfers between devices  178 us (53%)
  Pallas kernels  68.7 us (20%)
  local copies, waits for them, and re-layouts  34.4 us (10%)
  other arithmetic  23.7 us (7%)
  between operations  14.2 us (4%)
  starting transfers between devices  12.6 us (4%)
  matrix products  3.62 us (1%)
    pallas_call x2, Pallas kernels, slot_attention(): pl.pallas_call(kernel, grid_spec=grid_spec, out_shape=[jax.ShapeDtypeStru...  68.7 us
    all_gather x1, waiting for transfers between devices, body(): both = lax.all_gather(both, 'req', axis=0, tiled=True)  55.4 us
    all_gather x2, waiting for transfers between devices, body(): gathered.append(lax.all_gather(piece[None], 'req', axis=0, tiled=True))  47.7 us
    reduce_scatter x1, waiting for transfers between devices, body(): lax.psum_scatter(jnp.concatenate(outs, axis=0), 'tp', scatter_dimension=1...  32.3 us
    all_to_all x2, waiting for transfers between devices, body(): got = lax.all_to_all(sent, 'req', 0, 0, tiled=True)  21.8 us
    all_gather x1, waiting for transfers between devices, body(): whole = lax.all_gather(hidden, 'tp', axis=1, tiled=True)  20.3 us
    unnamed x19, local copies, waits for them, and re-layouts  12.9 us
    all_to_all x2, starting transfers between devices, body(): got = lax.all_to_all(sent, 'req', 0, 0, tiled=True)  12.2 us
  transfers between devices with their start and end apart: 7, of which 5 were waited for; matrix products, arithmetic and copies ran while one was open for 11% of the time, Pallas kernels for 20%

profile of v6, /device:TPU:0, one launch (start us, length us, event | category | flops | bytes accessed | tf_op | source)
XLA Modules:
  0.0 335.4 jit_solution(6114632998972901622)
XLA Ops:
  14.2 55.4 %all-gather.13.cloned.1.call-done = bf16[16,1,81920]{2,1,0:T(2,128)(2,1)} async-done(((bf16[1,1,81920]{2,1,0:T(2,128)(2,1)}), bf16[16,1,81920]{2,1,0:T(2,128)(2,1)}) %all-gather.13.cloned.1.call-update) | async-done | bytes 2621456 | tf_op jit(solution)/shard_map/all_gather | solution.py:165
  69.6 5.4 %copy.95 = bf16[16,1,81920]{2,0,1:T(8,128)(2,1)S(1)} copy(bf16[16,1,81920]{2,1,0:T(2,128)(2,1)} %all-gather.13.cloned.1.call-done) | data formatting | bytes 5242880
  77.4 20.3 %all-gather.7.cloned.1.call-done = bf16[512,2048]{1,0:T(8,128)(2,1)} async-done(((bf16[512,256]{1,0:T(8,128)(2,1)}), bf16[512,2048]{1,0:T(8,128)(2,1)}) %all-gather.7.cloned.1.call-update) | async-done | bytes 2097168 | tf_op jit(solution)/shard_map/all_gather | solution.py:160
  97.7 2.6 fusion.17
  103.1 2.0 sort.17
  106.8 47.6 %all-gather.11.cloned.1.call-done = bf16[2048,1024]{1,0:T(8,128)(2,1)} async-done(((bf16[128,1024]{1,0:T(8,128)(2,1)}), bf16[2048,1024]{1,0:T(8,128)(2,1)}) %all-gather.11.cloned.1.call-update) | async-done | bytes 4194320 | tf_op jit(solution)/shard_map/all_gather | solution.py:198
  154.4 1.8 slice.108
  156.2 2.3 reshape_reshape.3
  158.5 2.5 gather_fusion.2
  161.1 2.0 broadcast_select_fusion.page_ref
  163.1 34.8 %shard_map.77 = (bf16[16,64,1024]{2,1,0:T(8,128)(2,1)S(1)}, f32[16,2,1024]{2,1,0:T(2,128)S(1)}) custom-call(s32[64]{0:T(128)S(1)} %gather_fusion, s32[64]{0:T(128)S(1)} %get-tuple-element.7.perm_ref, s32[64]{0:T(128)S(1)} %broadcast_multiply_fusion.1.kstart_ref, s32[16]{0:T(128)S(1)} %get-tuple-element.42.qstart_ref, bf16[16,128,1024]{2,1,0:T(8,128)(2,1)} %bitcast.93, ...), custom_call_target="tpu_custom_call" | custom-call | tf_op jit(solution)/shard_map/pallas_call | solution.py:146
  198.1 1.9 pad_maximum_fusion
  200.1 5.2 %all-to-all-start = ((bf16[16,70,1024]{2,1,0:T(8,128)(2,1)}), bf16[16,70,1024]{2,1,0:T(8,128)(2,1)}, u32[]{:S(2)}, u32[]{:S(2)}) async-start(bf16[16,70,1024]{2,1,0:T(8,128)(2,1)} %pad_maximum_fusion), calls=%async_computation | async-start | bytes 4718592 | tf_op jit(solution)/shard_map/all_to_all | solution.py:223
  206.9 33.9 %shard_map.78 = (bf16[16,64,1024]{2,1,0:T(8,128)(2,1)S(1)}, f32[16,2,1024]{2,1,0:T(2,128)S(1)}) custom-call(s32[64]{0:T(128)S(1)} %gather_fusion, s32[64]{0:T(128)S(1)} %get-tuple-element.7.perm_ref, s32[64]{0:T(128)S(1)} %broadcast_multiply_fusion.1.kstart_ref, s32[16]{0:T(128)S(1)} %get-tuple-element.40.qstart_ref, bf16[16,64,1024]{2,1,0:T(8,128)(2,1)S(1)} %copy-done.1, ...), custom_call_target="tpu_custom_call" | custom-call | tf_op jit(solution)/shard_map/pallas_call | solution.py:146
  240.9 1.9 pad_maximum_fusion.1
  242.8 7.0 %all-to-all-start.1 = ((bf16[16,70,1024]{2,1,0:T(8,128)(2,1)}), bf16[16,70,1024]{2,1,0:T(8,128)(2,1)S(1)}, u32[]{:S(2)}, u32[]{:S(2)}) async-start(bf16[16,70,1024]{2,1,0:T(8,128)(2,1)} %pad_maximum_fusion.1), calls=%async_computation.1 | async-start | bytes 4718592 | tf_op jit(solution)/shard_map/all_to_all | solution.py:223
  254.8 1.8 slice_convert_fusion.1
  256.6 2.0 reshape.276
  258.6 1.7 fusion.16
  260.3 21.8 %all-to-all-done.1 = bf16[16,70,1024]{2,1,0:T(8,128)(2,1)S(1)} async-done(((bf16[16,70,1024]{2,1,0:T(8,128)(2,1)}), bf16[16,70,1024]{2,1,0:T(8,128)(2,1)S(1)}, u32[]{:S(2)}, u32[]{:S(2)}) %all-to-all-start.1) | async-done | bytes 2293792 | tf_op jit(solution)/shard_map/all_to_all | solution.py:223
  283.0 2.0 reshape.277
  287.7 3.9 %multiply_reduce_fusion.1 = (f32[64,1024]{1,0:T(8,128)}, f32[64,1024]{1,0:T(8,128)}) fusion(bf16[16,70,1024]{2,1,0:T(8,128)(2,1)} %all-to-all-done, f32[16,1024]{1,0:T(8,128)S(1)} %bitcast.105, pred[16]{0:T(512)(128)(4,1)S(1)} %reduce_or.9, f32[16,1024]{1,0:T(8,128)S(1)} %bitcast.104, bf16[16,70,1024]{2,1,0:T(8,128)(2,1)S(1)} %all-to-all-done.1), kind=kLoop, calls=%fused_computation.4 | loop fusion | flops 8257536 | bytes 4849680 | tf_op jit(solution)/shard_map/reduce_sum | solution.py:234
  294.9 1.6 pad_maximum_fusion.2
  296.6 32.3 %reduce-scatter.2.cloned.1.call-done = bf16[512,256]{1,0:T(8,128)(2,1)} async-done(((bf16[512,2048]{1,0:T(8,128)(2,1)}), bf16[512,256]{1,0:T(8,128)(2,1)}) %reduce-scatter.2.cloned.1.call-update) | async-done | bytes 262160 | tf_op jit(solution)/shard_map/reduce_scatter | solution.py:240
  (91 shorter events, 27.2 us)
Async XLA Ops:
  7.2 62.5 %all-gather.13.cloned.1.call-start = ((), (), s32[]{:S(2)}) async-start(), calls=%async_computation.7 | async-start | bytes 5570560 | tf_op jit(solution)/shard_map/all_gather | solution.py:165
  10.3 87.4 %all-gather.7.cloned.1.call-start = ((), (), s32[]{:S(2)}) async-start(), calls=%async_computation.3 | async-start | bytes 2359296 | tf_op jit(solution)/shard_map/all_gather | solution.py:160
  11.1 143.4 %all-gather.11.cloned.1.call-start = ((), (), s32[]{:S(2)}) async-start(), calls=%async_computation.6 | async-start | bytes 4456448 | tf_op jit(solution)/shard_map/all_gather | solution.py:198
  75.0 1.5 copy-start.2
  77.3 23.1 %copy-start.5 = (f32[5]{0:T(128)S(1)}, f32[5]{0:T(128)}, u32[]{:S(2)}) copy-start(f32[5]{0:T(128)} %constant.14.clone.1) | copy-start | bytes 64
  100.4 1.5 copy-start.3
  100.5 5.4 %copy-start.4 = (s32[16]{0:T(128)S(1)}, s32[16]{0:T(128)}, u32[]{:S(2)}) copy-start(s32[16]{0:T(128)} %param.10) | copy-start | bytes 196
  101.8 103.4 %all-gather.9.cloned.1.call-start = ((), (), s32[]{:S(2)}) async-start(), calls=%async_computation.4 | async-start | bytes 2228224 | tf_op jit(solution)/shard_map/all_gather | solution.py:198
  163.1 34.9 %copy-start = (bf16[64,128,128]{2,1,0:T(8,128)(2,1)}, bf16[64,128,128]{2,1,0:T(8,128)(2,1)S(1)}, u32[]{:S(2)}) copy-start(bf16[64,128,128]{2,1,0:T(8,128)(2,1)S(1)} %broadcast_select_fusion.page_ref) | copy-start | bytes 6291460
  200.1 42.8 %all-to-all-start = ((bf16[16,70,1024]{2,1,0:T(8,128)(2,1)}), bf16[16,70,1024]{2,1,0:T(8,128)(2,1)}, u32[]{:S(2)}, u32[]{:S(2)}) async-start(bf16[16,70,1024]{2,1,0:T(8,128)(2,1)} %pad_maximum_fusion), calls=%async_computation | async-start | bytes 4718592 | tf_op jit(solution)/shard_map/all_to_all | solution.py:223
  205.3 1.6 copy-start.1
  242.8 39.3 %all-to-all-start.1 = ((bf16[16,70,1024]{2,1,0:T(8,128)(2,1)}), bf16[16,70,1024]{2,1,0:T(8,128)(2,1)S(1)}, u32[]{:S(2)}, u32[]{:S(2)}) async-start(bf16[16,70,1024]{2,1,0:T(8,128)(2,1)} %pad_maximum_fusion.1), calls=%async_computation.1 | async-start | bytes 4718592 | tf_op jit(solution)/shard_map/all_to_all | solution.py:223
  249.8 79.1 %reduce-scatter.2.cloned.1.call-start = ((), (), s32[]{:S(2)}) async-start(), calls=%async_computation.5 | async-start | bytes 2359296 | tf_op jit(solution)/shard_map/reduce_scatter | solution.py:240
Sparse Core Ops, SparseCore 0:
  10.7 58.8 all-gather.12
  71.3 26.3 all-gather.6
  101.9 52.4 all-gather.10
  156.4 44.6 all-gather.8
  296.7 32.1 reduce-scatter.1

commit v7 on v6

--- a/solution.py
+++ b/solution.py
@@ -157,16 +157,18 @@
 
 
 def body(hidden, qkv_weight, out_weight, kv_pages, cache_pages, slot_order):
-    whole = lax.all_gather(hidden, "tp", axis=1, tiled=True)
+    n_tp = lax.axis_size("tp")
+    copies = jnp.broadcast_to(hidden[None], (n_tp,) + hidden.shape)
+    whole = lax.all_to_all(copies, "tp", 0, 0, tiled=True)
+    whole = jnp.moveaxis(whole, 0, 1).reshape(hidden.shape[0], n_tp * hidden.shape[1])
     tok_rows = whole.shape[0]
     n_req = lax.axis_size("req")
-    qkv_size = qkv_weight.size
-    both = jnp.concatenate([qkv_weight.reshape(1, -1), out_weight.reshape(1, -1)], axis=1)
-    both = lax.all_gather(both, "req", axis=0, tiled=True)
-    qkv_full = both[:, :qkv_size].reshape(n_req * qkv_weight.shape[0], qkv_weight.shape[1])
-    out_full = jnp.moveaxis(
-        both[:, qkv_size:].reshape(n_req, out_weight.shape[0], out_weight.shape[1]), 0, 1
-    ).reshape(out_weight.shape[0], n_req * out_weight.shape[1])
+    lanes = out_weight.shape[1]
+    qkv_rows = qkv_weight.size // lanes
+    both = jnp.concatenate([qkv_weight.reshape(qkv_rows, lanes), out_weight], axis=0)
+    both = lax.all_gather(both[None], "req", axis=0, tiled=True)
+    qkv_full = both[:, :qkv_rows].reshape(n_req * qkv_weight.shape[0], qkv_weight.shape[1])
+    out_full = jnp.moveaxis(both[:, qkv_rows:], 0, 1).reshape(out_weight.shape[0], n_req * lanes)
     projected = jnp.dot(whole, qkv_full, preferred_element_type=jnp.float32)
     local_slots = kv_pages.shape[0]
     page_rows = kv_pages.shape[1]

time: 336 us -> 298 us (0.89)
  waiting for transfers between devices: 178 us -> 141 us
  starting transfers between devices: 12.6 us -> 17.7 us
  local copies, waits for them, and re-layouts: 34.4 us -> 30.4 us
    all_gather x2 -> x1, waiting for transfers between devices: 75.7 us -> 40.5 us  [body(): both = lax.all_gather(both[None], 'req', axis=0, tiled=True)]
    unnamed x19 -> x13, local copies, waits for them, and re-layouts: 12.9 us -> 2.73 us
    all_to_all x0 -> x1, starting transfers between devices: none -> 4.71 us  [body(): whole = lax.all_to_all(copies, 'tp', 0, 0, tiled=True)]
    transpose x0 -> x2, local copies, waits for them, and re-layouts: none -> 3.78 us  [body(): jnp.moveaxis(both[:, qkv_rows:], 0, 1)]
  transfers between devices with their start and end apart: 7 -> 7, of which waited for: 5 -> 4; matrix products, arithmetic and copies ran while one was open for 11% -> 12% of each run, Pallas kernels for 20% -> 23%
where the time goes in v7:
time: 298 us; the launch traced here: 297 us
  waiting for transfers between devices  141 us (47%)
  Pallas kernels  68.3 us (23%)
  local copies, waits for them, and re-layouts  30.4 us (10%)
  other arithmetic  22.3 us (7%)
  starting transfers between devices  17.7 us (6%)
  between operations  14.2 us (5%)
  matrix products  3.58 us (1%)
    pallas_call x2, Pallas kernels, slot_attention(): pl.pallas_call(kernel, grid_spec=grid_spec, out_shape=[jax.ShapeDtypeStru...  68.3 us
    all_gather x2, waiting for transfers between devices, body(): gathered.append(lax.all_gather(piece[None], 'req', axis=0, tiled=True))  45.9 us
    all_gather x1, waiting for transfers between devices, body(): both = lax.all_gather(both[None], 'req', axis=0, tiled=True)  40.5 us
    reduce_scatter x1, waiting for transfers between devices, body(): lax.psum_scatter(jnp.concatenate(outs, axis=0), 'tp', scatter_dimension=1...  32.3 us
    all_to_all x2, waiting for transfers between devices, body(): got = lax.all_to_all(sent, 'req', 0, 0, tiled=True)  22 us
    all_to_all x2, starting transfers between devices, body(): got = lax.all_to_all(sent, 'req', 0, 0, tiled=True)  12.6 us
  transfers between devices with their start and end apart: 7, of which 4 were waited for; matrix products, arithmetic and copies ran while one was open for 12% of the time, Pallas kernels for 23%

profile of v7, /device:TPU:0, one launch (start us, length us, event | category | flops | bytes accessed | tf_op | source)
XLA Modules:
  0.0 297.2 jit_solution(5520901674301761729)
XLA Ops:
  12.3 4.7 %all-to-all-start = ((bf16[8,512,256]{1,2,0:T(8,128)(2,1)}), bf16[8,512,256]{1,2,0:T(8,128)(2,1)}, u32[]{:S(2)}, u32[]{:S(2)}) async-start(bf16[8,512,256]{1,2,0:T(8,128)(2,1)} %broadcast_in_dim.146), calls=%async_computation | async-start | bytes 4194304 | tf_op jit(solution)/shard_map/all_to_all | solution.py:162
  18.9 40.5 %all-gather.8.cloned.1.call-done = bf16[10240,128]{1,0:T(8,128)(2,1)} async-done(((bf16[640,128]{1,0:T(8,128)(2,1)}), bf16[10240,128]{1,0:T(8,128)(2,1)}) %all-gather.8.cloned.1.call-update) | async-done | bytes 2621456 | tf_op jit(solution)/shard_map/all_gather | solution.py:169
  61.7 2.6 fusion.17
  67.0 2.0 sort.17
  70.8 45.8 %all-gather.10.cloned.1.call-done = bf16[2048,1024]{1,0:T(8,128)(2,1)} async-done(((bf16[128,1024]{1,0:T(8,128)(2,1)}), bf16[2048,1024]{1,0:T(8,128)(2,1)}) %all-gather.10.cloned.1.call-update) | async-done | bytes 4194320 | tf_op jit(solution)/shard_map/all_gather | solution.py:200
  116.6 1.8 slice.108
  118.4 2.3 reshape_reshape.3
  120.7 2.5 gather_fusion.2
  123.3 1.9 broadcast_select_fusion.page_ref
  125.2 34.7 %shard_map.77 = (bf16[16,64,1024]{2,1,0:T(8,128)(2,1)S(1)}, f32[16,2,1024]{2,1,0:T(2,128)S(1)}) custom-call(s32[64]{0:T(128)S(1)} %gather_fusion, s32[64]{0:T(128)S(1)} %get-tuple-element.7.perm_ref, s32[64]{0:T(128)S(1)} %broadcast_multiply_fusion.1.kstart_ref, s32[16]{0:T(128)S(1)} %get-tuple-element.42.qstart_ref, bf16[16,128,1024]{2,1,0:T(8,128)(2,1)} %bitcast.79, ...), custom_call_target="tpu_custom_call" | custom-call | tf_op jit(solution)/shard_map/pallas_call | solution.py:146
  160.0 1.9 pad_maximum_fusion
  161.9 5.4 %all-to-all-start.1 = ((bf16[16,70,1024]{2,1,0:T(8,128)(2,1)}), bf16[16,70,1024]{2,1,0:T(8,128)(2,1)}, u32[]{:S(2)}, u32[]{:S(2)}) async-start(bf16[16,70,1024]{2,1,0:T(8,128)(2,1)} %pad_maximum_fusion), calls=%async_computation.1 | async-start | bytes 4718592 | tf_op jit(solution)/shard_map/all_to_all | solution.py:225
  168.9 33.7 %shard_map.78 = (bf16[16,64,1024]{2,1,0:T(8,128)(2,1)S(1)}, f32[16,2,1024]{2,1,0:T(2,128)S(1)}) custom-call(s32[64]{0:T(128)S(1)} %gather_fusion, s32[64]{0:T(128)S(1)} %get-tuple-element.7.perm_ref, s32[64]{0:T(128)S(1)} %broadcast_multiply_fusion.1.kstart_ref, s32[16]{0:T(128)S(1)} %get-tuple-element.40.qstart_ref, bf16[16,64,1024]{2,1,0:T(8,128)(2,1)S(1)} %copy-done.1, ...), custom_call_target="tpu_custom_call" | custom-call | tf_op jit(solution)/shard_map/pallas_call | solution.py:146
  202.7 1.9 pad_maximum_fusion.1
  204.6 7.3 %all-to-all-start.2 = ((bf16[16,70,1024]{2,1,0:T(8,128)(2,1)}), bf16[16,70,1024]{2,1,0:T(8,128)(2,1)S(1)}, u32[]{:S(2)}, u32[]{:S(2)}) async-start(bf16[16,70,1024]{2,1,0:T(8,128)(2,1)} %pad_maximum_fusion.1), calls=%async_computation.2 | async-start | bytes 4718592 | tf_op jit(solution)/shard_map/all_to_all | solution.py:225
  212.9 2.3 slice_bitcast_fusion
  216.7 1.8 slice_convert_fusion.1
  218.6 2.0 reshape.272
  220.5 1.7 fusion.16
  222.3 22.0 %all-to-all-done.2 = bf16[16,70,1024]{2,1,0:T(8,128)(2,1)S(1)} async-done(((bf16[16,70,1024]{2,1,0:T(8,128)(2,1)}), bf16[16,70,1024]{2,1,0:T(8,128)(2,1)S(1)}, u32[]{:S(2)}, u32[]{:S(2)}) %all-to-all-start.2) | async-done | bytes 2293792 | tf_op jit(solution)/shard_map/all_to_all | solution.py:225
  245.1 2.0 reshape.273
  249.8 3.7 %multiply_reduce_fusion.1 = (f32[64,1024]{1,0:T(8,128)}, f32[64,1024]{1,0:T(8,128)}) fusion(bf16[16,70,1024]{2,1,0:T(8,128)(2,1)} %all-to-all-done.1, f32[16,1024]{1,0:T(8,128)S(1)} %bitcast.90, pred[16]{0:T(512)(128)(4,1)S(1)} %reduce_or.9, f32[16,1024]{1,0:T(8,128)S(1)} %bitcast.89, bf16[16,70,1024]{2,1,0:T(8,128)(2,1)S(1)} %all-to-all-done.2), kind=kLoop, calls=%fused_computation.4 | loop fusion | flops 8257536 | bytes 4849680 | tf_op jit(solution)/shard_map/reduce_sum | solution.py:236
  256.8 1.6 pad_maximum_fusion.2
  258.4 32.3 %reduce-scatter.2.cloned.1.call-done = bf16[512,256]{1,0:T(8,128)(2,1)} async-done(((bf16[512,2048]{1,0:T(8,128)(2,1)}), bf16[512,256]{1,0:T(8,128)(2,1)}) %reduce-scatter.2.cloned.1.call-update) | async-done | bytes 262160 | tf_op jit(solution)/shard_map/reduce_scatter | solution.py:242
  (87 shorter events, 24.6 us)
Async XLA Ops:
  7.2 52.3 %all-gather.8.cloned.1.call-start = ((), (), s32[]{:S(2)}) async-start(), calls=%async_computation.6 | async-start | bytes 2785280 | tf_op jit(solution)/shard_map/all_gather | solution.py:169
  12.3 4.8 %copy-start.3 = (s32[16]{0:T(128)S(1)}, s32[16]{0:T(128)}, u32[]{:S(2)}) copy-start(s32[16]{0:T(128)} %param.10) | copy-start | bytes 196
  12.3 49.4 %all-to-all-start = ((bf16[8,512,256]{1,2,0:T(8,128)(2,1)}), bf16[8,512,256]{1,2,0:T(8,128)(2,1)}, u32[]{:S(2)}, u32[]{:S(2)}) async-start(bf16[8,512,256]{1,2,0:T(8,128)(2,1)} %broadcast_in_dim.146), calls=%async_computation | async-start | bytes 4194304 | tf_op jit(solution)/shard_map/all_to_all | solution.py:162
  17.0 99.6 %all-gather.10.cloned.1.call-start = ((), (), s32[]{:S(2)}) async-start(), calls=%async_computation.7 | async-start | bytes 4456448 | tf_op jit(solution)/shard_map/all_gather | solution.py:200
  61.7 2.7 copy-start.4
  64.4 1.5 copy-start.2
  65.8 101.5 %all-gather.6.cloned.1.call-start = ((), (), s32[]{:S(2)}) async-start(), calls=%async_computation.4 | async-start | bytes 2228224 | tf_op jit(solution)/shard_map/all_gather | solution.py:200
  125.1 34.7 %copy-start = (bf16[64,128,128]{2,1,0:T(8,128)(2,1)}, bf16[64,128,128]{2,1,0:T(8,128)(2,1)S(1)}, u32[]{:S(2)}) copy-start(bf16[64,128,128]{2,1,0:T(8,128)(2,1)S(1)} %broadcast_select_fusion.page_ref) | copy-start | bytes 6291460
  161.9 42.7 %all-to-all-start.1 = ((bf16[16,70,1024]{2,1,0:T(8,128)(2,1)}), bf16[16,70,1024]{2,1,0:T(8,128)(2,1)}, u32[]{:S(2)}, u32[]{:S(2)}) async-start(bf16[16,70,1024]{2,1,0:T(8,128)(2,1)} %pad_maximum_fusion), calls=%async_computation.1 | async-start | bytes 4718592 | tf_op jit(solution)/shard_map/all_to_all | solution.py:225
  167.3 1.6 copy-start.1
  204.6 39.6 %all-to-all-start.2 = ((bf16[16,70,1024]{2,1,0:T(8,128)(2,1)}), bf16[16,70,1024]{2,1,0:T(8,128)(2,1)S(1)}, u32[]{:S(2)}, u32[]{:S(2)}) async-start(bf16[16,70,1024]{2,1,0:T(8,128)(2,1)} %pad_maximum_fusion.1), calls=%async_computation.2 | async-start | bytes 4718592 | tf_op jit(solution)/shard_map/all_to_all | solution.py:225
  211.9 78.8 %reduce-scatter.2.cloned.1.call-start = ((), (), s32[]{:S(2)}) async-start(), calls=%async_computation.5 | async-start | bytes 2359296 | tf_op jit(solution)/shard_map/reduce_scatter | solution.py:242
Sparse Core Ops, SparseCore 0:
  10.7 48.6 all-gather.7
  65.9 50.6 all-gather.9
  118.8 44.7 all-gather.5
  258.5 32.1 reduce-scatter.1

commit v8 on v7

--- a/solution.py
+++ b/solution.py
@@ -195,10 +195,9 @@
     gathered = []
     for h in range(halves):
         piece = jnp.transpose(rotated[h * sub:(h + 1) * sub, :GROUP, :], (2, 1, 0)).reshape(HD, width)
-        if h == 0:
-            piece = jnp.concatenate([piece, fresh.reshape(-1, width)], axis=0)
         gathered.append(lax.all_gather(piece[None], "req", axis=0, tiled=True))
-    fresh_all = gathered[0][:, HD:, :].reshape(requests, SPAN, 2 * HD)
+    fresh_copies = jnp.broadcast_to(fresh.reshape(1, -1, width), (n_req, fresh.size // width, width))
+    fresh_all = lax.all_to_all(fresh_copies, "req", 0, 0, tiled=True).reshape(requests, SPAN, 2 * HD)
 
     my_slots = my_index * local_slots + jnp.arange(local_slots, dtype=jnp.int32)
     slot_req, page_index, cached = locate(my_slots, cache_pages, slot_order, new_pages)

time: 298 us -> 306 us (1.027)
  starting transfers between devices: 17.7 us -> 29.1 us
  waiting for transfers between devices: 141 us -> 135 us
    all_to_all x0 -> x1, waiting for transfers between devices: none -> 25.5 us  [body(): lax.all_to_all(fresh_copies, 'req', 0, 0, tiled=True)]
    all_gather x2, waiting for transfers between devices: 45.9 us -> 24 us  [body(): gathered.append(lax.all_gather(piece[None], 'req', axis=0, tiled=True))]
    all_to_all x2, waiting for transfers between devices: 22 us -> 10.7 us  [body(): got = lax.all_to_all(sent, 'req', 0, 0, tiled=True)]
    all_to_all x2, starting transfers between devices: 12.6 us -> 19.1 us  [body(): got = lax.all_to_all(sent, 'req', 0, 0, tiled=True)]
    all_to_all x0 -> x1, starting transfers between devices: none -> 4.94 us  [body(): lax.all_to_all(fresh_copies, 'req', 0, 0, tiled=True)]
  transfers between devices with their start and end apart: 7 -> 8, of which waited for: 4 -> 6; matrix products, arithmetic and copies ran while one was open for 12% -> 11% of each run, Pallas kernels for 23% -> 22%
where the time goes in v8:
time: 306 us; the launch traced here: 305 us
  waiting for transfers between devices  135 us (44%)
  Pallas kernels  67.5 us (22%)
  local copies, waits for them, and re-layouts  32.5 us (11%)
  starting transfers between devices  29.1 us (10%)
  other arithmetic  23 us (8%)
  between operations  14.2 us (5%)
  matrix products  3.6 us (1%)
    pallas_call x2, Pallas kernels, slot_attention(): pl.pallas_call(kernel, grid_spec=grid_spec, out_shape=[jax.ShapeDtypeStru...  67.5 us
    all_gather x1, waiting for transfers between devices, body(): both = lax.all_gather(both[None], 'req', axis=0, tiled=True)  40.7 us
    reduce_scatter x1, waiting for transfers between devices, body(): lax.psum_scatter(jnp.concatenate(outs, axis=0), 'tp', scatter_dimension=1...  33.9 us
    all_to_all x1, waiting for transfers between devices, body(): lax.all_to_all(fresh_copies, 'req', 0, 0, tiled=True)  25.5 us
    all_gather x2, waiting for transfers between devices, body(): gathered.append(lax.all_gather(piece[None], 'req', axis=0, tiled=True))  24 us
    all_to_all x2, starting transfers between devices, body(): got = lax.all_to_all(sent, 'req', 0, 0, tiled=True)  19.1 us
    all_to_all x2, waiting for transfers between devices, body(): got = lax.all_to_all(sent, 'req', 0, 0, tiled=True)  10.7 us
  transfers between devices with their start and end apart: 8, of which 6 were waited for; matrix products, arithmetic and copies ran while one was open for 11% of the time, Pallas kernels for 22%

profile of v8, /device:TPU:0, one launch (start us, length us, event | category | flops | bytes accessed | tf_op | source)
XLA Modules:
  0.0 304.7 jit_solution(5199368597444951380)
XLA Ops:
  12.3 4.7 %all-to-all-start = ((bf16[8,512,256]{1,2,0:T(8,128)(2,1)}), bf16[8,512,256]{1,2,0:T(8,128)(2,1)}, u32[]{:S(2)}, u32[]{:S(2)}) async-start(bf16[8,512,256]{1,2,0:T(8,128)(2,1)} %broadcast_in_dim.150), calls=%async_computation | async-start | bytes 4194304 | tf_op jit(solution)/shard_map/all_to_all | solution.py:162
  18.8 40.7 %all-gather.9.cloned.1.call-done = bf16[10240,128]{1,0:T(8,128)(2,1)} async-done(((bf16[640,128]{1,0:T(8,128)(2,1)}), bf16[10240,128]{1,0:T(8,128)(2,1)}) %all-gather.9.cloned.1.call-update) | async-done | bytes 2621456 | tf_op jit(solution)/shard_map/all_gather | solution.py:169
  61.8 2.6 fusion.17
  67.5 4.9 %all-to-all-start.1 = ((bf16[16,64,1024]{2,1,0:T(8,128)(2,1)}), bf16[16,64,1024]{2,1,0:T(8,128)(2,1)S(1)}, u32[]{:S(2)}, u32[]{:S(2)}) async-start(bf16[16,64,1024]{2,1,0:T(8,128)(2,1)} %broadcast_in_dim.154), calls=%async_computation.1 | async-start | bytes 4194304 | tf_op jit(solution)/shard_map/all_to_all | solution.py:200
  73.7 2.1 sort.17
  77.5 25.5 %all-to-all-done.1 = bf16[16,64,1024]{2,1,0:T(8,128)(2,1)S(1)} async-done(((bf16[16,64,1024]{2,1,0:T(8,128)(2,1)}), bf16[16,64,1024]{2,1,0:T(8,128)(2,1)S(1)}, u32[]{:S(2)}, u32[]{:S(2)}) %all-to-all-start.1) | async-done | bytes 2097184 | tf_op jit(solution)/shard_map/all_to_all | solution.py:200
  103.0 2.3 reshape_reshape.3
  105.2 2.5 gather_fusion.2
  107.8 3.4 %broadcast_select_fusion.page_ref = bf16[64,128,128]{2,1,0:T(8,128)(2,1)} fusion(bf16[64,128,128]{2,1,0:T(8,128)(2,1)S(1)} %gather_fusion.2, bf16[64,128,128]{2,1,0:T(8,128)(2,1)} %param.9, pred[64]{0:T(512)(128)(4,1)S(1)} %get-tuple-element.18), kind=kLoop, calls=%fused_computation.12 | loop fusion | flops 1048576 | bytes 6291520 | tf_op jit(solution)/shard_map/jit(_where)/select_n | solution.py:60
  111.2 12.8 %all-gather.7.cloned.1.call-done.q_ref = bf16[16,64,1024]{2,1,0:T(8,128)(2,1)} async-done(((bf16[1,64,1024]{2,1,0:T(8,128)(2,1)}), bf16[16,64,1024]{2,1,0:T(8,128)(2,1)}) %all-gather.7.cloned.1.call-update) | async-done | bytes 2097168 | tf_op jit(solution)/shard_map/all_gather | solution.py:198
  125.6 33.7 %shard_map.78 = (bf16[16,64,1024]{2,1,0:T(8,128)(2,1)S(1)}, f32[16,2,1024]{2,1,0:T(2,128)S(1)}) custom-call(s32[64]{0:T(128)S(1)} %gather_fusion, s32[64]{0:T(128)S(1)} %get-tuple-element.7.perm_ref, s32[64]{0:T(128)S(1)} %broadcast_multiply_fusion.1.kstart_ref, s32[16]{0:T(128)S(1)} %get-tuple-element.40.qstart_ref, bf16[16,64,1024]{2,1,0:T(8,128)(2,1)S(1)} %copy-done, ...), custom_call_target="tpu_custom_call" | custom-call | tf_op jit(solution)/shard_map/pallas_call | solution.py:146
  159.5 1.8 pad_maximum_fusion.1
  161.2 4.9 %all-to-all-start.3 = ((bf16[16,70,1024]{2,1,0:T(8,128)(2,1)}), bf16[16,70,1024]{2,1,0:T(8,128)(2,1)S(1)}, u32[]{:S(2)}, u32[]{:S(2)}) async-start(bf16[16,70,1024]{2,1,0:T(8,128)(2,1)} %pad_maximum_fusion.1), calls=%async_computation.3 | async-start | bytes 4718592 | tf_op jit(solution)/shard_map/all_to_all | solution.py:224
  166.2 11.3 %all-gather.5.cloned.1.call-done.q_ref = bf16[16,64,1024]{2,1,0:T(8,128)(2,1)} async-done(((bf16[1,64,1024]{2,1,0:T(8,128)(2,1)}), bf16[16,64,1024]{2,1,0:T(8,128)(2,1)}) %all-gather.5.cloned.1.call-update) | async-done | bytes 2097168 | tf_op jit(solution)/shard_map/all_gather | solution.py:198
  179.0 33.8 %shard_map.77 = (bf16[16,64,1024]{2,1,0:T(8,128)(2,1)S(1)}, f32[16,2,1024]{2,1,0:T(2,128)S(1)}) custom-call(s32[64]{0:T(128)S(1)} %gather_fusion, s32[64]{0:T(128)S(1)} %get-tuple-element.7.perm_ref, s32[64]{0:T(128)S(1)} %broadcast_multiply_fusion.1.kstart_ref, s32[16]{0:T(128)S(1)} %get-tuple-element.42.qstart_ref, bf16[16,64,1024]{2,1,0:T(8,128)(2,1)S(1)} %copy-done.1, ...), custom_call_target="tpu_custom_call" | custom-call | tf_op jit(solution)/shard_map/pallas_call | solution.py:146
  212.9 1.9 pad_maximum_fusion
  214.8 14.2 %all-to-all-start.2 = ((bf16[16,70,1024]{2,1,0:T(8,128)(2,1)}), bf16[16,70,1024]{2,1,0:T(8,128)(2,1)}, u32[]{:S(2)}, u32[]{:S(2)}) async-start(bf16[16,70,1024]{2,1,0:T(8,128)(2,1)} %pad_maximum_fusion), calls=%async_computation.2 | async-start | bytes 4718592 | tf_op jit(solution)/shard_map/all_to_all | solution.py:224
  230.1 2.3 slice_bitcast_fusion
  234.7 2.0 reshape.266
  238.5 10.7 %all-to-all-done.2 = bf16[16,70,1024]{2,1,0:T(8,128)(2,1)} async-done(((bf16[16,70,1024]{2,1,0:T(8,128)(2,1)}), bf16[16,70,1024]{2,1,0:T(8,128)(2,1)}, u32[]{:S(2)}, u32[]{:S(2)}) %all-to-all-start.2) | async-done | bytes 2293792 | tf_op jit(solution)/shard_map/all_to_all | solution.py:224
  249.1 1.8 slice_convert_fusion.1
  250.9 2.0 reshape.265
  255.6 3.7 %multiply_reduce_fusion.1 = (f32[64,1024]{1,0:T(8,128)}, f32[64,1024]{1,0:T(8,128)}) fusion(bf16[16,70,1024]{2,1,0:T(8,128)(2,1)} %all-to-all-done.2, f32[16,1024]{1,0:T(8,128)S(1)} %bitcast.84, pred[16]{0:T(512)(128)(4,1)S(1)} %reduce_or.9, f32[16,1024]{1,0:T(8,128)S(1)} %bitcast.83, bf16[16,70,1024]{2,1,0:T(8,128)(2,1)S(1)} %all-to-all-done.3), kind=kLoop, calls=%fused_computation.4 | loop fusion | flops 8257536 | bytes 4849680 | tf_op jit(solution)/shard_map/reduce_sum | solution.py:235
  264.3 33.9 %reduce-scatter.2.cloned.1.call-done = bf16[512,256]{1,0:T(8,128)(2,1)} async-done(((bf16[512,2048]{1,0:T(8,128)(2,1)}), bf16[512,256]{1,0:T(8,128)(2,1)}) %reduce-scatter.2.cloned.1.call-update) | async-done | bytes 262160 | tf_op jit(solution)/shard_map/reduce_scatter | solution.py:241
  (89 shorter events, 31.2 us)
Async XLA Ops:
  7.2 52.3 %all-gather.9.cloned.1.call-start = ((), (), s32[]{:S(2)}) async-start(), calls=%async_computation.8 | async-start | bytes 2785280 | tf_op jit(solution)/shard_map/all_gather | solution.py:169
  12.3 4.8 %copy-start.3 = (s32[16]{0:T(128)S(1)}, s32[16]{0:T(128)}, u32[]{:S(2)}) copy-start(s32[16]{0:T(128)} %param.10) | copy-start | bytes 196
  12.3 49.4 %all-to-all-start = ((bf16[8,512,256]{1,2,0:T(8,128)(2,1)}), bf16[8,512,256]{1,2,0:T(8,128)(2,1)}, u32[]{:S(2)}, u32[]{:S(2)}) async-start(bf16[8,512,256]{1,2,0:T(8,128)(2,1)} %broadcast_in_dim.150), calls=%async_computation | async-start | bytes 4194304 | tf_op jit(solution)/shard_map/all_to_all | solution.py:162
  17.0 107.0 %all-gather.7.cloned.1.call-start = ((), (), s32[]{:S(2)}) async-start(), calls=%async_computation.6 | async-start | bytes 2228224 | tf_op jit(solution)/shard_map/all_gather | solution.py:198
  61.7 2.7 copy-start.4
  67.5 5.0 %copy-start.2 = (s32[1024]{0:T(1024)S(1)}, s32[1024]{0:T(1024)}, u32[]{:S(2)}) copy-start(s32[1024]{0:T(1024)} %param.11) | copy-start | bytes 12292
  67.5 35.5 %all-to-all-start.1 = ((bf16[16,64,1024]{2,1,0:T(8,128)(2,1)}), bf16[16,64,1024]{2,1,0:T(8,128)(2,1)S(1)}, u32[]{:S(2)}, u32[]{:S(2)}) async-start(bf16[16,64,1024]{2,1,0:T(8,128)(2,1)} %broadcast_in_dim.154), calls=%async_computation.1 | async-start | bytes 4194304 | tf_op jit(solution)/shard_map/all_to_all | solution.py:200
  72.4 105.0 %all-gather.5.cloned.1.call-start = ((), (), s32[]{:S(2)}) async-start(), calls=%async_computation.5 | async-start | bytes 2228224 | tf_op jit(solution)/shard_map/all_gather | solution.py:198
  124.0 1.6 copy-start
  161.2 53.6 %all-to-all-start.3 = ((bf16[16,70,1024]{2,1,0:T(8,128)(2,1)}), bf16[16,70,1024]{2,1,0:T(8,128)(2,1)S(1)}, u32[]{:S(2)}, u32[]{:S(2)}) async-start(bf16[16,70,1024]{2,1,0:T(8,128)(2,1)} %pad_maximum_fusion.1), calls=%async_computation.3 | async-start | bytes 4718592 | tf_op jit(solution)/shard_map/all_to_all | solution.py:224
  177.4 1.6 copy-start.1
  214.8 34.3 %all-to-all-start.2 = ((bf16[16,70,1024]{2,1,0:T(8,128)(2,1)}), bf16[16,70,1024]{2,1,0:T(8,128)(2,1)}, u32[]{:S(2)}, u32[]{:S(2)}) async-start(bf16[16,70,1024]{2,1,0:T(8,128)(2,1)} %pad_maximum_fusion), calls=%async_computation.2 | async-start | bytes 4718592 | tf_op jit(solution)/shard_map/all_to_all | solution.py:224
  229.0 69.1 %reduce-scatter.2.cloned.1.call-start = ((), (), s32[]{:S(2)}) async-start(), calls=%async_computation.7 | async-start | bytes 2359296 | tf_op jit(solution)/shard_map/reduce_scatter | solution.py:241
Sparse Core Ops, SparseCore 0:
  10.7 48.6 all-gather.8
  65.6 58.3 all-gather.6
  126.7 50.6 all-gather.4
  264.4 33.6 reduce-scatter.1

commit v9 on v7

--- a/solution.py
+++ b/solution.py
@@ -239,9 +239,11 @@
 
         head_terms = jnp.dot(attention_flat, out_full, preferred_element_type=jnp.float32)
         outs.append(head_terms.astype(jnp.bfloat16))
-    attention_out = lax.psum_scatter(
-        jnp.concatenate(outs, axis=0), "tp", scatter_dimension=1, tiled=True
-    )
+    partial_t = jnp.concatenate(outs, axis=0)
+    cols = partial_t.shape[1] // n_tp
+    partial_t = jnp.moveaxis(partial_t.reshape(partial_t.shape[0], n_tp, cols), 1, 0)
+    got_t = lax.all_to_all(partial_t, "tp", 0, 0, tiled=True)
+    attention_out = jnp.sum(got_t.astype(jnp.float32), axis=0).astype(jnp.bfloat16)
     return (attention_out, pages_out)
 
 

time: 298 us -> 298 us (level)
  waiting for transfers between devices: 141 us -> 109 us
  blocking collectives: 0 us -> 31.3 us
    reduce_scatter x1 -> x0, waiting for transfers between devices: 32.3 us -> none  [body(): lax.psum_scatter(jnp.concatenate(outs, axis=0), 'tp', scatter_dimension=1...]
    all_to_all x0 -> x1, blocking collectives: none -> 31.3 us  [body(): got_t = lax.all_to_all(partial_t, 'tp', 0, 0, tiled=True)]
  transfers between devices with their start and end apart: 7 -> 6, of which waited for: 4 -> 3; matrix products, arithmetic and copies ran while one was open for 12% -> 12% of each run, Pallas kernels for 23% -> 23%
where the time goes in v9:
time: 298 us; the launch traced here: 296 us
  waiting for transfers between devices  109 us (37%)
  Pallas kernels  68.4 us (23%)
  blocking collectives  31.3 us (11%)
  local copies, waits for them, and re-layouts  30.5 us (10%)
  other arithmetic  22 us (7%)
  starting transfers between devices  17.5 us (6%)
  between operations  14.2 us (5%)
  matrix products  3.57 us (1%)
    pallas_call x2, Pallas kernels, slot_attention(): pl.pallas_call(kernel, grid_spec=grid_spec, out_shape=[jax.ShapeDtypeStru...  68.4 us
    all_gather x2, waiting for transfers between devices, body(): gathered.append(lax.all_gather(piece[None], 'req', axis=0, tiled=True))  45.9 us
    all_gather x1, waiting for transfers between devices, body(): both = lax.all_gather(both[None], 'req', axis=0, tiled=True)  40.5 us
    all_to_all x1, blocking collectives, body(): got_t = lax.all_to_all(partial_t, 'tp', 0, 0, tiled=True)  31.3 us
    all_to_all x2, waiting for transfers between devices, body(): got = lax.all_to_all(sent, 'req', 0, 0, tiled=True)  22.2 us
    all_to_all x2, starting transfers between devices, body(): got = lax.all_to_all(sent, 'req', 0, 0, tiled=True)  12.7 us
  transfers between devices with their start and end apart: 6, of which 3 were waited for; matrix products, arithmetic and copies ran while one was open for 12% of the time, Pallas kernels for 23%

profile of v9, /device:TPU:0, one launch (start us, length us, event | category | flops | bytes accessed | tf_op | source)
XLA Modules:
  0.0 296.2 jit_solution(3853116823141587653)
XLA Ops:
  12.3 4.7 %all-to-all-start = ((bf16[8,512,256]{1,2,0:T(8,128)(2,1)}), bf16[8,512,256]{1,2,0:T(8,128)(2,1)}, u32[]{:S(2)}, u32[]{:S(2)}) async-start(bf16[8,512,256]{1,2,0:T(8,128)(2,1)} %broadcast_in_dim.146), calls=%async_computation | async-start | bytes 4194304 | tf_op jit(solution)/shard_map/all_to_all | solution.py:162
  18.9 40.5 %all-gather.8.cloned.1.call-done = bf16[10240,128]{1,0:T(8,128)(2,1)} async-done(((bf16[640,128]{1,0:T(8,128)(2,1)}), bf16[10240,128]{1,0:T(8,128)(2,1)}) %all-gather.8.cloned.1.call-update) | async-done | bytes 2621456 | tf_op jit(solution)/shard_map/all_gather | solution.py:169
  61.7 2.6 fusion.17
  67.0 2.0 sort.17
  70.8 45.8 %all-gather.10.cloned.1.call-done = bf16[2048,1024]{1,0:T(8,128)(2,1)} async-done(((bf16[128,1024]{1,0:T(8,128)(2,1)}), bf16[2048,1024]{1,0:T(8,128)(2,1)}) %all-gather.10.cloned.1.call-update) | async-done | bytes 4194320 | tf_op jit(solution)/shard_map/all_gather | solution.py:200
  116.6 1.8 slice.108
  118.4 2.3 reshape_reshape.3
  120.7 2.5 gather_fusion.2
  123.3 1.9 broadcast_select_fusion.page_ref
  125.2 34.7 %shard_map.77 = (bf16[16,64,1024]{2,1,0:T(8,128)(2,1)S(1)}, f32[16,2,1024]{2,1,0:T(2,128)S(1)}) custom-call(s32[64]{0:T(128)S(1)} %gather_fusion, s32[64]{0:T(128)S(1)} %get-tuple-element.7.perm_ref, s32[64]{0:T(128)S(1)} %broadcast_multiply_fusion.1.kstart_ref, s32[16]{0:T(128)S(1)} %get-tuple-element.42.qstart_ref, bf16[16,128,1024]{2,1,0:T(8,128)(2,1)} %bitcast.86, ...), custom_call_target="tpu_custom_call" | custom-call | tf_op jit(solution)/shard_map/pallas_call | solution.py:146
  160.0 1.9 pad_maximum_fusion
  161.9 5.5 %all-to-all-start.1 = ((bf16[16,70,1024]{2,1,0:T(8,128)(2,1)}), bf16[16,70,1024]{2,1,0:T(8,128)(2,1)}, u32[]{:S(2)}, u32[]{:S(2)}) async-start(bf16[16,70,1024]{2,1,0:T(8,128)(2,1)} %pad_maximum_fusion), calls=%async_computation.1 | async-start | bytes 4718592 | tf_op jit(solution)/shard_map/all_to_all | solution.py:225
  167.5 1.6 copy-done.1
  169.0 33.7 %shard_map.78 = (bf16[16,64,1024]{2,1,0:T(8,128)(2,1)S(1)}, f32[16,2,1024]{2,1,0:T(2,128)S(1)}) custom-call(s32[64]{0:T(128)S(1)} %gather_fusion, s32[64]{0:T(128)S(1)} %get-tuple-element.7.perm_ref, s32[64]{0:T(128)S(1)} %broadcast_multiply_fusion.1.kstart_ref, s32[16]{0:T(128)S(1)} %get-tuple-element.40.qstart_ref, bf16[16,64,1024]{2,1,0:T(8,128)(2,1)S(1)} %copy-done.1, ...), custom_call_target="tpu_custom_call" | custom-call | tf_op jit(solution)/shard_map/pallas_call | solution.py:146
  202.9 1.9 pad_maximum_fusion.1
  204.8 7.2 %all-to-all-start.2 = ((bf16[16,70,1024]{2,1,0:T(8,128)(2,1)}), bf16[16,70,1024]{2,1,0:T(8,128)(2,1)S(1)}, u32[]{:S(2)}, u32[]{:S(2)}) async-start(bf16[16,70,1024]{2,1,0:T(8,128)(2,1)} %pad_maximum_fusion.1), calls=%async_computation.2 | async-start | bytes 4718592 | tf_op jit(solution)/shard_map/all_to_all | solution.py:225
  212.9 2.3 slice_bitcast_fusion
  216.7 1.8 slice_convert_fusion.1
  218.5 2.0 reshape.276
  220.5 1.7 fusion.16
  222.2 22.2 %all-to-all-done.2 = bf16[16,70,1024]{2,1,0:T(8,128)(2,1)S(1)} async-done(((bf16[16,70,1024]{2,1,0:T(8,128)(2,1)}), bf16[16,70,1024]{2,1,0:T(8,128)(2,1)S(1)}, u32[]{:S(2)}, u32[]{:S(2)}) %all-to-all-start.2) | async-done | bytes 2293792 | tf_op jit(solution)/shard_map/all_to_all | solution.py:225
  245.2 2.0 reshape.277
  249.9 3.7 %multiply_reduce_fusion.1 = (f32[64,1024]{1,0:T(8,128)}, f32[64,1024]{1,0:T(8,128)}) fusion(bf16[16,70,1024]{2,1,0:T(8,128)(2,1)} %all-to-all-done.1, f32[16,1024]{1,0:T(8,128)S(1)} %bitcast.99, pred[16]{0:T(512)(128)(4,1)S(1)} %reduce_or.9, f32[16,1024]{1,0:T(8,128)S(1)} %bitcast.98, bf16[16,70,1024]{2,1,0:T(8,128)(2,1)S(1)} %all-to-all-done.2), kind=kLoop, calls=%fused_computation.4 | loop fusion | flops 8257536 | bytes 4849680 | tf_op jit(solution)/shard_map/reduce_sum | solution.py:236
  257.3 31.3 %all_to_all.20 = bf16[8,512,256]{2,1,0:T(8,128)(2,1)S(1)} all-to-all(bf16[8,512,256]{2,1,0:T(8,128)(2,1)S(1)} %bitcast.90), channel_id=1, replica_groups=mesh['req'=16,'tp'=8] {'tp'}, dimensions={0} | all-to-all | bytes 4194304 | tf_op jit(solution)/shard_map/all_to_all | solution.py:245
  (87 shorter events, 24.2 us)
Async XLA Ops:
  7.2 52.3 %all-gather.8.cloned.1.call-start = ((), (), s32[]{:S(2)}) async-start(), calls=%async_computation.5 | async-start | bytes 2785280 | tf_op jit(solution)/shard_map/all_gather | solution.py:169
  12.3 4.8 %copy-start.3 = (s32[16]{0:T(128)S(1)}, s32[16]{0:T(128)}, u32[]{:S(2)}) copy-start(s32[16]{0:T(128)} %param.10) | copy-start | bytes 196
  12.3 49.4 %all-to-all-start = ((bf16[8,512,256]{1,2,0:T(8,128)(2,1)}), bf16[8,512,256]{1,2,0:T(8,128)(2,1)}, u32[]{:S(2)}, u32[]{:S(2)}) async-start(bf16[8,512,256]{1,2,0:T(8,128)(2,1)} %broadcast_in_dim.146), calls=%async_computation | async-start | bytes 4194304 | tf_op jit(solution)/shard_map/all_to_all | solution.py:162
  17.0 99.6 %all-gather.10.cloned.1.call-start = ((), (), s32[]{:S(2)}) async-start(), calls=%async_computation.6 | async-start | bytes 4456448 | tf_op jit(solution)/shard_map/all_gather | solution.py:200
  61.7 2.7 copy-start.4
  64.4 1.5 copy-start.2
  65.8 101.6 %all-gather.6.cloned.1.call-start = ((), (), s32[]{:S(2)}) async-start(), calls=%async_computation.4 | async-start | bytes 2228224 | tf_op jit(solution)/shard_map/all_gather | solution.py:200
  125.1 34.7 %copy-start = (bf16[64,128,128]{2,1,0:T(8,128)(2,1)}, bf16[64,128,128]{2,1,0:T(8,128)(2,1)S(1)}, u32[]{:S(2)}) copy-start(bf16[64,128,128]{2,1,0:T(8,128)(2,1)S(1)} %broadcast_select_fusion.page_ref) | copy-start | bytes 6291460
  161.9 42.9 %all-to-all-start.1 = ((bf16[16,70,1024]{2,1,0:T(8,128)(2,1)}), bf16[16,70,1024]{2,1,0:T(8,128)(2,1)}, u32[]{:S(2)}, u32[]{:S(2)}) async-start(bf16[16,70,1024]{2,1,0:T(8,128)(2,1)} %pad_maximum_fusion), calls=%async_computation.1 | async-start | bytes 4718592 | tf_op jit(solution)/shard_map/all_to_all | solution.py:225
  167.4 1.6 copy-start.1
  204.8 39.6 %all-to-all-start.2 = ((bf16[16,70,1024]{2,1,0:T(8,128)(2,1)}), bf16[16,70,1024]{2,1,0:T(8,128)(2,1)S(1)}, u32[]{:S(2)}, u32[]{:S(2)}) async-start(bf16[16,70,1024]{2,1,0:T(8,128)(2,1)} %pad_maximum_fusion.1), calls=%async_computation.2 | async-start | bytes 4718592 | tf_op jit(solution)/shard_map/all_to_all | solution.py:225
Sparse Core Ops, SparseCore 0:
  10.7 48.6 all-gather.7
  65.9 50.6 all-gather.9
  118.8 44.7 all-gather.5

commit v10 on v9

--- a/solution.py
+++ b/solution.py
@@ -239,11 +239,13 @@
 
         head_terms = jnp.dot(attention_flat, out_full, preferred_element_type=jnp.float32)
         outs.append(head_terms.astype(jnp.bfloat16))
-    partial_t = jnp.concatenate(outs, axis=0)
+    first_out = lax.psum_scatter(outs[0], "tp", scatter_dimension=1, tiled=True)
+    partial_t = outs[1]
     cols = partial_t.shape[1] // n_tp
     partial_t = jnp.moveaxis(partial_t.reshape(partial_t.shape[0], n_tp, cols), 1, 0)
     got_t = lax.all_to_all(partial_t, "tp", 0, 0, tiled=True)
-    attention_out = jnp.sum(got_t.astype(jnp.float32), axis=0).astype(jnp.bfloat16)
+    second_out = jnp.sum(got_t.astype(jnp.float32), axis=0).astype(jnp.bfloat16)
+    attention_out = jnp.concatenate([first_out, second_out], axis=0)
     return (attention_out, pages_out)
 
 

time: 298 us -> 300 us (level)
  waiting for transfers between devices: 109 us -> 119 us
  blocking collectives: 31.3 us -> 23.2 us
    reduce_scatter x0 -> x1, waiting for transfers between devices: none -> 10.5 us  [body(): first_out = lax.psum_scatter(outs[0], 'tp', scatter_dimension=1, tiled=True)]
    all_to_all x1, blocking collectives: 31.3 us -> 23.2 us  [body(): got_t = lax.all_to_all(partial_t, 'tp', 0, 0, tiled=True)]
  transfers between devices with their start and end apart: 6 -> 7, of which waited for: 3 -> 4; matrix products, arithmetic and copies ran while one was open for 12% -> 12% of each run, Pallas kernels for 23% -> 23%
where the time goes in v10:
time: 300 us; the launch traced here: 299 us
  waiting for transfers between devices  119 us (40%)
  Pallas kernels  68.1 us (23%)
  local copies, waits for them, and re-layouts  29.6 us (10%)
  blocking collectives  23.2 us (8%)
  other arithmetic  22.5 us (8%)
  starting transfers between devices  17.9 us (6%)
  between operations  14.2 us (5%)
  matrix products  4.57 us (2%)
    pallas_call x2, Pallas kernels, slot_attention(): pl.pallas_call(kernel, grid_spec=grid_spec, out_shape=[jax.ShapeDtypeStru...  68.1 us
    all_gather x2, waiting for transfers between devices, body(): gathered.append(lax.all_gather(piece[None], 'req', axis=0, tiled=True))  45.9 us
    all_gather x1, waiting for transfers between devices, body(): both = lax.all_gather(both[None], 'req', axis=0, tiled=True)  40.5 us
    all_to_all x1, blocking collectives, body(): got_t = lax.all_to_all(partial_t, 'tp', 0, 0, tiled=True)  23.2 us
    all_to_all x2, waiting for transfers between devices, body(): got = lax.all_to_all(sent, 'req', 0, 0, tiled=True)  22 us
    all_to_all x2, starting transfers between devices, body(): got = lax.all_to_all(sent, 'req', 0, 0, tiled=True)  12.8 us
    reduce_scatter x1, waiting for transfers between devices, body(): first_out = lax.psum_scatter(outs[0], 'tp', scatter_dimension=1, tiled=True)  10.5 us
  transfers between devices with their start and end apart: 7, of which 4 were waited for; matrix products, arithmetic and copies ran while one was open for 12% of the time, Pallas kernels for 23%

profile of v10, /device:TPU:0, one launch (start us, length us, event | category | flops | bytes accessed | tf_op | source)
XLA Modules:
  0.0 299.0 jit_solution(17123284121118233341)
XLA Ops:
  12.3 4.7 %all-to-all-start = ((bf16[8,512,256]{1,2,0:T(8,128)(2,1)}), bf16[8,512,256]{1,2,0:T(8,128)(2,1)}, u32[]{:S(2)}, u32[]{:S(2)}) async-start(bf16[8,512,256]{1,2,0:T(8,128)(2,1)} %broadcast_in_dim.146), calls=%async_computation | async-start | bytes 4194304 | tf_op jit(solution)/shard_map/all_to_all | solution.py:162
  18.9 40.5 %all-gather.8.cloned.1.call-done = bf16[10240,128]{1,0:T(8,128)(2,1)} async-done(((bf16[640,128]{1,0:T(8,128)(2,1)}), bf16[10240,128]{1,0:T(8,128)(2,1)}) %all-gather.8.cloned.1.call-update) | async-done | bytes 2621456 | tf_op jit(solution)/shard_map/all_gather | solution.py:169
  61.7 2.6 fusion.17
  67.0 2.0 sort.17
  70.8 45.8 %all-gather.10.cloned.1.call-done = bf16[2048,1024]{1,0:T(8,128)(2,1)} async-done(((bf16[128,1024]{1,0:T(8,128)(2,1)}), bf16[2048,1024]{1,0:T(8,128)(2,1)}) %all-gather.10.cloned.1.call-update) | async-done | bytes 4194320 | tf_op jit(solution)/shard_map/all_gather | solution.py:200
  116.6 1.8 slice.108
  118.4 2.3 reshape_reshape.3
  120.7 2.5 gather_fusion.2
  123.3 1.9 broadcast_select_fusion.page_ref
  125.2 34.5 %shard_map.77 = (bf16[16,64,1024]{2,1,0:T(8,128)(2,1)S(1)}, f32[16,2,1024]{2,1,0:T(2,128)S(1)}) custom-call(s32[64]{0:T(128)S(1)} %gather_fusion, s32[64]{0:T(128)S(1)} %get-tuple-element.7.perm_ref, s32[64]{0:T(128)S(1)} %broadcast_multiply_fusion.1.kstart_ref, s32[16]{0:T(128)S(1)} %get-tuple-element.42.qstart_ref, bf16[16,128,1024]{2,1,0:T(8,128)(2,1)} %bitcast.86, ...), custom_call_target="tpu_custom_call" | custom-call | tf_op jit(solution)/shard_map/pallas_call | solution.py:146
  159.9 1.9 pad_maximum_fusion
  161.8 5.5 %all-to-all-start.1 = ((bf16[16,70,1024]{2,1,0:T(8,128)(2,1)}), bf16[16,70,1024]{2,1,0:T(8,128)(2,1)}, u32[]{:S(2)}, u32[]{:S(2)}) async-start(bf16[16,70,1024]{2,1,0:T(8,128)(2,1)} %pad_maximum_fusion), calls=%async_computation.1 | async-start | bytes 4718592 | tf_op jit(solution)/shard_map/all_to_all | solution.py:225
  168.9 33.5 %shard_map.78 = (bf16[16,64,1024]{2,1,0:T(8,128)(2,1)S(1)}, f32[16,2,1024]{2,1,0:T(2,128)S(1)}) custom-call(s32[64]{0:T(128)S(1)} %gather_fusion, s32[64]{0:T(128)S(1)} %get-tuple-element.7.perm_ref, s32[64]{0:T(128)S(1)} %broadcast_multiply_fusion.1.kstart_ref, s32[16]{0:T(128)S(1)} %get-tuple-element.40.qstart_ref, bf16[16,64,1024]{2,1,0:T(8,128)(2,1)S(1)} %copy-done.1, ...), custom_call_target="tpu_custom_call" | custom-call | tf_op jit(solution)/shard_map/pallas_call | solution.py:146
  202.6 1.9 pad_maximum_fusion.1
  204.5 7.4 %all-to-all-start.2 = ((bf16[16,70,1024]{2,1,0:T(8,128)(2,1)}), bf16[16,70,1024]{2,1,0:T(8,128)(2,1)S(1)}, u32[]{:S(2)}, u32[]{:S(2)}) async-start(bf16[16,70,1024]{2,1,0:T(8,128)(2,1)} %pad_maximum_fusion.1), calls=%async_computation.3 | async-start | bytes 4718592 | tf_op jit(solution)/shard_map/all_to_all | solution.py:225
  212.9 2.3 slice_bitcast_fusion
  216.7 1.8 slice_convert_fusion.1
  218.5 2.0 reshape.276
  220.4 1.8 fusion.16
  222.2 22.0 %all-to-all-done.2 = bf16[16,70,1024]{2,1,0:T(8,128)(2,1)S(1)} async-done(((bf16[16,70,1024]{2,1,0:T(8,128)(2,1)}), bf16[16,70,1024]{2,1,0:T(8,128)(2,1)S(1)}, u32[]{:S(2)}, u32[]{:S(2)}) %all-to-all-start.2) | async-done | bytes 2293792 | tf_op jit(solution)/shard_map/all_to_all | solution.py:225
  245.0 2.0 reshape.277
  249.6 3.7 %multiply_reduce_fusion.1 = (f32[64,1024]{1,0:T(8,128)}, f32[64,1024]{1,0:T(8,128)}) fusion(bf16[16,70,1024]{2,1,0:T(8,128)(2,1)} %all-to-all-done.1, f32[16,1024]{1,0:T(8,128)S(1)} %bitcast.99, pred[16]{0:T(512)(128)(4,1)S(1)} %reduce_or.9, f32[16,1024]{1,0:T(8,128)S(1)} %bitcast.98, bf16[16,70,1024]{2,1,0:T(8,128)(2,1)S(1)} %all-to-all-done.2), kind=kLoop, calls=%fused_computation.4 | loop fusion | flops 8257536 | bytes 4849680 | tf_op jit(solution)/shard_map/reduce_sum | solution.py:236
  257.0 23.2 %all_to_all.20 = bf16[8,256,256]{2,1,0:T(8,128)(2,1)S(1)} all-to-all(bf16[8,256,256]{2,1,0:T(8,128)(2,1)S(1)} %bitcast.90), channel_id=1, replica_groups=mesh['req'=16,'tp'=8] {'tp'}, dimensions={0} | all-to-all | bytes 2097152 | tf_op jit(solution)/shard_map/all_to_all | solution.py:246
  280.3 10.5 %reduce-scatter.2.cloned.1.call-done = bf16[256,256]{1,0:T(8,128)(2,1)} async-done(((bf16[256,2048]{1,0:T(8,128)(2,1)}), bf16[256,256]{1,0:T(8,128)(2,1)}) %reduce-scatter.2.cloned.1.call-update) | async-done | bytes 131088 | tf_op jit(solution)/shard_map/reduce_scatter | solution.py:242
  (92 shorter events, 26.6 us)
Async XLA Ops:
  7.2 52.3 %all-gather.8.cloned.1.call-start = ((), (), s32[]{:S(2)}) async-start(), calls=%async_computation.7 | async-start | bytes 2785280 | tf_op jit(solution)/shard_map/all_gather | solution.py:169
  12.3 4.8 %copy-start.4 = (s32[16]{0:T(128)S(1)}, s32[16]{0:T(128)}, u32[]{:S(2)}) copy-start(s32[16]{0:T(128)} %param.10) | copy-start | bytes 196
  12.3 49.4 %all-to-all-start = ((bf16[8,512,256]{1,2,0:T(8,128)(2,1)}), bf16[8,512,256]{1,2,0:T(8,128)(2,1)}, u32[]{:S(2)}, u32[]{:S(2)}) async-start(bf16[8,512,256]{1,2,0:T(8,128)(2,1)} %broadcast_in_dim.146), calls=%async_computation | async-start | bytes 4194304 | tf_op jit(solution)/shard_map/all_to_all | solution.py:162
  17.0 99.6 %all-gather.10.cloned.1.call-start = ((), (), s32[]{:S(2)}) async-start(), calls=%async_computation.8 | async-start | bytes 4456448 | tf_op jit(solution)/shard_map/all_gather | solution.py:200
  61.7 2.7 copy-start.5
  64.4 1.5 copy-start.3
  65.8 101.5 %all-gather.6.cloned.1.call-start = ((), (), s32[]{:S(2)}) async-start(), calls=%async_computation.6 | async-start | bytes 2228224 | tf_op jit(solution)/shard_map/all_gather | solution.py:200
  125.1 34.6 %copy-start = (bf16[64,128,128]{2,1,0:T(8,128)(2,1)}, bf16[64,128,128]{2,1,0:T(8,128)(2,1)S(1)}, u32[]{:S(2)}) copy-start(bf16[64,128,128]{2,1,0:T(8,128)(2,1)S(1)} %broadcast_select_fusion.page_ref) | copy-start | bytes 6291460
  161.8 42.7 %all-to-all-start.1 = ((bf16[16,70,1024]{2,1,0:T(8,128)(2,1)}), bf16[16,70,1024]{2,1,0:T(8,128)(2,1)}, u32[]{:S(2)}, u32[]{:S(2)}) async-start(bf16[16,70,1024]{2,1,0:T(8,128)(2,1)} %pad_maximum_fusion), calls=%async_computation.1 | async-start | bytes 4718592 | tf_op jit(solution)/shard_map/all_to_all | solution.py:225
  167.3 1.6 copy-start.1
  204.5 39.7 %all-to-all-start.2 = ((bf16[16,70,1024]{2,1,0:T(8,128)(2,1)}), bf16[16,70,1024]{2,1,0:T(8,128)(2,1)S(1)}, u32[]{:S(2)}, u32[]{:S(2)}) async-start(bf16[16,70,1024]{2,1,0:T(8,128)(2,1)} %pad_maximum_fusion.1), calls=%async_computation.3 | async-start | bytes 4718592 | tf_op jit(solution)/shard_map/all_to_all | solution.py:225
  211.8 79.0 %reduce-scatter.2.cloned.1.call-start = ((), (), s32[]{:S(2)}) async-start(), calls=%async_computation.5 | async-start | bytes 1179648 | tf_op jit(solution)/shard_map/reduce_scatter | solution.py:242
  253.3 2.7 copy-start.2
Sparse Core Ops, SparseCore 0:
  10.7 48.6 all-gather.7
  65.9 50.6 all-gather.9
  118.8 44.7 all-gather.5
  256.1 34.6 reduce-scatter.1

commit v11 on v9

--- a/solution.py
+++ b/solution.py
@@ -158,15 +158,13 @@
 
 def body(hidden, qkv_weight, out_weight, kv_pages, cache_pages, slot_order):
     n_tp = lax.axis_size("tp")
-    copies = jnp.broadcast_to(hidden[None], (n_tp,) + hidden.shape)
-    whole = lax.all_to_all(copies, "tp", 0, 0, tiled=True)
-    whole = jnp.moveaxis(whole, 0, 1).reshape(hidden.shape[0], n_tp * hidden.shape[1])
+    whole = lax.all_gather(hidden, "tp", axis=1, tiled=True)
     tok_rows = whole.shape[0]
     n_req = lax.axis_size("req")
     lanes = out_weight.shape[1]
     qkv_rows = qkv_weight.size // lanes
     both = jnp.concatenate([qkv_weight.reshape(qkv_rows, lanes), out_weight], axis=0)
-    both = lax.all_gather(both[None], "req", axis=0, tiled=True)
+    both = lax.all_to_all(jnp.broadcast_to(both[None], (n_req,) + both.shape), "req", 0, 0, tiled=True)
     qkv_full = both[:, :qkv_rows].reshape(n_req * qkv_weight.shape[0], qkv_weight.shape[1])
     out_full = jnp.moveaxis(both[:, qkv_rows:], 0, 1).reshape(out_weight.shape[0], n_req * lanes)
     projected = jnp.dot(whole, qkv_full, preferred_element_type=jnp.float32)

time: 298 us -> 296 us (level)
  starting transfers between devices: 17.5 us -> 20.9 us
  waiting for transfers between devices: 109 us -> 106 us
    all_gather x1, waiting for transfers between devices: 40.5 us -> 0.02 us  [body(): whole = lax.all_gather(hidden, 'tp', axis=1, tiled=True)]
    all_to_all x1, waiting for transfers between devices: 0.01 us -> 35.2 us  [body(): lax.all_to_all(jnp.broadcast_to(both[None], (n_req,) + both.shape), 'req'...]
    transpose x2 -> x0, local copies, waits for them, and re-layouts: 3.78 us -> none  [body(): jnp.moveaxis(both[:, qkv_rows:], 0, 1)]
    all_to_all x1, starting transfers between devices: 4.71 us -> 8.17 us  [body(): lax.all_to_all(jnp.broadcast_to(both[None], (n_req,) + both.shape), 'req'...]
where the time goes in v11:
time: 296 us; the launch traced here: 295 us
  waiting for transfers between devices  106 us (36%)
  Pallas kernels  68.4 us (23%)
  blocking collectives  31.3 us (11%)
  local copies, waits for them, and re-layouts  29.4 us (10%)
  starting transfers between devices  20.9 us (7%)
  other arithmetic  20.5 us (7%)
  between operations  14.2 us (5%)
  matrix products  3.63 us (1%)
    pallas_call x2, Pallas kernels, slot_attention(): pl.pallas_call(kernel, grid_spec=grid_spec, out_shape=[jax.ShapeDtypeStru...  68.4 us
    all_gather x2, waiting for transfers between devices, body(): gathered.append(lax.all_gather(piece[None], 'req', axis=0, tiled=True))  45.7 us
    all_to_all x1, waiting for transfers between devices, body(): lax.all_to_all(jnp.broadcast_to(both[None], (n_req,) + both.shape), 'req'...  35.2 us
    all_to_all x1, blocking collectives, body(): got_t = lax.all_to_all(partial_t, 'tp', 0, 0, tiled=True)  31.3 us
    all_to_all x2, waiting for transfers between devices, body(): got = lax.all_to_all(sent, 'req', 0, 0, tiled=True)  24.7 us
    all_to_all x2, starting transfers between devices, body(): got = lax.all_to_all(sent, 'req', 0, 0, tiled=True)  12.6 us
    all_to_all x1, starting transfers between devices, body(): lax.all_to_all(jnp.broadcast_to(both[None], (n_req,) + both.shape), 'req'...  8.17 us
  transfers between devices with their start and end apart: 6, of which 3 were waited for; matrix products, arithmetic and copies ran while one was open for 12% of the time, Pallas kernels for 23%

profile of v11, /device:TPU:0, one launch (start us, length us, event | category | flops | bytes accessed | tf_op | source)
XLA Modules:
  0.0 294.7 jit_solution(12233392450289561417)
XLA Ops:
  9.9 1.8 broadcast_in_dim.142
  11.8 8.2 %all-to-all-start = ((bf16[16,640,128]{1,2,0:T(8,128)(2,1)}), bf16[16,640,128]{1,2,0:T(8,128)(2,1)}, u32[]{:S(2)}, u32[]{:S(2)}) async-start(bf16[16,640,128]{1,2,0:T(8,128)(2,1)} %broadcast_in_dim.142), calls=%async_computation | async-start | bytes 5242880 | tf_op jit(solution)/shard_map/all_to_all | solution.py:167
  21.9 35.2 %all-to-all-done = bf16[16,640,128]{1,2,0:T(8,128)(2,1)} async-done(((bf16[16,640,128]{1,2,0:T(8,128)(2,1)}), bf16[16,640,128]{1,2,0:T(8,128)(2,1)}, u32[]{:S(2)}, u32[]{:S(2)}) %all-to-all-start) | async-done | bytes 2621472 | tf_op jit(solution)/shard_map/all_to_all | solution.py:167
  57.1 1.6 slice.102
  60.5 2.6 fusion.17
  65.8 2.0 sort.17
  69.5 45.6 %all-gather.9.cloned.1.call-done = bf16[2048,1024]{1,0:T(8,128)(2,1)} async-done(((bf16[128,1024]{1,0:T(8,128)(2,1)}), bf16[2048,1024]{1,0:T(8,128)(2,1)}) %all-gather.9.cloned.1.call-update) | async-done | bytes 4194320 | tf_op jit(solution)/shard_map/all_gather | solution.py:198
  115.2 1.8 slice.108
  117.0 2.3 reshape_reshape.3
  119.3 2.5 gather_fusion.2
  121.8 1.9 broadcast_select_fusion.page_ref
  123.7 34.8 %shard_map.77 = (bf16[16,64,1024]{2,1,0:T(8,128)(2,1)S(1)}, f32[16,2,1024]{2,1,0:T(2,128)S(1)}) custom-call(s32[64]{0:T(128)S(1)} %gather_fusion, s32[64]{0:T(128)S(1)} %get-tuple-element.7.perm_ref, s32[64]{0:T(128)S(1)} %broadcast_multiply_fusion.1.kstart_ref, s32[16]{0:T(128)S(1)} %get-tuple-element.42.qstart_ref, bf16[16,128,1024]{2,1,0:T(8,128)(2,1)} %bitcast.82, ...), custom_call_target="tpu_custom_call" | custom-call | tf_op jit(solution)/shard_map/pallas_call | solution.py:146
  158.7 1.9 pad_maximum_fusion
  160.6 5.4 %all-to-all-start.1 = ((bf16[16,70,1024]{2,1,0:T(8,128)(2,1)}), bf16[16,70,1024]{2,1,0:T(8,128)(2,1)}, u32[]{:S(2)}, u32[]{:S(2)}) async-start(bf16[16,70,1024]{2,1,0:T(8,128)(2,1)} %pad_maximum_fusion), calls=%async_computation.1 | async-start | bytes 4718592 | tf_op jit(solution)/shard_map/all_to_all | solution.py:223
  167.6 33.7 %shard_map.78 = (bf16[16,64,1024]{2,1,0:T(8,128)(2,1)S(1)}, f32[16,2,1024]{2,1,0:T(2,128)S(1)}) custom-call(s32[64]{0:T(128)S(1)} %gather_fusion, s32[64]{0:T(128)S(1)} %get-tuple-element.7.perm_ref, s32[64]{0:T(128)S(1)} %broadcast_multiply_fusion.1.kstart_ref, s32[16]{0:T(128)S(1)} %get-tuple-element.40.qstart_ref, bf16[16,64,1024]{2,1,0:T(8,128)(2,1)S(1)} %copy-done.1, ...), custom_call_target="tpu_custom_call" | custom-call | tf_op jit(solution)/shard_map/pallas_call | solution.py:146
  201.4 1.9 pad_maximum_fusion.1
  203.3 7.3 %all-to-all-start.2 = ((bf16[16,70,1024]{2,1,0:T(8,128)(2,1)}), bf16[16,70,1024]{2,1,0:T(8,128)(2,1)S(1)}, u32[]{:S(2)}, u32[]{:S(2)}) async-start(bf16[16,70,1024]{2,1,0:T(8,128)(2,1)} %pad_maximum_fusion.1), calls=%async_computation.2 | async-start | bytes 4718592 | tf_op jit(solution)/shard_map/all_to_all | solution.py:223
  212.7 1.8 slice_convert_fusion.1
  214.5 2.0 reshape.271
  216.5 1.7 fusion.16
  218.3 24.7 %all-to-all-done.2 = bf16[16,70,1024]{2,1,0:T(8,128)(2,1)S(1)} async-done(((bf16[16,70,1024]{2,1,0:T(8,128)(2,1)}), bf16[16,70,1024]{2,1,0:T(8,128)(2,1)S(1)}, u32[]{:S(2)}, u32[]{:S(2)}) %all-to-all-start.2) | async-done | bytes 2293792 | tf_op jit(solution)/shard_map/all_to_all | solution.py:223
  243.8 2.0 reshape.272
  248.4 3.7 %multiply_reduce_fusion.1 = (f32[64,1024]{1,0:T(8,128)}, f32[64,1024]{1,0:T(8,128)}) fusion(bf16[16,70,1024]{2,1,0:T(8,128)(2,1)} %all-to-all-done.1, f32[16,1024]{1,0:T(8,128)S(1)} %bitcast.93, pred[16]{0:T(512)(128)(4,1)S(1)} %reduce_or.9, f32[16,1024]{1,0:T(8,128)S(1)} %bitcast.92, bf16[16,70,1024]{2,1,0:T(8,128)(2,1)S(1)} %all-to-all-done.2), kind=kLoop, calls=%fused_computation.4 | loop fusion | flops 8257536 | bytes 4849680 | tf_op jit(solution)/shard_map/reduce_sum | solution.py:234
  255.8 31.3 %all_to_all.20 = bf16[8,512,256]{2,1,0:T(8,128)(2,1)S(1)} all-to-all(bf16[8,512,256]{2,1,0:T(8,128)(2,1)S(1)} %bitcast.86), channel_id=1, replica_groups=mesh['req'=16,'tp'=8] {'tp'}, dimensions={0} | all-to-all | bytes 4194304 | tf_op jit(solution)/shard_map/all_to_all | solution.py:243
  (88 shorter events, 22.7 us)
Async XLA Ops:
  7.2 53.3 %all-gather.5.cloned.1.call-start = ((), (), s32[]{:S(2)}) async-start(), calls=%async_computation.4 | async-start | bytes 2359296 | tf_op jit(solution)/shard_map/all_gather | solution.py:161
  11.8 8.2 %copy-start.3 = (s32[16]{0:T(128)S(1)}, s32[16]{0:T(128)}, u32[]{:S(2)}) copy-start(s32[16]{0:T(128)} %param.10) | copy-start | bytes 196
  11.8 45.3 %all-to-all-start = ((bf16[16,640,128]{1,2,0:T(8,128)(2,1)}), bf16[16,640,128]{1,2,0:T(8,128)(2,1)}, u32[]{:S(2)}, u32[]{:S(2)}) async-start(bf16[16,640,128]{1,2,0:T(8,128)(2,1)} %broadcast_in_dim.142), calls=%async_computation | async-start | bytes 5242880 | tf_op jit(solution)/shard_map/all_to_all | solution.py:167
  20.0 95.2 %all-gather.9.cloned.1.call-start = ((), (), s32[]{:S(2)}) async-start(), calls=%async_computation.6 | async-start | bytes 4456448 | tf_op jit(solution)/shard_map/all_gather | solution.py:198
  60.4 2.8 copy-start.4
  63.1 1.5 copy-start.2
  64.6 101.4 %all-gather.7.cloned.1.call-start = ((), (), s32[]{:S(2)}) async-start(), calls=%async_computation.5 | async-start | bytes 2228224 | tf_op jit(solution)/shard_map/all_gather | solution.py:198
  123.7 34.8 %copy-start = (bf16[64,128,128]{2,1,0:T(8,128)(2,1)}, bf16[64,128,128]{2,1,0:T(8,128)(2,1)S(1)}, u32[]{:S(2)}) copy-start(bf16[64,128,128]{2,1,0:T(8,128)(2,1)S(1)} %broadcast_select_fusion.page_ref) | copy-start | bytes 6291460
  160.6 42.7 %all-to-all-start.1 = ((bf16[16,70,1024]{2,1,0:T(8,128)(2,1)}), bf16[16,70,1024]{2,1,0:T(8,128)(2,1)}, u32[]{:S(2)}, u32[]{:S(2)}) async-start(bf16[16,70,1024]{2,1,0:T(8,128)(2,1)} %pad_maximum_fusion), calls=%async_computation.1 | async-start | bytes 4718592 | tf_op jit(solution)/shard_map/all_to_all | solution.py:223
  166.0 1.6 copy-start.1
  203.3 39.6 %all-to-all-start.2 = ((bf16[16,70,1024]{2,1,0:T(8,128)(2,1)}), bf16[16,70,1024]{2,1,0:T(8,128)(2,1)S(1)}, u32[]{:S(2)}, u32[]{:S(2)}) async-start(bf16[16,70,1024]{2,1,0:T(8,128)(2,1)} %pad_maximum_fusion.1), calls=%async_computation.2 | async-start | bytes 4718592 | tf_op jit(solution)/shard_map/all_to_all | solution.py:223
Sparse Core Ops, SparseCore 0:
  9.7 29.2 all-gather.4
  64.7 50.4 all-gather.8
  117.3 44.6 all-gather.6

commit v12 on v11

--- a/solution.py
+++ b/solution.py
@@ -65,70 +65,101 @@
     slots, page_rows, _ = pages.shape
     assert width == GROUP * sub and sub & (sub - 1) == 0
 
+    assert slots % 2 == 0
+
     def kernel(sreq_ref, perm_ref, kstart_ref, qstart_ref, q_ref, page_ref, o_ref, st_ref, m_sc, l_sc, acc_sc):
-        i = pl.program_id(0)
-        n = pl.num_programs(0)
-        req = sreq_ref[i]
-        prev = sreq_ref[jnp.maximum(i - 1, 0)]
-        nxt = sreq_ref[jnp.minimum(i + 1, n - 1)]
-        first = jnp.logical_or(i == 0, prev != req)
-        last = jnp.logical_or(i == n - 1, nxt != req)
-
-        @pl.when(first)
-        def _():
+        j = pl.program_id(0)
+        a = 2 * j
+        b = a + 1
+        req_a = sreq_ref[a]
+        req_b = sreq_ref[b]
+        first_a = jnp.logical_or(a == 0, sreq_ref[jnp.maximum(a - 1, 0)] != req_a)
+        last_b = jnp.logical_or(b == slots - 1, sreq_ref[jnp.minimum(b + 1, slots - 1)] != req_b)
+        same = req_a == req_b
+        kst_a = kstart_ref[a]
+        kst_b = kstart_ref[b]
+        page_a = page_ref[perm_ref[a]]
+        page_b = page_ref[perm_ref[b]]
+
+        def init():
             m_sc[...] = jnp.full(m_sc.shape, NEG_BIG, jnp.float32)
             l_sc[...] = jnp.zeros(l_sc.shape, jnp.float32)
             acc_sc[...] = jnp.zeros(acc_sc.shape, jnp.float32)
 
-        kst = kstart_ref[i]
-        qst = qstart_ref[req]
-        page = page_ref[perm_ref[i]]
-        keys = page[:, :HD]
-        vals = page[:, HD:]
-        q = q_ref[req]
-
-        def update(masked):
-            s = jnp.dot(keys, q, preferred_element_type=jnp.float32)
-            if masked:
-                key_pos = lax.broadcasted_iota(jnp.int32, (page_rows, width), 0) + kst
-                token = jnp.bitwise_and(lax.broadcasted_iota(jnp.int32, (page_rows, width), 1), sub - 1)
-                vis = key_pos <= token + qst
-                s = jnp.where(vis, s, NEG_BIG)
-            m_prev = m_sc[...]
-            m_next = jnp.maximum(m_prev, jnp.max(s, axis=0, keepdims=True))
-            alpha = jnp.exp(m_prev - m_next)
-            p = jnp.exp(s - m_next)
-            if masked:
-                p = jnp.where(vis, p, 0.0)
-            l_sc[...] = alpha * l_sc[...] + jnp.sum(p, axis=0, keepdims=True)
-            m_sc[...] = m_next
-            pv = lax.dot_general(
-                vals, p.astype(jnp.bfloat16), (((0,), (0,)), ((), ())),
-                preferred_element_type=jnp.float32,
-            )
-            acc_sc[...] = acc_sc[...] * alpha + pv
-
-        partial = kst + (page_rows - 1) > qst
-
-        @pl.when(partial)
-        def _():
-            update(True)
-
-        @pl.when(jnp.logical_not(partial))
-        def _():
-            update(False)
-
-        @pl.when(last)
-        def _():
+        def finish(req):
             l_all = l_sc[...]
             safe = jnp.where(l_all > 0.0, l_all, 1.0)
             o_ref[req] = (acc_sc[...] / safe).astype(o_ref.dtype)
             st_ref[req, 0:1, :] = m_sc[...]
             st_ref[req, 1:2, :] = l_all
 
+        def update(items, req, masked):
+            q = q_ref[req]
+            qst = qstart_ref[req]
+            if masked:
+                token = jnp.bitwise_and(lax.broadcasted_iota(jnp.int32, (page_rows, width), 1), sub - 1) + qst
+                row = lax.broadcasted_iota(jnp.int32, (page_rows, width), 0)
+            scores = []
+            for page, kst in items:
+                sc = jnp.dot(page[:, :HD], q, preferred_element_type=jnp.float32)
+                vis = None
+                if masked:
+                    vis = row + kst <= token
+                    sc = jnp.where(vis, sc, NEG_BIG)
+                scores.append((sc, vis))
+            m_prev = m_sc[...]
+            m_cur = jnp.max(scores[0][0], axis=0, keepdims=True)
+            for sc, vis in scores[1:]:
+                m_cur = jnp.maximum(m_cur, jnp.max(sc, axis=0, keepdims=True))
+            m_next = jnp.maximum(m_prev, m_cur)
+            alpha = jnp.exp(m_prev - m_next)
+            l_add = None
+            pv = None
+            for (sc, vis), (page, kst) in zip(scores, items):
+                p = jnp.exp(sc - m_next)
+                if masked:
+                    p = jnp.where(vis, p, 0.0)
+                part_l = jnp.sum(p, axis=0, keepdims=True)
+                part_pv = lax.dot_general(
+                    page[:, HD:], p.astype(jnp.bfloat16), (((0,), (0,)), ((), ())),
+                    preferred_element_type=jnp.float32,
+                )
+                l_add = part_l if l_add is None else l_add + part_l
+                pv = part_pv if pv is None else pv + part_pv
+            l_sc[...] = alpha * l_sc[...] + l_add
+            m_sc[...] = m_next
+            acc_sc[...] = acc_sc[...] * alpha + pv
+
+        partial_a = kst_a + (page_rows - 1) > qstart_ref[req_a]
+        partial_b = kst_b + (page_rows - 1) > qstart_ref[req_b]
+        pair = [(page_a, kst_a), (page_b, kst_b)]
+
+        @pl.when(first_a)
+        def _():
+            init()
+
+        @pl.when(jnp.logical_and(same, jnp.logical_or(partial_a, partial_b)))
+        def _():
+            update(pair, req_a, True)
+
+        @pl.when(jnp.logical_and(same, jnp.logical_not(jnp.logical_or(partial_a, partial_b))))
+        def _():
+            update(pair, req_a, False)
+
+        @pl.when(jnp.logical_not(same))
+        def _():
+            update(pair[:1], req_a, True)
+            finish(req_a)
+            init()
+            update(pair[1:], req_b, True)
+
+        @pl.when(last_b)
+        def _():
+            finish(req_b)
+
     grid_spec = pltpu.PrefetchScalarGridSpec(
         num_scalar_prefetch=4,
-        grid=(slots,),
+        grid=(slots // 2,),
         in_specs=[
             pl.BlockSpec((reqs, HD, width), lambda i, sr, pm, ks, qs: (0, 0, 0)),
             pl.BlockSpec((slots, page_rows, 2 * HD), lambda i, sr, pm, ks, qs: (0, 0, 0)),

time: 296 us -> 282 us (0.953)
  Pallas kernels: 68.4 us -> 54.6 us
    pallas_call x2, Pallas kernels: 68.4 us -> 54.6 us  [slot_attention(): pl.pallas_call(kernel, grid_spec=grid_spec, out_shape=[jax.ShapeDtypeStru...]
    all_gather x2, waiting for transfers between devices: 45.7 us -> 52 us  [body(): gathered.append(lax.all_gather(piece[None], 'req', axis=0, tiled=True))]
    all_to_all x2, waiting for transfers between devices: 24.7 us -> 18.4 us  [body(): got = lax.all_to_all(sent, 'req', 0, 0, tiled=True)]
  transfers between devices with their start and end apart: 6 -> 6, of which waited for: 3 -> 4; matrix products, arithmetic and copies ran while one was open for 12% -> 12% of each run, Pallas kernels for 23% -> 19%
where the time goes in v12:
time: 282 us; the launch traced here: 280 us
  waiting for transfers between devices  106 us (38%)
  Pallas kernels  54.6 us (19%)
  blocking collectives  31.4 us (11%)
  local copies, waits for them, and re-layouts  29.4 us (10%)
  other arithmetic  20.5 us (7%)
  starting transfers between devices  20.1 us (7%)
  between operations  14.2 us (5%)
  matrix products  3.62 us (1%)
    pallas_call x2, Pallas kernels, slot_attention(): pl.pallas_call(kernel, grid_spec=grid_spec, out_shape=[jax.ShapeDtypeStru...  54.6 us
    all_gather x2, waiting for transfers between devices, body(): gathered.append(lax.all_gather(piece[None], 'req', axis=0, tiled=True))  52 us
    all_to_all x1, waiting for transfers between devices, body(): lax.all_to_all(jnp.broadcast_to(both[None], (n_req,) + both.shape), 'req'...  35.2 us
    all_to_all x1, blocking collectives, body(): got_t = lax.all_to_all(partial_t, 'tp', 0, 0, tiled=True)  31.4 us
    all_to_all x2, waiting for transfers between devices, body(): got = lax.all_to_all(sent, 'req', 0, 0, tiled=True)  18.4 us
    all_to_all x2, starting transfers between devices, body(): got = lax.all_to_all(sent, 'req', 0, 0, tiled=True)  11.8 us
    all_to_all x1, starting transfers between devices, body(): lax.all_to_all(jnp.broadcast_to(both[None], (n_req,) + both.shape), 'req'...  8.17 us
  transfers between devices with their start and end apart: 6, of which 4 were waited for; matrix products, arithmetic and copies ran while one was open for 12% of the time, Pallas kernels for 19%

profile of v12, /device:TPU:0, one launch (start us, length us, event | category | flops | bytes accessed | tf_op | source)
XLA Modules:
  0.0 280.3 jit_solution(16718047630692061107)
XLA Ops:
  9.9 1.8 broadcast_in_dim.142
  11.8 8.2 %all-to-all-start = ((bf16[16,640,128]{1,2,0:T(8,128)(2,1)}), bf16[16,640,128]{1,2,0:T(8,128)(2,1)}, u32[]{:S(2)}, u32[]{:S(2)}) async-start(bf16[16,640,128]{1,2,0:T(8,128)(2,1)} %broadcast_in_dim.142), calls=%async_computation | async-start | bytes 5242880 | tf_op jit(solution)/shard_map/all_to_all | solution.py:198
  21.9 35.2 %all-to-all-done = bf16[16,640,128]{1,2,0:T(8,128)(2,1)} async-done(((bf16[16,640,128]{1,2,0:T(8,128)(2,1)}), bf16[16,640,128]{1,2,0:T(8,128)(2,1)}, u32[]{:S(2)}, u32[]{:S(2)}) %all-to-all-start) | async-done | bytes 2621472 | tf_op jit(solution)/shard_map/all_to_all | solution.py:198
  60.5 2.6 fusion.17
  65.8 2.0 sort.17
  69.5 45.6 %all-gather.9.cloned.1.call-done = bf16[2048,1024]{1,0:T(8,128)(2,1)} async-done(((bf16[128,1024]{1,0:T(8,128)(2,1)}), bf16[2048,1024]{1,0:T(8,128)(2,1)}) %all-gather.9.cloned.1.call-update) | async-done | bytes 4194320 | tf_op jit(solution)/shard_map/all_gather | solution.py:229
  115.2 1.8 slice.108
  117.0 2.3 reshape_reshape.3
  119.3 2.5 gather_fusion.2
  121.8 1.9 broadcast_select_fusion.page_ref
  123.7 27.6 %shard_map.77 = (bf16[16,64,1024]{2,1,0:T(8,128)(2,1)S(1)}, f32[16,2,1024]{2,1,0:T(2,128)S(1)}) custom-call(s32[64]{0:T(128)S(1)} %gather_fusion, s32[64]{0:T(128)S(1)} %get-tuple-element.7.perm_ref, s32[64]{0:T(128)S(1)} %broadcast_multiply_fusion.1.kstart_ref, s32[16]{0:T(128)S(1)} %get-tuple-element.42.qstart_ref, bf16[16,128,1024]{2,1,0:T(8,128)(2,1)} %bitcast.82, ...), custom_call_target="tpu_custom_call" | custom-call | tf_op jit(solution)/shard_map/pallas_call | solution.py:177
  151.5 1.9 pad_maximum_fusion
  153.4 5.7 %all-to-all-start.1 = ((bf16[16,70,1024]{2,1,0:T(8,128)(2,1)}), bf16[16,70,1024]{2,1,0:T(8,128)(2,1)}, u32[]{:S(2)}, u32[]{:S(2)}) async-start(bf16[16,70,1024]{2,1,0:T(8,128)(2,1)} %pad_maximum_fusion), calls=%async_computation.1 | async-start | bytes 4718592 | tf_op jit(solution)/shard_map/all_to_all | solution.py:254
  159.1 6.4 %all-gather.7.cloned.1.call-done.q_ref = bf16[16,64,1024]{2,1,0:T(8,128)(2,1)} async-done(((bf16[1,64,1024]{2,1,0:T(8,128)(2,1)}), bf16[16,64,1024]{2,1,0:T(8,128)(2,1)}) %all-gather.7.cloned.1.call-update) | async-done | bytes 2097168 | tf_op jit(solution)/shard_map/all_gather | solution.py:229
  167.1 27.0 %shard_map.78 = (bf16[16,64,1024]{2,1,0:T(8,128)(2,1)S(1)}, f32[16,2,1024]{2,1,0:T(2,128)S(1)}) custom-call(s32[64]{0:T(128)S(1)} %gather_fusion, s32[64]{0:T(128)S(1)} %get-tuple-element.7.perm_ref, s32[64]{0:T(128)S(1)} %broadcast_multiply_fusion.1.kstart_ref, s32[16]{0:T(128)S(1)} %get-tuple-element.40.qstart_ref, bf16[16,64,1024]{2,1,0:T(8,128)(2,1)S(1)} %copy-done.1, ...), custom_call_target="tpu_custom_call" | custom-call | tf_op jit(solution)/shard_map/pallas_call | solution.py:177
  194.3 1.9 pad_maximum_fusion.1
  196.2 6.1 %all-to-all-start.2 = ((bf16[16,70,1024]{2,1,0:T(8,128)(2,1)}), bf16[16,70,1024]{2,1,0:T(8,128)(2,1)S(1)}, u32[]{:S(2)}, u32[]{:S(2)}) async-start(bf16[16,70,1024]{2,1,0:T(8,128)(2,1)} %pad_maximum_fusion.1), calls=%async_computation.2 | async-start | bytes 4718592 | tf_op jit(solution)/shard_map/all_to_all | solution.py:254
  204.5 1.8 slice_convert_fusion.1
  206.3 2.0 reshape.271
  208.2 1.7 fusion.16
  210.0 18.4 %all-to-all-done.2 = bf16[16,70,1024]{2,1,0:T(8,128)(2,1)S(1)} async-done(((bf16[16,70,1024]{2,1,0:T(8,128)(2,1)}), bf16[16,70,1024]{2,1,0:T(8,128)(2,1)S(1)}, u32[]{:S(2)}, u32[]{:S(2)}) %all-to-all-start.2) | async-done | bytes 2293792 | tf_op jit(solution)/shard_map/all_to_all | solution.py:254
  229.2 2.0 reshape.272
  233.9 3.7 %multiply_reduce_fusion.1 = (f32[64,1024]{1,0:T(8,128)}, f32[64,1024]{1,0:T(8,128)}) fusion(bf16[16,70,1024]{2,1,0:T(8,128)(2,1)} %all-to-all-done.1, f32[16,1024]{1,0:T(8,128)S(1)} %bitcast.93, pred[16]{0:T(512)(128)(4,1)S(1)} %reduce_or.9, f32[16,1024]{1,0:T(8,128)S(1)} %bitcast.92, bf16[16,70,1024]{2,1,0:T(8,128)(2,1)S(1)} %all-to-all-done.2), kind=kLoop, calls=%fused_computation.4 | loop fusion | flops 8257536 | bytes 4849680 | tf_op jit(solution)/shard_map/reduce_sum | solution.py:265
  241.3 31.4 %all_to_all.20 = bf16[8,512,256]{2,1,0:T(8,128)(2,1)S(1)} all-to-all(bf16[8,512,256]{2,1,0:T(8,128)(2,1)S(1)} %bitcast.86), channel_id=1, replica_groups=mesh['req'=16,'tp'=8] {'tp'}, dimensions={0} | all-to-all | bytes 4194304 | tf_op jit(solution)/shard_map/all_to_all | solution.py:274
  (88 shorter events, 24.3 us)
Async XLA Ops:
  7.2 53.3 %all-gather.5.cloned.1.call-start = ((), (), s32[]{:S(2)}) async-start(), calls=%async_computation.4 | async-start | bytes 2359296 | tf_op jit(solution)/shard_map/all_gather | solution.py:192
  11.8 8.2 %copy-start.3 = (s32[16]{0:T(128)S(1)}, s32[16]{0:T(128)}, u32[]{:S(2)}) copy-start(s32[16]{0:T(128)} %param.10) | copy-start | bytes 196
  11.8 45.3 %all-to-all-start = ((bf16[16,640,128]{1,2,0:T(8,128)(2,1)}), bf16[16,640,128]{1,2,0:T(8,128)(2,1)}, u32[]{:S(2)}, u32[]{:S(2)}) async-start(bf16[16,640,128]{1,2,0:T(8,128)(2,1)} %broadcast_in_dim.142), calls=%async_computation | async-start | bytes 5242880 | tf_op jit(solution)/shard_map/all_to_all | solution.py:198
  20.0 95.2 %all-gather.9.cloned.1.call-start = ((), (), s32[]{:S(2)}) async-start(), calls=%async_computation.6 | async-start | bytes 4456448 | tf_op jit(solution)/shard_map/all_gather | solution.py:229
  60.4 2.8 %copy-start.4 = (f32[5]{0:T(128)S(1)}, f32[5]{0:T(128)}, u32[]{:S(2)}) copy-start(f32[5]{0:T(128)} %constant.16.clone.1) | copy-start | bytes 64
  63.1 1.5 copy-start.2
  64.6 100.9 %all-gather.7.cloned.1.call-start = ((), (), s32[]{:S(2)}) async-start(), calls=%async_computation.5 | async-start | bytes 2228224 | tf_op jit(solution)/shard_map/all_gather | solution.py:229
  123.7 27.6 %copy-start = (bf16[64,128,128]{2,1,0:T(8,128)(2,1)}, bf16[64,128,128]{2,1,0:T(8,128)(2,1)S(1)}, u32[]{:S(2)}) copy-start(bf16[64,128,128]{2,1,0:T(8,128)(2,1)S(1)} %broadcast_select_fusion.page_ref) | copy-start | bytes 6291460
  153.4 42.8 %all-to-all-start.1 = ((bf16[16,70,1024]{2,1,0:T(8,128)(2,1)}), bf16[16,70,1024]{2,1,0:T(8,128)(2,1)}, u32[]{:S(2)}, u32[]{:S(2)}) async-start(bf16[16,70,1024]{2,1,0:T(8,128)(2,1)} %pad_maximum_fusion), calls=%async_computation.1 | async-start | bytes 4718592 | tf_op jit(solution)/shard_map/all_to_all | solution.py:254
  165.5 1.6 copy-start.1
  196.2 32.2 %all-to-all-start.2 = ((bf16[16,70,1024]{2,1,0:T(8,128)(2,1)}), bf16[16,70,1024]{2,1,0:T(8,128)(2,1)S(1)}, u32[]{:S(2)}, u32[]{:S(2)}) async-start(bf16[16,70,1024]{2,1,0:T(8,128)(2,1)} %pad_maximum_fusion.1), calls=%async_computation.2 | async-start | bytes 4718592 | tf_op jit(solution)/shard_map/all_to_all | solution.py:254
Sparse Core Ops, SparseCore 0:
  9.7 29.2 all-gather.4
  64.7 50.4 all-gather.8
  117.3 48.1 all-gather.6

commit v13 on v12

--- a/solution.py
+++ b/solution.py
@@ -226,7 +226,11 @@
         piece = jnp.transpose(rotated[h * sub:(h + 1) * sub, :GROUP, :], (2, 1, 0)).reshape(HD, width)
         if h == 0:
             piece = jnp.concatenate([piece, fresh.reshape(-1, width)], axis=0)
-        gathered.append(lax.all_gather(piece[None], "req", axis=0, tiled=True))
+        if h == 0:
+            gathered.append(lax.all_gather(piece[None], "req", axis=0, tiled=True))
+        else:
+            copies = jnp.broadcast_to(piece[None], (n_req,) + piece.shape)
+            gathered.append(lax.all_to_all(copies, "req", 0, 0, tiled=True))
     fresh_all = gathered[0][:, HD:, :].reshape(requests, SPAN, 2 * HD)
 
     my_slots = my_index * local_slots + jnp.arange(local_slots, dtype=jnp.int32)

time: 282 us -> 299 us (1.060)
  waiting for transfers between devices: 106 us -> 121 us
    all_to_all x2, waiting for transfers between devices: 18.4 us -> 27.9 us  [body(): got = lax.all_to_all(sent, 'req', 0, 0, tiled=True)]
    all_gather x2 -> x1, waiting for transfers between devices: 52 us -> 57.5 us  [body(): gathered.append(lax.all_gather(piece[None], 'req', axis=0, tiled=True))]
    all_to_all x0 -> x1, starting transfers between devices: none -> 4.49 us  [body(): gathered.append(lax.all_to_all(copies, 'req', 0, 0, tiled=True))]
where the time goes in v13:
time: 299 us; the launch traced here: 297 us
  waiting for transfers between devices  121 us (40%)
  Pallas kernels  55.7 us (19%)
  blocking collectives  31.2 us (10%)
  local copies, waits for them, and re-layouts  28.6 us (10%)
  starting transfers between devices  21.9 us (7%)
  other arithmetic  20.5 us (7%)
  between operations  14.5 us (5%)
  matrix products  3.62 us (1%)
    all_gather x1, waiting for transfers between devices, body(): gathered.append(lax.all_gather(piece[None], 'req', axis=0, tiled=True))  57.5 us
    pallas_call x2, Pallas kernels, slot_attention(): pl.pallas_call(kernel, grid_spec=grid_spec, out_shape=[jax.ShapeDtypeStru...  55.7 us
    all_to_all x1, waiting for transfers between devices, body(): lax.all_to_all(jnp.broadcast_to(both[None], (n_req,) + both.shape), 'req'...  35.2 us
    all_to_all x1, blocking collectives, body(): got_t = lax.all_to_all(partial_t, 'tp', 0, 0, tiled=True)  31.2 us
    all_to_all x2, waiting for transfers between devices, body(): got = lax.all_to_all(sent, 'req', 0, 0, tiled=True)  27.9 us
    all_to_all x2, starting transfers between devices, body(): got = lax.all_to_all(sent, 'req', 0, 0, tiled=True)  9.16 us
    all_to_all x1, starting transfers between devices, body(): lax.all_to_all(jnp.broadcast_to(both[None], (n_req,) + both.shape), 'req'...  8.17 us
  transfers between devices with their start and end apart: 6, of which 4 were waited for; matrix products, arithmetic and copies ran while one was open for 12% of the time, Pallas kernels for 19%

profile of v13, /device:TPU:0, one launch (start us, length us, event | category | flops | bytes accessed | tf_op | source)
XLA Modules:
  0.0 297.4 jit_solution(2933932174764560081)
XLA Ops:
  9.9 1.8 broadcast_in_dim.149
  11.8 8.2 %all-to-all-start = ((bf16[16,640,128]{1,2,0:T(8,128)(2,1)}), bf16[16,640,128]{1,2,0:T(8,128)(2,1)}, u32[]{:S(2)}, u32[]{:S(2)}) async-start(bf16[16,640,128]{1,2,0:T(8,128)(2,1)} %broadcast_in_dim.149), calls=%async_computation | async-start | bytes 5242880 | tf_op jit(solution)/shard_map/all_to_all | solution.py:198
  21.9 35.2 %all-to-all-done = bf16[16,640,128]{1,2,0:T(8,128)(2,1)} async-done(((bf16[16,640,128]{1,2,0:T(8,128)(2,1)}), bf16[16,640,128]{1,2,0:T(8,128)(2,1)}, u32[]{:S(2)}, u32[]{:S(2)}) %all-to-all-start) | async-done | bytes 2621472 | tf_op jit(solution)/shard_map/all_to_all | solution.py:198
  60.5 2.6 fusion.17
  64.9 2.0 sort.17
  68.6 4.5 %all-to-all-start.2 = ((bf16[16,64,1024]{2,1,0:T(8,128)(2,1)}), bf16[16,64,1024]{2,1,0:T(8,128)(2,1)}, u32[]{:S(2)}, u32[]{:S(2)}) async-start(bf16[16,64,1024]{2,1,0:T(8,128)(2,1)} %broadcast_in_dim.161), calls=%async_computation.2 | async-start | bytes 4194304 | tf_op jit(solution)/shard_map/all_to_all | solution.py:233
  74.8 57.5 %all-gather.6.cloned.1.call-done = bf16[2048,1024]{1,0:T(8,128)(2,1)} async-done(((bf16[128,1024]{1,0:T(8,128)(2,1)}), bf16[2048,1024]{1,0:T(8,128)(2,1)}) %all-gather.6.cloned.1.call-update) | async-done | bytes 4194320 | tf_op jit(solution)/shard_map/all_gather | solution.py:230
  132.3 1.8 slice.108
  134.1 2.3 reshape_reshape.3
  136.4 2.5 gather_fusion.2
  138.9 1.9 broadcast_select_fusion.page_ref
  140.8 27.7 %shard_map.77 = (bf16[16,64,1024]{2,1,0:T(8,128)(2,1)S(1)}, f32[16,2,1024]{2,1,0:T(2,128)S(1)}) custom-call(s32[64]{0:T(128)S(1)} %gather_fusion, s32[64]{0:T(128)S(1)} %get-tuple-element.7.perm_ref, s32[64]{0:T(128)S(1)} %broadcast_multiply_fusion.1.kstart_ref, s32[16]{0:T(128)S(1)} %get-tuple-element.42.qstart_ref, bf16[16,128,1024]{2,1,0:T(8,128)(2,1)} %bitcast.84, ...), custom_call_target="tpu_custom_call" | custom-call | tf_op jit(solution)/shard_map/pallas_call | solution.py:177
  168.7 1.9 pad_maximum_fusion
  170.6 5.3 %all-to-all-start.1 = ((bf16[16,70,1024]{2,1,0:T(8,128)(2,1)}), bf16[16,70,1024]{2,1,0:T(8,128)(2,1)}, u32[]{:S(2)}, u32[]{:S(2)}) async-start(bf16[16,70,1024]{2,1,0:T(8,128)(2,1)} %pad_maximum_fusion), calls=%async_computation.1 | async-start | bytes 4718592 | tf_op jit(solution)/shard_map/all_to_all | solution.py:258
  175.9 28.0 %shard_map.78 = (bf16[16,64,1024]{2,1,0:T(8,128)(2,1)S(1)}, f32[16,2,1024]{2,1,0:T(2,128)S(1)}) custom-call(s32[64]{0:T(128)S(1)} %gather_fusion, s32[64]{0:T(128)S(1)} %get-tuple-element.7.perm_ref, s32[64]{0:T(128)S(1)} %broadcast_multiply_fusion.1.kstart_ref, s32[16]{0:T(128)S(1)} %get-tuple-element.40.qstart_ref, ...), custom_call_target="tpu_custom_call" | custom-call | tf_op jit(solution)/shard_map/pallas_call | solution.py:177
  204.0 1.9 pad_maximum_fusion.1
  205.9 3.5 %all-to-all-done.1 = bf16[16,70,1024]{2,1,0:T(8,128)(2,1)} async-done(((bf16[16,70,1024]{2,1,0:T(8,128)(2,1)}), bf16[16,70,1024]{2,1,0:T(8,128)(2,1)}, u32[]{:S(2)}, u32[]{:S(2)}) %all-to-all-start.1) | async-done | bytes 2293792 | tf_op jit(solution)/shard_map/all_to_all | solution.py:258
  209.5 3.9 %all-to-all-start.3 = ((bf16[16,70,1024]{2,1,0:T(8,128)(2,1)}), bf16[16,70,1024]{2,1,0:T(8,128)(2,1)S(1)}, u32[]{:S(2)}, u32[]{:S(2)}) async-start(bf16[16,70,1024]{2,1,0:T(8,128)(2,1)} %pad_maximum_fusion.1), calls=%async_computation.3 | async-start | bytes 4718592 | tf_op jit(solution)/shard_map/all_to_all | solution.py:258
  215.5 1.8 slice_convert_fusion.1
  217.3 2.0 reshape.272
  221.0 24.4 %all-to-all-done.3 = bf16[16,70,1024]{2,1,0:T(8,128)(2,1)S(1)} async-done(((bf16[16,70,1024]{2,1,0:T(8,128)(2,1)}), bf16[16,70,1024]{2,1,0:T(8,128)(2,1)S(1)}, u32[]{:S(2)}, u32[]{:S(2)}) %all-to-all-start.3) | async-done | bytes 2293792 | tf_op jit(solution)/shard_map/all_to_all | solution.py:258
  246.2 2.0 reshape.273
  250.9 3.7 %multiply_reduce_fusion.1 = (f32[64,1024]{1,0:T(8,128)}, f32[64,1024]{1,0:T(8,128)}) fusion(bf16[16,70,1024]{2,1,0:T(8,128)(2,1)} %all-to-all-done.1, f32[16,1024]{1,0:T(8,128)S(1)} %bitcast.96, pred[16]{0:T(512)(128)(4,1)S(1)} %reduce_or.9, f32[16,1024]{1,0:T(8,128)S(1)} %bitcast.95, bf16[16,70,1024]{2,1,0:T(8,128)(2,1)S(1)} %all-to-all-done.3), kind=kLoop, calls=%fused_computation.4 | loop fusion | flops 8257536 | bytes 4849680 | tf_op jit(solution)/shard_map/reduce_sum | solution.py:269
  258.3 31.2 %all_to_all.25 = bf16[8,512,256]{2,1,0:T(8,128)(2,1)S(1)} all-to-all(bf16[8,512,256]{2,1,0:T(8,128)(2,1)S(1)} %bitcast.88), channel_id=1, replica_groups=mesh['req'=16,'tp'=8] {'tp'}, dimensions={0} | all-to-all | bytes 4194304 | tf_op jit(solution)/shard_map/all_to_all | solution.py:278
  (85 shorter events, 25.2 us)
Async XLA Ops:
  7.2 53.3 %all-gather.4.cloned.1.call-start = ((), (), s32[]{:S(2)}) async-start(), calls=%async_computation.5 | async-start | bytes 2359296 | tf_op jit(solution)/shard_map/all_gather | solution.py:192
  11.8 8.2 %copy-start.2 = (s32[16]{0:T(128)S(1)}, s32[16]{0:T(128)}, u32[]{:S(2)}) copy-start(s32[16]{0:T(128)} %param.10) | copy-start | bytes 196
  11.8 45.3 %all-to-all-start = ((bf16[16,640,128]{1,2,0:T(8,128)(2,1)}), bf16[16,640,128]{1,2,0:T(8,128)(2,1)}, u32[]{:S(2)}, u32[]{:S(2)}) async-start(bf16[16,640,128]{1,2,0:T(8,128)(2,1)} %broadcast_in_dim.149), calls=%async_computation | async-start | bytes 5242880 | tf_op jit(solution)/shard_map/all_to_all | solution.py:198
  20.0 112.3 %all-gather.6.cloned.1.call-start = ((), (), s32[]{:S(2)}) async-start(), calls=%async_computation.6 | async-start | bytes 4456448 | tf_op jit(solution)/shard_map/all_gather | solution.py:230
  60.4 2.8 copy-start.3
  63.1 1.5 copy-start.1
  68.6 102.1 %all-to-all-start.2 = ((bf16[16,64,1024]{2,1,0:T(8,128)(2,1)}), bf16[16,64,1024]{2,1,0:T(8,128)(2,1)}, u32[]{:S(2)}, u32[]{:S(2)}) async-start(bf16[16,64,1024]{2,1,0:T(8,128)(2,1)} %broadcast_in_dim.161), calls=%async_computation.2 | async-start | bytes 4194304 | tf_op jit(solution)/shard_map/all_to_all | solution.py:233
  140.8 27.8 %copy-start = (bf16[64,128,128]{2,1,0:T(8,128)(2,1)}, bf16[64,128,128]{2,1,0:T(8,128)(2,1)S(1)}, u32[]{:S(2)}) copy-start(bf16[64,128,128]{2,1,0:T(8,128)(2,1)S(1)} %broadcast_select_fusion.page_ref) | copy-start | bytes 6291460
  170.6 38.8 %all-to-all-start.1 = ((bf16[16,70,1024]{2,1,0:T(8,128)(2,1)}), bf16[16,70,1024]{2,1,0:T(8,128)(2,1)}, u32[]{:S(2)}, u32[]{:S(2)}) async-start(bf16[16,70,1024]{2,1,0:T(8,128)(2,1)} %pad_maximum_fusion), calls=%async_computation.1 | async-start | bytes 4718592 | tf_op jit(solution)/shard_map/all_to_all | solution.py:258
  209.5 35.9 %all-to-all-start.3 = ((bf16[16,70,1024]{2,1,0:T(8,128)(2,1)}), bf16[16,70,1024]{2,1,0:T(8,128)(2,1)S(1)}, u32[]{:S(2)}, u32[]{:S(2)}) async-start(bf16[16,70,1024]{2,1,0:T(8,128)(2,1)} %pad_maximum_fusion.1), calls=%async_computation.3 | async-start | bytes 4718592 | tf_op jit(solution)/shard_map/all_to_all | solution.py:258
Sparse Core Ops, SparseCore 0:
  9.7 29.2 all-gather.3
  64.7 67.5 all-gather.5

commit v14 on v12

--- a/solution.py
+++ b/solution.py
@@ -65,21 +65,10 @@
     slots, page_rows, _ = pages.shape
     assert width == GROUP * sub and sub & (sub - 1) == 0
 
-    assert slots % 2 == 0
+    assert slots % 4 == 0
 
     def kernel(sreq_ref, perm_ref, kstart_ref, qstart_ref, q_ref, page_ref, o_ref, st_ref, m_sc, l_sc, acc_sc):
         j = pl.program_id(0)
-        a = 2 * j
-        b = a + 1
-        req_a = sreq_ref[a]
-        req_b = sreq_ref[b]
-        first_a = jnp.logical_or(a == 0, sreq_ref[jnp.maximum(a - 1, 0)] != req_a)
-        last_b = jnp.logical_or(b == slots - 1, sreq_ref[jnp.minimum(b + 1, slots - 1)] != req_b)
-        same = req_a == req_b
-        kst_a = kstart_ref[a]
-        kst_b = kstart_ref[b]
-        page_a = page_ref[perm_ref[a]]
-        page_b = page_ref[perm_ref[b]]
 
         def init():
             m_sc[...] = jnp.full(m_sc.shape, NEG_BIG, jnp.float32)
@@ -130,36 +119,84 @@
             m_sc[...] = m_next
             acc_sc[...] = acc_sc[...] * alpha + pv
 
-        partial_a = kst_a + (page_rows - 1) > qstart_ref[req_a]
-        partial_b = kst_b + (page_rows - 1) > qstart_ref[req_b]
-        pair = [(page_a, kst_a), (page_b, kst_b)]
-
-        @pl.when(first_a)
+        def item(k):
+            return (page_ref[perm_ref[k]], kstart_ref[k])
+
+        def partial_of(k):
+            return kstart_ref[k] + (page_rows - 1) > qstart_ref[sreq_ref[k]]
+
+        def is_first(k):
+            return jnp.logical_or(k == 0, sreq_ref[jnp.maximum(k - 1, 0)] != sreq_ref[k])
+
+        def is_last(k):
+            return jnp.logical_or(k == slots - 1, sreq_ref[jnp.minimum(k + 1, slots - 1)] != sreq_ref[k])
+
+        def pair_step(a):
+            b = a + 1
+            req_a = sreq_ref[a]
+            req_b = sreq_ref[b]
+            same = req_a == req_b
+            pair = [item(a), item(b)]
+            masked = jnp.logical_or(partial_of(a), partial_of(b))
+
+            @pl.when(is_first(a))
+            def _():
+                init()
+
+            @pl.when(jnp.logical_and(same, masked))
+            def _():
+                update(pair, req_a, True)
+
+            @pl.when(jnp.logical_and(same, jnp.logical_not(masked)))
+            def _():
+                update(pair, req_a, False)
+
+            @pl.when(jnp.logical_not(same))
+            def _():
+                update(pair[:1], req_a, True)
+                finish(req_a)
+                init()
+                update(pair[1:], req_b, True)
+
+            @pl.when(is_last(b))
+            def _():
+                finish(req_b)
+
+        a = 4 * j
+        req = sreq_ref[a]
+        whole = req == sreq_ref[a + 3]
+        quad_masked = partial_of(a)
+        for k in range(1, 4):
+            quad_masked = jnp.logical_or(quad_masked, partial_of(a + k))
+
+        @pl.when(whole)
         def _():
-            init()
-
-        @pl.when(jnp.logical_and(same, jnp.logical_or(partial_a, partial_b)))
+            quad = [item(a + k) for k in range(4)]
+
+            @pl.when(is_first(a))
+            def _():
+                init()
+
+            @pl.when(quad_masked)
+            def _():
+                update(quad, req, True)
+
+            @pl.when(jnp.logical_not(quad_masked))
+            def _():
+                update(quad, req, False)
+
+            @pl.when(is_last(a + 3))
+            def _():
+                finish(req)
+
+        @pl.when(jnp.logical_not(whole))
         def _():
-            update(pair, req_a, True)
-
-        @pl.when(jnp.logical_and(same, jnp.logical_not(jnp.logical_or(partial_a, partial_b))))
-        def _():
-            update(pair, req_a, False)
-
-        @pl.when(jnp.logical_not(same))
-        def _():
-            update(pair[:1], req_a, True)
-            finish(req_a)
-            init()
-            update(pair[1:], req_b, True)
-
-        @pl.when(last_b)
-        def _():
-            finish(req_b)
+            pair_step(a)
+            pair_step(a + 2)
 
     grid_spec = pltpu.PrefetchScalarGridSpec(
         num_scalar_prefetch=4,
-        grid=(slots // 2,),
+        grid=(slots // 4,),
         in_specs=[
             pl.BlockSpec((reqs, HD, width), lambda i, sr, pm, ks, qs: (0, 0, 0)),
             pl.BlockSpec((slots, page_rows, 2 * HD), lambda i, sr, pm, ks, qs: (0, 0, 0)),

time: 282 us -> 283 us (level)
  starting transfers between devices: 20.1 us -> 27.3 us
  Pallas kernels: 54.6 us -> 48.8 us
    all_to_all x2, starting transfers between devices: 11.8 us -> 18.8 us  [body(): got = lax.all_to_all(sent, 'req', 0, 0, tiled=True)]
    pallas_call x2, Pallas kernels: 54.6 us -> 48.8 us  [slot_attention(): pl.pallas_call(kernel, grid_spec=grid_spec, out_shape=[jax.ShapeDtypeStru...]
    all_gather x2, waiting for transfers between devices: 52 us -> 57.8 us  [body(): gathered.append(lax.all_gather(piece[None], 'req', axis=0, tiled=True))]
    all_to_all x2, waiting for transfers between devices: 18.4 us -> 13.1 us  [body(): got = lax.all_to_all(sent, 'req', 0, 0, tiled=True)]
  transfers between devices with their start and end apart: 6 -> 6, of which waited for: 4 -> 4; matrix products, arithmetic and copies ran while one was open for 12% -> 12% of each run, Pallas kernels for 19% -> 17%
where the time goes in v14:
time: 283 us; the launch traced here: 282 us
  waiting for transfers between devices  107 us (38%)
  Pallas kernels  48.8 us (17%)
  blocking collectives  31.3 us (11%)
  local copies, waits for them, and re-layouts  29.4 us (10%)
  starting transfers between devices  27.3 us (10%)
  other arithmetic  20.5 us (7%)
  between operations  14.2 us (5%)
  matrix products  3.62 us (1%)
    all_gather x2, waiting for transfers between devices, body(): gathered.append(lax.all_gather(piece[None], 'req', axis=0, tiled=True))  57.8 us
    pallas_call x2, Pallas kernels, slot_attention(): pl.pallas_call(kernel, grid_spec=grid_spec, out_shape=[jax.ShapeDtypeStru...  48.8 us
    all_to_all x1, waiting for transfers between devices, body(): lax.all_to_all(jnp.broadcast_to(both[None], (n_req,) + both.shape), 'req'...  35.2 us
    all_to_all x1, blocking collectives, body(): got_t = lax.all_to_all(partial_t, 'tp', 0, 0, tiled=True)  31.3 us
    all_to_all x2, starting transfers between devices, body(): got = lax.all_to_all(sent, 'req', 0, 0, tiled=True)  18.8 us
    all_to_all x2, waiting for transfers between devices, body(): got = lax.all_to_all(sent, 'req', 0, 0, tiled=True)  13.1 us
    all_to_all x1, starting transfers between devices, body(): lax.all_to_all(jnp.broadcast_to(both[None], (n_req,) + both.shape), 'req'...  8.17 us
  transfers between devices with their start and end apart: 6, of which 4 were waited for; matrix products, arithmetic and copies ran while one was open for 12% of the time, Pallas kernels for 17%

profile of v14, /device:TPU:0, one launch (start us, length us, event | category | flops | bytes accessed | tf_op | source)
XLA Modules:
  0.0 282.0 jit_solution(9912982764414549122)
XLA Ops:
  9.9 1.8 broadcast_in_dim.142
  11.8 8.2 %all-to-all-start = ((bf16[16,640,128]{1,2,0:T(8,128)(2,1)}), bf16[16,640,128]{1,2,0:T(8,128)(2,1)}, u32[]{:S(2)}, u32[]{:S(2)}) async-start(bf16[16,640,128]{1,2,0:T(8,128)(2,1)} %broadcast_in_dim.142), calls=%async_computation | async-start | bytes 5242880 | tf_op jit(solution)/shard_map/all_to_all | solution.py:235
  21.9 35.2 %all-to-all-done = bf16[16,640,128]{1,2,0:T(8,128)(2,1)} async-done(((bf16[16,640,128]{1,2,0:T(8,128)(2,1)}), bf16[16,640,128]{1,2,0:T(8,128)(2,1)}, u32[]{:S(2)}, u32[]{:S(2)}) %all-to-all-start) | async-done | bytes 2621472 | tf_op jit(solution)/shard_map/all_to_all | solution.py:235
  60.5 2.6 fusion.17
  66.0 2.0 sort.17
  69.7 45.4 %all-gather.9.cloned.1.call-done = bf16[2048,1024]{1,0:T(8,128)(2,1)} async-done(((bf16[128,1024]{1,0:T(8,128)(2,1)}), bf16[2048,1024]{1,0:T(8,128)(2,1)}) %all-gather.9.cloned.1.call-update) | async-done | bytes 4194320 | tf_op jit(solution)/shard_map/all_gather | solution.py:266
  115.2 1.8 slice.108
  117.0 2.3 reshape_reshape.3
  119.3 2.5 gather_fusion.2
  121.8 1.9 broadcast_select_fusion.page_ref
  123.7 24.5 %shard_map.77 = (bf16[16,64,1024]{2,1,0:T(8,128)(2,1)S(1)}, f32[16,2,1024]{2,1,0:T(2,128)S(1)}) custom-call(s32[64]{0:T(128)S(1)} %gather_fusion, s32[64]{0:T(128)S(1)} %get-tuple-element.7.perm_ref, s32[64]{0:T(128)S(1)} %broadcast_multiply_fusion.1.kstart_ref, s32[16]{0:T(128)S(1)} %get-tuple-element.42.qstart_ref, bf16[16,128,1024]{2,1,0:T(8,128)(2,1)} %bitcast.82, ...), custom_call_target="tpu_custom_call" | custom-call | tf_op jit(solution)/shard_map/pallas_call | solution.py:214
  148.4 1.9 pad_maximum_fusion
  150.3 6.0 %all-to-all-start.1 = ((bf16[16,70,1024]{2,1,0:T(8,128)(2,1)}), bf16[16,70,1024]{2,1,0:T(8,128)(2,1)}, u32[]{:S(2)}, u32[]{:S(2)}) async-start(bf16[16,70,1024]{2,1,0:T(8,128)(2,1)} %pad_maximum_fusion), calls=%async_computation.1 | async-start | bytes 4718592 | tf_op jit(solution)/shard_map/all_to_all | solution.py:291
  156.3 12.4 %all-gather.7.cloned.1.call-done.q_ref = bf16[16,64,1024]{2,1,0:T(8,128)(2,1)} async-done(((bf16[1,64,1024]{2,1,0:T(8,128)(2,1)}), bf16[16,64,1024]{2,1,0:T(8,128)(2,1)}) %all-gather.7.cloned.1.call-update) | async-done | bytes 2097168 | tf_op jit(solution)/shard_map/all_gather | solution.py:266
  170.3 24.3 %shard_map.78 = (bf16[16,64,1024]{2,1,0:T(8,128)(2,1)S(1)}, f32[16,2,1024]{2,1,0:T(2,128)S(1)}) custom-call(s32[64]{0:T(128)S(1)} %gather_fusion, s32[64]{0:T(128)S(1)} %get-tuple-element.7.perm_ref, s32[64]{0:T(128)S(1)} %broadcast_multiply_fusion.1.kstart_ref, s32[16]{0:T(128)S(1)} %get-tuple-element.40.qstart_ref, bf16[16,64,1024]{2,1,0:T(8,128)(2,1)S(1)} %copy-done.1, ...), custom_call_target="tpu_custom_call" | custom-call | tf_op jit(solution)/shard_map/pallas_call | solution.py:214
  194.7 1.9 pad_maximum_fusion.1
  196.6 12.9 %all-to-all-start.2 = ((bf16[16,70,1024]{2,1,0:T(8,128)(2,1)}), bf16[16,70,1024]{2,1,0:T(8,128)(2,1)S(1)}, u32[]{:S(2)}, u32[]{:S(2)}) async-start(bf16[16,70,1024]{2,1,0:T(8,128)(2,1)} %pad_maximum_fusion.1), calls=%async_computation.2 | async-start | bytes 4718592 | tf_op jit(solution)/shard_map/all_to_all | solution.py:291
  211.6 1.8 slice_convert_fusion.1
  213.4 2.0 reshape.271
  215.4 1.7 fusion.16
  217.1 13.1 %all-to-all-done.2 = bf16[16,70,1024]{2,1,0:T(8,128)(2,1)S(1)} async-done(((bf16[16,70,1024]{2,1,0:T(8,128)(2,1)}), bf16[16,70,1024]{2,1,0:T(8,128)(2,1)S(1)}, u32[]{:S(2)}, u32[]{:S(2)}) %all-to-all-start.2) | async-done | bytes 2293792 | tf_op jit(solution)/shard_map/all_to_all | solution.py:291
  231.1 2.0 reshape.272
  235.7 3.7 %multiply_reduce_fusion.1 = (f32[64,1024]{1,0:T(8,128)}, f32[64,1024]{1,0:T(8,128)}) fusion(bf16[16,70,1024]{2,1,0:T(8,128)(2,1)} %all-to-all-done.1, f32[16,1024]{1,0:T(8,128)S(1)} %bitcast.93, pred[16]{0:T(512)(128)(4,1)S(1)} %reduce_or.9, f32[16,1024]{1,0:T(8,128)S(1)} %bitcast.92, bf16[16,70,1024]{2,1,0:T(8,128)(2,1)S(1)} %all-to-all-done.2), kind=kLoop, calls=%fused_computation.4 | loop fusion | flops 8257536 | bytes 4849680 | tf_op jit(solution)/shard_map/reduce_sum | solution.py:302
  243.1 31.3 %all_to_all.20 = bf16[8,512,256]{2,1,0:T(8,128)(2,1)S(1)} all-to-all(bf16[8,512,256]{2,1,0:T(8,128)(2,1)S(1)} %bitcast.86), channel_id=1, replica_groups=mesh['req'=16,'tp'=8] {'tp'}, dimensions={0} | all-to-all | bytes 4194304 | tf_op jit(solution)/shard_map/all_to_all | solution.py:311
  (88 shorter events, 24.5 us)
Async XLA Ops:
  7.2 53.3 %all-gather.5.cloned.1.call-start = ((), (), s32[]{:S(2)}) async-start(), calls=%async_computation.4 | async-start | bytes 2359296 | tf_op jit(solution)/shard_map/all_gather | solution.py:229
  11.8 8.2 %copy-start.3 = (s32[16]{0:T(128)S(1)}, s32[16]{0:T(128)}, u32[]{:S(2)}) copy-start(s32[16]{0:T(128)} %param.10) | copy-start | bytes 196
  11.8 45.3 %all-to-all-start = ((bf16[16,640,128]{1,2,0:T(8,128)(2,1)}), bf16[16,640,128]{1,2,0:T(8,128)(2,1)}, u32[]{:S(2)}, u32[]{:S(2)}) async-start(bf16[16,640,128]{1,2,0:T(8,128)(2,1)} %broadcast_in_dim.142), calls=%async_computation | async-start | bytes 5242880 | tf_op jit(solution)/shard_map/all_to_all | solution.py:235
  20.0 95.2 %all-gather.9.cloned.1.call-start = ((), (), s32[]{:S(2)}) async-start(), calls=%async_computation.6 | async-start | bytes 4456448 | tf_op jit(solution)/shard_map/all_gather | solution.py:266
  60.4 2.8 %copy-start.4 = (f32[5]{0:T(128)S(1)}, f32[5]{0:T(128)}, u32[]{:S(2)}) copy-start(f32[5]{0:T(128)} %constant.16.clone.1) | copy-start | bytes 64
  63.1 1.7 copy-start.2
  64.6 104.1 %all-gather.7.cloned.1.call-start = ((), (), s32[]{:S(2)}) async-start(), calls=%async_computation.5 | async-start | bytes 2228224 | tf_op jit(solution)/shard_map/all_gather | solution.py:266
  123.7 24.6 %copy-start = (bf16[64,128,128]{2,1,0:T(8,128)(2,1)}, bf16[64,128,128]{2,1,0:T(8,128)(2,1)S(1)}, u32[]{:S(2)}) copy-start(bf16[64,128,128]{2,1,0:T(8,128)(2,1)S(1)} %broadcast_select_fusion.page_ref) | copy-start | bytes 6291460
  150.3 46.3 %all-to-all-start.1 = ((bf16[16,70,1024]{2,1,0:T(8,128)(2,1)}), bf16[16,70,1024]{2,1,0:T(8,128)(2,1)}, u32[]{:S(2)}, u32[]{:S(2)}) async-start(bf16[16,70,1024]{2,1,0:T(8,128)(2,1)} %pad_maximum_fusion), calls=%async_computation.1 | async-start | bytes 4718592 | tf_op jit(solution)/shard_map/all_to_all | solution.py:291
  168.7 1.6 copy-start.1
  196.6 33.6 %all-to-all-start.2 = ((bf16[16,70,1024]{2,1,0:T(8,128)(2,1)}), bf16[16,70,1024]{2,1,0:T(8,128)(2,1)S(1)}, u32[]{:S(2)}, u32[]{:S(2)}) async-start(bf16[16,70,1024]{2,1,0:T(8,128)(2,1)} %pad_maximum_fusion.1), calls=%async_computation.2 | async-start | bytes 4718592 | tf_op jit(solution)/shard_map/all_to_all | solution.py:291
Sparse Core Ops, SparseCore 0:
  9.7 29.2 all-gather.4
  64.7 50.4 all-gather.8
  117.3 51.3 all-gather.6

commit v15 on v12

--- a/solution.py
+++ b/solution.py
@@ -60,7 +60,7 @@
     return jnp.where((page_index >= cached)[:, None, None], fresh_pages[pick], kv_pages)
 
 
-def slot_attention(sreq, perm, kstart, qstart, packed, pages, sub):
+def slot_attention(sreq, perm, kstart, qstart, packed, pages, sub, row_block=0):
     reqs, _, width = packed.shape
     slots, page_rows, _ = pages.shape
     assert width == GROUP * sub and sub & (sub - 1) == 0
@@ -161,7 +161,7 @@
         num_scalar_prefetch=4,
         grid=(slots // 2,),
         in_specs=[
-            pl.BlockSpec((reqs, HD, width), lambda i, sr, pm, ks, qs: (0, 0, 0)),
+            pl.BlockSpec((reqs, HD, width), lambda i, sr, pm, ks, qs: (0, row_block, 0)),
             pl.BlockSpec((slots, page_rows, 2 * HD), lambda i, sr, pm, ks, qs: (0, 0, 0)),
         ],
         out_specs=[
@@ -221,13 +221,13 @@
     halves = 2
     sub = SPAN // halves
     width = GROUP * sub
-    gathered = []
+    pieces = []
     for h in range(halves):
-        piece = jnp.transpose(rotated[h * sub:(h + 1) * sub, :GROUP, :], (2, 1, 0)).reshape(HD, width)
+        pieces.append(jnp.transpose(rotated[h * sub:(h + 1) * sub, :GROUP, :], (2, 1, 0)).reshape(HD, width))
         if h == 0:
-            piece = jnp.concatenate([piece, fresh.reshape(-1, width)], axis=0)
-        gathered.append(lax.all_gather(piece[None], "req", axis=0, tiled=True))
-    fresh_all = gathered[0][:, HD:, :].reshape(requests, SPAN, 2 * HD)
+            pieces.append(fresh.reshape(-1, width))
+    packed_all = lax.all_gather(jnp.concatenate(pieces, axis=0)[None], "req", axis=0, tiled=True)
+    fresh_all = packed_all[:, HD:2 * HD, :].reshape(requests, SPAN, 2 * HD)
 
     my_slots = my_index * local_slots + jnp.arange(local_slots, dtype=jnp.int32)
     slot_req, page_index, cached = locate(my_slots, cache_pages, slot_order, new_pages)
@@ -245,7 +245,9 @@
     outs = []
     for h in range(halves):
         q_start = (query_start + h * sub).astype(jnp.int32)
-        part_o, part_st = slot_attention(sreq, perm, kstart, q_start, gathered[h], pages_out, sub)
+        part_o, part_st = slot_attention(
+            sreq, perm, kstart, q_start, packed_all, pages_out, sub, row_block=0 if h == 0 else h + 1
+        )
         hi = lax.reduce_precision(part_st, exponent_bits=8, mantissa_bits=7)
         rest = part_st - hi
         mid = lax.reduce_precision(rest, exponent_bits=8, mantissa_bits=7)

time: 282 us -> 298 us (1.057)
  waiting for transfers between devices: 106 us -> 119 us
  local copies, waits for them, and re-layouts: 29.4 us -> 32.9 us
  starting transfers between devices: 20.1 us -> 16.6 us
    all_to_all x2, waiting for transfers between devices: 18.4 us -> 26.8 us  [body(): got = lax.all_to_all(sent, 'req', 0, 0, tiled=True)]
    all_gather x2 -> x1, waiting for transfers between devices: 52 us -> 56.5 us  [body(): lax.all_gather(jnp.concatenate(pieces, axis=0)[None], 'req', axis=0, tile...]
    all_to_all x2, starting transfers between devices: 11.8 us -> 8.44 us  [body(): got = lax.all_to_all(sent, 'req', 0, 0, tiled=True)]
  transfers between devices with their start and end apart: 6 -> 5, of which waited for: 4 -> 4; matrix products, arithmetic and copies ran while one was open for 12% -> 9% of each run, Pallas kernels for 19% -> 10%
where the time goes in v15:
time: 298 us; the launch traced here: 296 us
  waiting for transfers between devices  119 us (40%)
  Pallas kernels  56.6 us (19%)
  local copies, waits for them, and re-layouts  32.9 us (11%)
  blocking collectives  31.3 us (11%)
  other arithmetic  21.2 us (7%)
  starting transfers between devices  16.6 us (6%)
  between operations  14.4 us (5%)
  matrix products  4.08 us (1%)
    pallas_call x2, Pallas kernels, slot_attention(): pl.pallas_call(kernel, grid_spec=grid_spec, out_shape=[jax.ShapeDtypeStru...  56.6 us
    all_gather x1, waiting for transfers between devices, body(): lax.all_gather(jnp.concatenate(pieces, axis=0)[None], 'req', axis=0, tile...  56.5 us
    all_to_all x1, waiting for transfers between devices, body(): lax.all_to_all(jnp.broadcast_to(both[None], (n_req,) + both.shape), 'req'...  35.2 us
    all_to_all x1, blocking collectives, body(): got_t = lax.all_to_all(partial_t, 'tp', 0, 0, tiled=True)  31.3 us
    all_to_all x2, waiting for transfers between devices, body(): got = lax.all_to_all(sent, 'req', 0, 0, tiled=True)  26.8 us
    all_to_all x2, starting transfers between devices, body(): got = lax.all_to_all(sent, 'req', 0, 0, tiled=True)  8.44 us
    all_to_all x1, starting transfers between devices, body(): lax.all_to_all(jnp.broadcast_to(both[None], (n_req,) + both.shape), 'req'...  8.12 us
  transfers between devices with their start and end apart: 5, of which 4 were waited for; matrix products, arithmetic and copies ran while one was open for 9% of the time, Pallas kernels for 10%

profile of v15, /device:TPU:0, one launch (start us, length us, event | category | flops | bytes accessed | tf_op | source)
XLA Modules:
  0.0 296.3 jit_solution(3076136185150188636)
XLA Ops:
  9.9 1.8 broadcast_in_dim.142
  11.8 8.1 %all-to-all-start = ((bf16[16,640,128]{1,2,0:T(8,128)(2,1)}), bf16[16,640,128]{1,2,0:T(8,128)(2,1)S(1)}, u32[]{:S(2)}, u32[]{:S(2)}) async-start(bf16[16,640,128]{1,2,0:T(8,128)(2,1)} %broadcast_in_dim.142), calls=%async_computation | async-start | bytes 5242880 | tf_op jit(solution)/shard_map/all_to_all | solution.py:198
  21.8 35.2 %all-to-all-done = bf16[16,640,128]{1,2,0:T(8,128)(2,1)S(1)} async-done(((bf16[16,640,128]{1,2,0:T(8,128)(2,1)}), bf16[16,640,128]{1,2,0:T(8,128)(2,1)S(1)}, u32[]{:S(2)}, u32[]{:S(2)}) %all-to-all-start) | async-done | bytes 2621472 | tf_op jit(solution)/shard_map/all_to_all | solution.py:198
  58.4 2.6 copy.67
  61.1 3.7 %reshape.237 = bf16[2048,384]{1,0:T(8,128)(2,1)} reshape(bf16[16,384,128]{2,1,0:T(8,128)(2,1)} %copy.67) | data formatting | bytes 3145728 | tf_op jit(solution)/shard_map/reshape | solution.py:199
  64.8 3.1 %fusion.17 = f32[384,512]{1,0:T(8,128)S(1)} fusion(bf16[2048,384]{1,0:T(8,128)(2,1)} %reshape.237, bf16[512,2048]{1,0:T(8,128)(2,1)} %all-gather.4.cloned.1.call-done), kind=kOutput, calls=%fused_computation.84 | convolution fusion | flops 805306368 | bytes 4456448 | tf_op jit(solution)/shard_map/dot_general | solution.py:201
  69.8 2.0 sort.17
  73.5 56.5 %all-gather.6.cloned.1.call-done = bf16[3072,1024]{1,0:T(8,128)(2,1)} async-done(((bf16[192,1024]{1,0:T(8,128)(2,1)}), bf16[3072,1024]{1,0:T(8,128)(2,1)}) %all-gather.6.cloned.1.call-update) | async-done | bytes 6291472 | tf_op jit(solution)/shard_map/all_gather | solution.py:229
  130.0 3.1 %slice.109 = bf16[16,64,1024]{2,1,0:T(8,128)(2,1)} slice(bf16[16,192,1024]{2,1,0:T(8,128)(2,1)} %bitcast.83), slice={[0:16], [64:128], [0:1024]} | slice | bytes 4194304 | tf_op jit(solution)/shard_map/slice | solution.py:230
  133.1 2.8 reshape_reshape.3
  136.0 2.1 gather_fusion.2
  138.1 2.5 broadcast_select_fusion.page_ref
  140.6 28.4 %shard_map.77 = (bf16[16,64,1024]{2,1,0:T(8,128)(2,1)S(1)}, f32[16,2,1024]{2,1,0:T(2,128)S(1)}) custom-call(s32[64]{0:T(128)S(1)} %gather_fusion, s32[64]{0:T(128)S(1)} %get-tuple-element.7.perm_ref, s32[64]{0:T(128)S(1)} %broadcast_multiply_fusion.1.kstart_ref, s32[16]{0:T(128)S(1)} %get-tuple-element.42.qstart_ref, bf16[16,192,1024]{2,1,0:T(8,128)(2,1)} %bitcast.84, ...), custom_call_target="tpu_custom_call" | custom-call | tf_op jit(solution)/shard_map/pallas_call | solution.py:177
  169.2 2.0 pad_maximum_fusion
  171.1 4.5 %all-to-all-start.1 = ((bf16[16,70,1024]{2,1,0:T(8,128)(2,1)}), bf16[16,70,1024]{2,1,0:T(8,128)(2,1)}, u32[]{:S(2)}, u32[]{:S(2)}) async-start(bf16[16,70,1024]{2,1,0:T(8,128)(2,1)} %pad_maximum_fusion), calls=%async_computation.1 | async-start | bytes 4718592 | tf_op jit(solution)/shard_map/all_to_all | solution.py:256
  175.7 28.2 %shard_map.78 = (bf16[16,64,1024]{2,1,0:T(8,128)(2,1)S(1)}, f32[16,2,1024]{2,1,0:T(2,128)S(1)}) custom-call(s32[64]{0:T(128)S(1)} %gather_fusion, s32[64]{0:T(128)S(1)} %get-tuple-element.7.perm_ref, s32[64]{0:T(128)S(1)} %broadcast_multiply_fusion.1.kstart_ref, s32[16]{0:T(128)S(1)} %get-tuple-element.40.qstart_ref, bf16[16,192,1024]{2,1,0:T(8,128)(2,1)} %bitcast.85, ...), custom_call_target="tpu_custom_call" | custom-call | tf_op jit(solution)/shard_map/pallas_call | solution.py:177
  204.0 1.9 pad_maximum_fusion.1
  205.9 3.5 %all-to-all-done.1 = bf16[16,70,1024]{2,1,0:T(8,128)(2,1)} async-done(((bf16[16,70,1024]{2,1,0:T(8,128)(2,1)}), bf16[16,70,1024]{2,1,0:T(8,128)(2,1)}, u32[]{:S(2)}, u32[]{:S(2)}) %all-to-all-start.1) | async-done | bytes 2293792 | tf_op jit(solution)/shard_map/all_to_all | solution.py:256
  209.4 3.9 %all-to-all-start.2 = ((bf16[16,70,1024]{2,1,0:T(8,128)(2,1)}), bf16[16,70,1024]{2,1,0:T(8,128)(2,1)S(1)}, u32[]{:S(2)}, u32[]{:S(2)}) async-start(bf16[16,70,1024]{2,1,0:T(8,128)(2,1)} %pad_maximum_fusion.1), calls=%async_computation.2 | async-start | bytes 4718592 | tf_op jit(solution)/shard_map/all_to_all | solution.py:256
  217.2 2.0 reshape.275
  220.9 23.3 %all-to-all-done.2 = bf16[16,70,1024]{2,1,0:T(8,128)(2,1)S(1)} async-done(((bf16[16,70,1024]{2,1,0:T(8,128)(2,1)}), bf16[16,70,1024]{2,1,0:T(8,128)(2,1)S(1)}, u32[]{:S(2)}, u32[]{:S(2)}) %all-to-all-start.2) | async-done | bytes 2293792 | tf_op jit(solution)/shard_map/all_to_all | solution.py:256
  245.1 2.0 reshape.276
  249.8 3.7 %multiply_reduce_fusion.1 = (f32[64,1024]{1,0:T(8,128)}, f32[64,1024]{1,0:T(8,128)}) fusion(bf16[16,70,1024]{2,1,0:T(8,128)(2,1)} %all-to-all-done.1, f32[16,1024]{1,0:T(8,128)S(1)} %bitcast.97, pred[16]{0:T(512)(128)(4,1)S(1)} %reduce_or.9, f32[16,1024]{1,0:T(8,128)S(1)} %bitcast.96, bf16[16,70,1024]{2,1,0:T(8,128)(2,1)S(1)} %all-to-all-done.2), kind=kLoop, calls=%fused_computation.4 | loop fusion | flops 8257536 | bytes 4849680 | tf_op jit(solution)/shard_map/reduce_sum | solution.py:267
  257.2 31.3 %all_to_all.20 = bf16[8,512,256]{2,1,0:T(8,128)(2,1)S(1)} all-to-all(bf16[8,512,256]{2,1,0:T(8,128)(2,1)S(1)} %bitcast.89), channel_id=1, replica_groups=mesh['req'=16,'tp'=8] {'tp'}, dimensions={0} | all-to-all | bytes 4194304 | tf_op jit(solution)/shard_map/all_to_all | solution.py:276
  (84 shorter events, 23.6 us)
Async XLA Ops:
  7.2 57.6 %all-gather.4.cloned.1.call-start = ((), (), s32[]{:S(2)}) async-start(), calls=%async_computation.4 | async-start | bytes 2359296 | tf_op jit(solution)/shard_map/all_gather | solution.py:192
  11.8 8.2 %copy-start.3 = (s32[16]{0:T(128)S(1)}, s32[16]{0:T(128)}, u32[]{:S(2)}) copy-start(s32[16]{0:T(128)} %param.10) | copy-start | bytes 196
  11.8 45.2 %all-to-all-start = ((bf16[16,640,128]{1,2,0:T(8,128)(2,1)}), bf16[16,640,128]{1,2,0:T(8,128)(2,1)S(1)}, u32[]{:S(2)}, u32[]{:S(2)}) async-start(bf16[16,640,128]{1,2,0:T(8,128)(2,1)} %broadcast_in_dim.142), calls=%async_computation | async-start | bytes 5242880 | tf_op jit(solution)/shard_map/all_to_all | solution.py:198
  19.9 110.1 %all-gather.6.cloned.1.call-start = ((), (), s32[]{:S(2)}) async-start(), calls=%async_computation.5 | async-start | bytes 6684672 | tf_op jit(solution)/shard_map/all_gather | solution.py:229
  57.0 4.1 %copy-start.1 = (bf16[16,640,128]{1,2,0:T(8,128)(2,1)}, bf16[16,640,128]{1,2,0:T(8,128)(2,1)S(1)}, u32[]{:S(2)}) copy-start(bf16[16,640,128]{1,2,0:T(8,128)(2,1)S(1)} %all-to-all-done) | copy-start | bytes 7864324
  64.8 3.3 %copy-start.4 = (f32[5]{0:T(128)S(1)}, f32[5]{0:T(128)}, u32[]{:S(2)}) copy-start(f32[5]{0:T(128)} %constant.16.clone.1) | copy-start | bytes 64
  68.0 1.4 copy-start.2
  140.6 35.1 %copy-start = (bf16[64,128,128]{2,1,0:T(8,128)(2,1)}, bf16[64,128,128]{2,1,0:T(8,128)(2,1)S(1)}, u32[]{:S(2)}) copy-start(bf16[64,128,128]{2,1,0:T(8,128)(2,1)S(1)} %broadcast_select_fusion.page_ref) | copy-start | bytes 6291460
  171.1 38.3 %all-to-all-start.1 = ((bf16[16,70,1024]{2,1,0:T(8,128)(2,1)}), bf16[16,70,1024]{2,1,0:T(8,128)(2,1)}, u32[]{:S(2)}, u32[]{:S(2)}) async-start(bf16[16,70,1024]{2,1,0:T(8,128)(2,1)} %pad_maximum_fusion), calls=%async_computation.1 | async-start | bytes 4718592 | tf_op jit(solution)/shard_map/all_to_all | solution.py:256
  209.4 34.9 %all-to-all-start.2 = ((bf16[16,70,1024]{2,1,0:T(8,128)(2,1)}), bf16[16,70,1024]{2,1,0:T(8,128)(2,1)S(1)}, u32[]{:S(2)}, u32[]{:S(2)}) async-start(bf16[16,70,1024]{2,1,0:T(8,128)(2,1)} %pad_maximum_fusion.1), calls=%async_computation.2 | async-start | bytes 4718592 | tf_op jit(solution)/shard_map/all_to_all | solution.py:256
Sparse Core Ops, SparseCore 0:
  9.6 29.2 all-gather.3
  69.6 60.3 all-gather.5

commit v16 on v12

--- a/solution.py
+++ b/solution.py
@@ -252,18 +252,19 @@
         lo = rest - mid
         sent = jnp.concatenate([part_o] + [t.astype(jnp.bfloat16) for t in (hi, mid, lo)], axis=1)
         got = lax.all_to_all(sent, "req", 0, 0, tiled=True)
-        got_o = got[:, :HD].reshape(requests, HD, GROUP, sub)
-        got_bits = got[:, HD:].reshape(requests, 3, 2, GROUP, sub).astype(jnp.float32)
+        got_o = got[:, :HD]
+        got_bits = got[:, HD:].reshape(requests, 3, 2, width).astype(jnp.float32)
         got_st = (got_bits[:, 0] + got_bits[:, 1]) + got_bits[:, 2]
 
-        m_parts = jnp.where(valid, got_st[:, 0], NEG_BIG)
-        l_parts = jnp.where(valid, got_st[:, 1], 0.0)
+        valid_row = holds[:, None]
+        m_parts = jnp.where(valid_row, got_st[:, 0], NEG_BIG)
+        l_parts = jnp.where(valid_row, got_st[:, 1], 0.0)
         top = jnp.max(m_parts, axis=0)
         w = l_parts * jnp.exp(m_parts - top[None])
         den = jnp.sum(w, axis=0)
-        o_parts = jnp.where(valid[..., None], got_o.astype(jnp.float32), 0.0)
-        num = jnp.sum(o_parts * w[:, None, :, :], axis=0)
-        attention_t = (num / den[None]).astype(jnp.bfloat16)
+        o_parts = jnp.where(valid, got_o.astype(jnp.float32), 0.0)
+        num = jnp.sum(o_parts * w[:, None, :], axis=0)
+        attention_t = (num / den[None]).astype(jnp.bfloat16).reshape(HD, GROUP, sub)
         attention_flat = jnp.transpose(attention_t, (2, 1, 0)).reshape(sub, GROUP * HD)
 
         head_terms = jnp.dot(attention_flat, out_full, preferred_element_type=jnp.float32)

time: 282 us -> 277 us (0.982)
  local copies, waits for them, and re-layouts: 29.4 us -> 23.8 us
  waiting for transfers between devices: 106 us -> 109 us
  transfers between devices with their start and end apart: 6 -> 6, of which waited for: 4 -> 4; matrix products, arithmetic and copies ran while one was open for 12% -> 11% of each run, Pallas kernels for 19% -> 20%
where the time goes in v16:
time: 277 us; the launch traced here: 276 us
  waiting for transfers between devices  109 us (39%)
  Pallas kernels  54.9 us (20%)
  blocking collectives  31.4 us (11%)
  local copies, waits for them, and re-layouts  23.8 us (9%)
  starting transfers between devices  19.9 us (7%)
  other arithmetic  18.8 us (7%)
  between operations  14.2 us (5%)
  matrix products  3.62 us (1%)
    pallas_call x2, Pallas kernels, slot_attention(): pl.pallas_call(kernel, grid_spec=grid_spec, out_shape=[jax.ShapeDtypeStru...  54.9 us
    all_gather x2, waiting for transfers between devices, body(): gathered.append(lax.all_gather(piece[None], 'req', axis=0, tiled=True))  52.6 us
    all_to_all x1, waiting for transfers between devices, body(): lax.all_to_all(jnp.broadcast_to(both[None], (n_req,) + both.shape), 'req'...  35.2 us
    all_to_all x1, blocking collectives, body(): got_t = lax.all_to_all(partial_t, 'tp', 0, 0, tiled=True)  31.4 us
    all_to_all x2, waiting for transfers between devices, body(): got = lax.all_to_all(sent, 'req', 0, 0, tiled=True)  20.6 us
    all_to_all x2, starting transfers between devices, body(): got = lax.all_to_all(sent, 'req', 0, 0, tiled=True)  11.6 us
    all_to_all x1, starting transfers between devices, body(): lax.all_to_all(jnp.broadcast_to(both[None], (n_req,) + both.shape), 'req'...  8.17 us
  transfers between devices with their start and end apart: 6, of which 4 were waited for; matrix products, arithmetic and copies ran while one was open for 11% of the time, Pallas kernels for 20%

profile of v16, /device:TPU:0, one launch (start us, length us, event | category | flops | bytes accessed | tf_op | source)
XLA Modules:
  0.0 275.8 jit_solution(11353298521077462788)
XLA Ops:
  9.9 1.8 broadcast_in_dim.144
  11.8 8.2 %all-to-all-start = ((bf16[16,640,128]{1,2,0:T(8,128)(2,1)}), bf16[16,640,128]{1,2,0:T(8,128)(2,1)}, u32[]{:S(2)}, u32[]{:S(2)}) async-start(bf16[16,640,128]{1,2,0:T(8,128)(2,1)} %broadcast_in_dim.144), calls=%async_computation | async-start | bytes 5242880 | tf_op jit(solution)/shard_map/all_to_all | solution.py:198
  21.8 35.2 %all-to-all-done = bf16[16,640,128]{1,2,0:T(8,128)(2,1)} async-done(((bf16[16,640,128]{1,2,0:T(8,128)(2,1)}), bf16[16,640,128]{1,2,0:T(8,128)(2,1)}, u32[]{:S(2)}, u32[]{:S(2)}) %all-to-all-start) | async-done | bytes 2621472 | tf_op jit(solution)/shard_map/all_to_all | solution.py:198
  57.1 1.6 slice.102
  60.5 2.6 fusion.15
  65.8 2.0 sort.17
  69.5 45.7 %all-gather.9.cloned.1.call-done = bf16[2048,1024]{1,0:T(8,128)(2,1)} async-done(((bf16[128,1024]{1,0:T(8,128)(2,1)}), bf16[2048,1024]{1,0:T(8,128)(2,1)}) %all-gather.9.cloned.1.call-update) | async-done | bytes 4194320 | tf_op jit(solution)/shard_map/all_gather | solution.py:229
  115.2 1.8 slice.108
  117.0 2.3 reshape_reshape.3
  119.3 2.5 gather_fusion.2
  121.8 1.9 broadcast_select_fusion.page_ref
  123.7 27.6 %shard_map.77 = (bf16[16,64,1024]{2,1,0:T(8,128)(2,1)S(1)}, f32[16,2,1024]{2,1,0:T(2,128)S(1)}) custom-call(s32[64]{0:T(128)S(1)} %gather_fusion, s32[64]{0:T(128)S(1)} %get-tuple-element.7.perm_ref, s32[64]{0:T(128)S(1)} %broadcast_multiply_fusion.1.kstart_ref, s32[16]{0:T(128)S(1)} %get-tuple-element.36.qstart_ref, bf16[16,128,1024]{2,1,0:T(8,128)(2,1)} %bitcast.74, ...), custom_call_target="tpu_custom_call" | custom-call | tf_op jit(solution)/shard_map/pallas_call | solution.py:177
  151.5 1.9 pad_maximum_fusion
  153.4 5.6 %all-to-all-start.1 = ((bf16[16,70,1024]{2,1,0:T(8,128)(2,1)}), bf16[16,70,1024]{2,1,0:T(8,128)(2,1)}, u32[]{:S(2)}, u32[]{:S(2)}) async-start(bf16[16,70,1024]{2,1,0:T(8,128)(2,1)} %pad_maximum_fusion), calls=%async_computation.1 | async-start | bytes 4718592 | tf_op jit(solution)/shard_map/all_to_all | solution.py:254
  159.0 6.9 %all-gather.7.cloned.1.call-done.q_ref = bf16[16,64,1024]{2,1,0:T(8,128)(2,1)} async-done(((bf16[1,64,1024]{2,1,0:T(8,128)(2,1)}), bf16[16,64,1024]{2,1,0:T(8,128)(2,1)}) %all-gather.7.cloned.1.call-update) | async-done | bytes 2097168 | tf_op jit(solution)/shard_map/all_gather | solution.py:229
  165.9 1.6 copy-done.1
  167.5 27.3 %shard_map.78 = (bf16[16,64,1024]{2,1,0:T(8,128)(2,1)S(1)}, f32[16,2,1024]{2,1,0:T(2,128)S(1)}) custom-call(s32[64]{0:T(128)S(1)} %gather_fusion, s32[64]{0:T(128)S(1)} %get-tuple-element.7.perm_ref, s32[64]{0:T(128)S(1)} %broadcast_multiply_fusion.1.kstart_ref, s32[16]{0:T(128)S(1)} %get-tuple-element.34.qstart_ref, bf16[16,64,1024]{2,1,0:T(8,128)(2,1)S(1)} %copy-done.1, ...), custom_call_target="tpu_custom_call" | custom-call | tf_op jit(solution)/shard_map/pallas_call | solution.py:177
  194.9 1.9 pad_maximum_fusion.1
  196.9 6.0 %all-to-all-start.2 = ((bf16[16,70,1024]{2,1,0:T(8,128)(2,1)}), bf16[16,70,1024]{2,1,0:T(8,128)(2,1)S(1)}, u32[]{:S(2)}, u32[]{:S(2)}) async-start(bf16[16,70,1024]{2,1,0:T(8,128)(2,1)} %pad_maximum_fusion.1), calls=%async_computation.2 | async-start | bytes 4718592 | tf_op jit(solution)/shard_map/all_to_all | solution.py:254
  203.7 1.3 slice.116
  207.0 20.6 %all-to-all-done.2 = bf16[16,70,1024]{2,1,0:T(8,128)(2,1)S(1)} async-done(((bf16[16,70,1024]{2,1,0:T(8,128)(2,1)}), bf16[16,70,1024]{2,1,0:T(8,128)(2,1)S(1)}, u32[]{:S(2)}, u32[]{:S(2)}) %all-to-all-start.2) | async-done | bytes 2293792 | tf_op jit(solution)/shard_map/all_to_all | solution.py:254
  227.9 1.1 fusion.3
  229.4 3.7 %multiply_reduce_fusion.1 = (f32[64,1024]{1,0:T(8,128)}, f32[64,1024]{1,0:T(8,128)}) fusion(bf16[16,70,1024]{2,1,0:T(8,128)(2,1)} %all-to-all-done.1, f32[16,1024]{1,0:T(8,128)S(1)} %get-tuple-element.33, pred[16]{0:T(512)(128)(4,1)S(1)} %reduce_or.9, f32[16,1024]{1,0:T(8,128)S(1)} %get-tuple-element.32, bf16[16,70,1024]{2,1,0:T(8,128)(2,1)S(1)} %all-to-all-done.2), kind=kLoop, calls=%fused_computation.4 | loop fusion | flops 8257536 | bytes 4849680 | tf_op jit(solution)/shard_map/reduce_sum | solution.py:266
  236.8 31.4 %all_to_all.20 = bf16[8,512,256]{2,1,0:T(8,128)(2,1)S(1)} all-to-all(bf16[8,512,256]{2,1,0:T(8,128)(2,1)S(1)} %bitcast.78), channel_id=1, replica_groups=mesh['req'=16,'tp'=8] {'tp'}, dimensions={0} | all-to-all | bytes 4194304 | tf_op jit(solution)/shard_map/all_to_all | solution.py:275
  (86 shorter events, 19.0 us)
Async XLA Ops:
  7.2 53.3 %all-gather.5.cloned.1.call-start = ((), (), s32[]{:S(2)}) async-start(), calls=%async_computation.4 | async-start | bytes 2359296 | tf_op jit(solution)/shard_map/all_gather | solution.py:192
  11.8 8.2 %copy-start.3 = (s32[16]{0:T(128)S(1)}, s32[16]{0:T(128)}, u32[]{:S(2)}) copy-start(s32[16]{0:T(128)} %param.10) | copy-start | bytes 196
  11.8 45.3 %all-to-all-start = ((bf16[16,640,128]{1,2,0:T(8,128)(2,1)}), bf16[16,640,128]{1,2,0:T(8,128)(2,1)}, u32[]{:S(2)}, u32[]{:S(2)}) async-start(bf16[16,640,128]{1,2,0:T(8,128)(2,1)} %broadcast_in_dim.144), calls=%async_computation | async-start | bytes 5242880 | tf_op jit(solution)/shard_map/all_to_all | solution.py:198
  20.0 95.2 %all-gather.9.cloned.1.call-start = ((), (), s32[]{:S(2)}) async-start(), calls=%async_computation.6 | async-start | bytes 4456448 | tf_op jit(solution)/shard_map/all_gather | solution.py:229
  60.4 2.8 %copy-start.4 = (f32[5]{0:T(128)S(1)}, f32[5]{0:T(128)}, u32[]{:S(2)}) copy-start(f32[5]{0:T(128)} %constant.16.clone.1) | copy-start | bytes 64
  63.1 1.5 copy-start.2
  64.6 101.3 %all-gather.7.cloned.1.call-start = ((), (), s32[]{:S(2)}) async-start(), calls=%async_computation.5 | async-start | bytes 2228224 | tf_op jit(solution)/shard_map/all_gather | solution.py:229
  123.7 27.6 %copy-start = (bf16[64,128,128]{2,1,0:T(8,128)(2,1)}, bf16[64,128,128]{2,1,0:T(8,128)(2,1)S(1)}, u32[]{:S(2)}) copy-start(bf16[64,128,128]{2,1,0:T(8,128)(2,1)S(1)} %broadcast_select_fusion.page_ref) | copy-start | bytes 6291460
  153.4 43.5 %all-to-all-start.1 = ((bf16[16,70,1024]{2,1,0:T(8,128)(2,1)}), bf16[16,70,1024]{2,1,0:T(8,128)(2,1)}, u32[]{:S(2)}, u32[]{:S(2)}) async-start(bf16[16,70,1024]{2,1,0:T(8,128)(2,1)} %pad_maximum_fusion), calls=%async_computation.1 | async-start | bytes 4718592 | tf_op jit(solution)/shard_map/all_to_all | solution.py:254
  165.9 1.6 copy-start.1
  196.9 30.7 %all-to-all-start.2 = ((bf16[16,70,1024]{2,1,0:T(8,128)(2,1)}), bf16[16,70,1024]{2,1,0:T(8,128)(2,1)S(1)}, u32[]{:S(2)}, u32[]{:S(2)}) async-start(bf16[16,70,1024]{2,1,0:T(8,128)(2,1)} %pad_maximum_fusion.1), calls=%async_computation.2 | async-start | bytes 4718592 | tf_op jit(solution)/shard_map/all_to_all | solution.py:254
Sparse Core Ops, SparseCore 0:
  9.6 29.3 all-gather.4
  64.7 50.4 all-gather.8
  117.3 48.5 all-gather.6
